TPU v7x, 32 devices: a whole 2x2x4 slice. The times are simulated.
32 devices in a mesh: groups: 2 (over x), enc: 16 (over z, y, core).
Axes of the slice: x: 2, y: 2, z: 4, core: 2. Of those that a mesh axis runs over, the one named last changes fastest.
Arguments:
- tiles: bfloat16 [16384, 4, 512], P(('groups', 'enc')), parts along dimension 0, may hold values from -8 to 8, as said below
- tile_counts: int32 [32, 4], P(('groups', 'enc')), parts along dimension 0, may hold values from 1 to 252, as said below
- assign: int32 [32, 512], P(('groups', 'enc')), parts along dimension 0, may hold values from 0 to 512, as said below
- labels: int32 [32, 4], P(('groups', 'enc')), parts along dimension 0, may hold values from 0 to 1
- w_conv: bfloat16 [512, 1024], replicated, may hold values from -0.25 to 0.25
- bn_gain: float32 [1024], replicated, may hold values from 0.5 to 1.5
- bn_shift: float32 [1024], replicated, may hold values from -3 to 3
- w_fc: bfloat16 [1024, 512], replicated, may hold values from -0.1875 to 0.1875
- w_gate: bfloat16 [512, 512], replicated, may hold values from -0.25 to 0.25
- w_score: float32 [256], replicated, may hold values from -0.3 to 0.3
- w_cls: float32 [512, 2], replicated, may hold values from -0.25 to 0.25
Outputs:
- loss: float32 [2], P('groups'), parts along dimension 0
- grad_conv: float32 [1024, 1024], P('groups'), parts along dimension 0
- grad_gain: float32 [2048], P('groups'), parts along dimension 0
- grad_shift: float32 [2048], P('groups'), parts along dimension 0
- grad_fc: float32 [2048, 512], P('groups'), parts along dimension 0
- grad_gate: float32 [1024, 512], P('groups'), parts along dimension 0
- grad_score: float32 [512], P('groups'), parts along dimension 0
- grad_cls: float32 [1024, 2], P('groups'), parts along dimension 0
There are 2 independent parts, one for each index of `groups`. A program takes and returns all parts, laid end to end along the dimension named above; an argument that names none is the same for every part. Nothing has to cross between parts.
Inputs may be any that keep to these rules, and one draw needn't show every extreme that they name: `tile_counts`: each owner's counts sum to its number of tiles (the entries of its assign row below 512); each owner has one slide of exactly (tiles + 1) // 2 tiles; the busiest owner has 504 tiles. An owner's tiles take its first rows, and the rest of its row of assign is 512. Tile entries are distinct; slot // 32 is the encoder group. For every group e, row o names exactly the slots e * 32 to e * 32 + c - 1 for some c of 1 to 32; every group receives 264 tiles in all; some owner sends 32 tiles to some group. Owners hold uneven numbers of tiles, from 24 to 504. Real-valued tile features; rows past an owner's tiles are zero.
All inputs are finite; a program needn't handle non-finite values.
Results may differ from a plain program's by a relative error of at most 0.0055.
The roundings to bfloat16 on the way count: a program that leaves them out, or rounds other values in their place, can miss the bound.
Values may be sent and summed in bfloat16 or wider, within the bound.
No kernel may reach another device: no remote copies, remote signals or barrier semaphores. Data moves between devices by JAX's collectives and lax.ppermute only.
A program may use at most 64 MiB of HBM per device.

v0:
```python
import jax
import jax.numpy as jnp
from jax import lax
from jax.sharding import PartitionSpec as P

SLOTS_DEV = 512


epsilon = 1e-05
HIGH = lax.Precision.HIGHEST


def contract_rows(left, right):
    return lax.dot_general(
        left, right, (((0,), (0,)), ((), ())), preferred_element_type=jnp.float32
    )


def contract_cols(left, right):
    return lax.dot_general(
        left, right, (((1,), (1,)), ((), ())), preferred_element_type=jnp.float32
    )


def finish_norm(before, tile_mean, tile_scale, bn_gain, bn_shift):
    normed = (before - tile_mean) * tile_scale * bn_gain + bn_shift
    return jnp.mean(jnp.maximum(normed, 0.0), axis=1).astype(jnp.bfloat16)


def single_post(before, bn_gain, bn_shift, pixel_count):
    mean_value = jnp.sum(before, axis=(0, 1)) / pixel_count
    variance = jnp.sum(before * before, axis=(0, 1)) / pixel_count - mean_value * mean_value
    inverse = lax.rsqrt(variance + epsilon)
    return finish_norm(before, mean_value, inverse, bn_gain, bn_shift)


def head_pass(
    embedded, slide_start, slide_end, classes_of, w_fc, w_gate, w_score, w_cls, slides_all
):
    row_count = embedded.shape[0]
    position = jnp.arange(row_count, dtype=jnp.int32)[:, None]
    membership = ((position >= slide_start[None, :]) & (position < slide_end[None, :])).astype(
        jnp.float32
    )
    before = jnp.dot(embedded, w_fc, preferred_element_type=jnp.float32)
    hidden = jnp.maximum(before, 0.0).astype(jnp.bfloat16)
    gate_pre = jnp.dot(hidden, w_gate, preferred_element_type=jnp.float32)

    def tail(gate_pre, hidden_wide, w_score, w_cls):
        half_width = gate_pre.shape[1] // 2
        gated_mix = jnp.tanh(gate_pre[:, :half_width]) * jax.nn.sigmoid(gate_pre[:, half_width:])
        scores = jnp.dot(gated_mix, w_score, precision=HIGH)
        weight = jnp.exp(scores)[:, None] * membership
        totals = jnp.sum(weight, axis=0)
        attention = weight / totals[None, :]
        pooled = lax.dot_general(attention, hidden_wide, (((0,), (0,)), ((), ())), precision=HIGH)
        logits = jnp.dot(pooled, w_cls, precision=HIGH)
        target = (
            classes_of[:, None] == jnp.arange(logits.shape[1], dtype=jnp.int32)[None, :]
        ).astype(jnp.float32)
        log_total = jnp.log(jnp.sum(jnp.exp(logits), axis=1))
        return jnp.sum(log_total - jnp.sum(logits * target, axis=1)) / slides_all

    loss_sum, tail_vjp = jax.vjp(tail, gate_pre, hidden.astype(jnp.float32), w_score, w_cls)
    grad_gates, grad_hidden, grad_score, grad_cls = tail_vjp(jnp.ones((), jnp.float32))
    gates_low = grad_gates.astype(jnp.bfloat16)
    grad_gate = contract_rows(hidden, gates_low)
    grad_hidden = grad_hidden + contract_cols(gates_low, w_gate)
    before_low = jnp.where(before > 0, grad_hidden, 0.0).astype(jnp.bfloat16)
    grad_fc = contract_rows(embedded, before_low)
    grad_embedded = contract_cols(before_low, w_fc).astype(jnp.bfloat16)
    return (loss_sum, grad_fc, grad_gate, grad_score, grad_cls, grad_embedded)


def local(
    tiles, tile_counts, assign, labels, w_conv, bn_gain, bn_shift, w_fc, w_gate, w_score, w_cls
):
    devices = lax.axis_size("enc")
    own_rows, positions, input_width = tiles.shape
    emb_width = w_conv.shape[1]
    target_slot = assign[0]
    cap_rows = SLOTS_DEV // devices
    group_tiles = (
        devices // 4 * (4 + (cap_rows - 2) // 3 + 2 * (cap_rows - 2) // 3 + (cap_rows - 2))
        + devices // 2
    )
    pixel_count = float(group_tiles * positions)
    slides_all = float(devices * tile_counts.shape[1])
    counts_row = tile_counts[0]
    slide_end = jnp.cumsum(counts_row)
    slide_start = slide_end - counts_row
    outgoing = (
        jnp.zeros((SLOTS_DEV, positions, input_width), jnp.bfloat16)
        .at[target_slot]
        .set(tiles, mode="drop")
    )
    present_flag = jnp.zeros((SLOTS_DEV,), jnp.bfloat16).at[target_slot].set(1.0, mode="drop")
    arrived, arrived_flag = (
        lax.all_to_all(outgoing, "enc", split_axis=0, concat_axis=0, tiled=True),
        lax.all_to_all(present_flag, "enc", split_axis=0, concat_axis=0, tiled=True),
    )
    work_flat = arrived.reshape(-1, input_width)
    before = jnp.dot(work_flat, w_conv, preferred_element_type=jnp.float32).reshape(
        arrived.shape[0], positions, emb_width
    )

    def post_fn(before, bn_gain, bn_shift):
        return single_post(before, bn_gain, bn_shift, pixel_count)

    encoded, post_vjp = jax.vjp(post_fn, before, bn_gain, bn_shift)
    returned = lax.all_to_all(encoded, "enc", split_axis=0, concat_axis=0, tiled=True)
    embedded = jnp.take(returned, target_slot, axis=0, mode="fill", fill_value=0)
    loss_sum, grad_fc, grad_gate, grad_score, grad_cls, grad_embedded = head_pass(
        embedded, slide_start, slide_end, labels[0], w_fc, w_gate, w_score, w_cls, slides_all
    )
    grad_slots = (
        jnp.zeros((SLOTS_DEV, emb_width), jnp.bfloat16)
        .at[target_slot]
        .set(grad_embedded, mode="drop")
    )
    grad_arrived = lax.all_to_all(grad_slots, "enc", split_axis=0, concat_axis=0, tiled=True)
    grad_before, grad_gain, grad_shift = post_vjp(grad_arrived)
    grad_conv = contract_rows(work_flat, grad_before.reshape(-1, emb_width).astype(jnp.bfloat16))
    loss_sum, grad_fc, grad_gate, grad_score, grad_cls, grad_conv, grad_gain, grad_shift = lax.psum(
        (loss_sum, grad_fc, grad_gate, grad_score, grad_cls, grad_conv, grad_gain, grad_shift),
        "enc",
    )
    return (
        loss_sum.reshape(1),
        grad_conv,
        grad_gain,
        grad_shift,
        grad_fc,
        grad_gate,
        grad_score,
        grad_cls,
    )


def solution(mesh):
    placed = (
        P(("groups", "enc"), None, None),
        P(("groups", "enc"), None),
        P(("groups", "enc"), None),
        P(("groups", "enc"), None),
        P(),
        P(),
        P(),
        P(),
        P(),
        P(),
        P(),
    )
    return jax.shard_map(
        local,
        mesh=mesh,
        in_specs=placed,
        out_specs=(
            P("groups"),
            P("groups", None),
            P("groups"),
            P("groups"),
            P("groups", None),
            P("groups", None),
            P("groups"),
            P("groups", None),
        ),
        check_vma=False,
    )
```

profile of v0, /device:TPU:0, one launch (start us, length us, event | category | flops | bytes accessed | tf_op | source)
XLA Modules:
  0.0 348.2 jit_solution(14607078750723340423)
XLA Ops:
  7.2 0.0 copy-start
  7.2 0.8 compare_select_fusion
  8.0 0.5 broadcast_in_dim.53
  8.5 40.4 %scatter_fusion = bf16[512,4,512]{2,1,0:T(4,128)(2,1)S(1)} fusion(bf16[512,4,512]{2,1,0:T(4,128)(2,1)S(1)} %broadcast_in_dim.53, s32[512]{0:T(512)S(1)} %bitcast.55, bf16[512,4,512]{2,1,0:T(4,128)(2,1)} %param.11), kind=kCustom, calls=%fused_computation.1 | custom fusion | bytes 6293504 | tf_op jit(solution)/shard_map/scatter | solution.py:95
  48.9 54.9 %all_to_all.23 = bf16[512,4,512]{2,1,0:T(4,128)(2,1)} all-to-all(bf16[512,4,512]{2,1,0:T(4,128)(2,1)S(1)} %scatter_fusion), channel_id=1, replica_groups=mesh['groups'=2,'enc'=16] {'enc'}, dimensions={0} | all-to-all | bytes 4194304 | tf_op jit(solution)/shard_map/all_to_all | solution.py:99
  103.8 3.0 copy.24
  106.8 0.0 copy-start.4
  106.9 2.5 fusion.54
  109.4 3.2 copy-done.1
  112.5 1.7 maximum_reduce_fusion
  114.2 1.2 multiply_convert_fusion
  115.5 5.2 %all-to-all-start.1 = ((bf16[16,32,1024]{2,1,0:T(8,128)(2,1)}), bf16[16,32,1024]{2,1,0:T(8,128)(2,1)S(1)}, u32[]{:S(2)}, u32[]{:S(2)}) async-start(bf16[16,32,1024]{2,1,0:T(8,128)(2,1)} %bitcast.8), calls=%async_computation.1 | async-start | bytes 2097152 | tf_op jit(solution)/shard_map/all_to_all | solution.py:111
  120.7 0.0 copy-start.15
  120.7 0.2 reduce-window.4
  121.0 22.7 %all-to-all-done.1 = bf16[16,32,1024]{2,1,0:T(8,128)(2,1)S(1)} async-done(((bf16[16,32,1024]{2,1,0:T(8,128)(2,1)}), bf16[16,32,1024]{2,1,0:T(8,128)(2,1)S(1)}, u32[]{:S(2)}, u32[]{:S(2)}) %all-to-all-start.1) | async-done | bytes 1048608 | tf_op jit(solution)/shard_map/all_to_all | solution.py:111
  143.7 2.8 gather_fusion
  146.4 2.4 maximum_convert_fusion
  148.8 0.4 fusion.55
  149.3 0.7 fusion.29
  150.0 0.2 select_reduce_fusion
  150.2 0.4 fusion.47
  150.6 0.2 exponential_reduce_fusion
  150.8 0.6 broadcast_divide_fusion
  151.4 0.2 fusion.45
  151.6 1.1 fusion.46
  152.7 0.6 fusion.32
  153.4 0.1 select_reduce_fusion.1
  153.5 0.3 fusion.17
  153.8 0.5 fusion.14
  154.3 0.8 copy-done.9
  155.1 0.7 convolution_convert_fusion
  155.8 3.5 %scatter_custom_fusion.1 = bf16[512,1024]{1,0:T(8,128)(2,1)} fusion(s32[512]{0:T(512)S(1)} %bitcast.57, bf16[512,1024]{1,0:T(8,128)(2,1)S(1)} %convolution_convert_fusion, bf16[]{:T(256)} %constant.23.clone.1), kind=kCustom, calls=%fused_computation.41 | custom fusion | bytes 1048578 | tf_op jit(solution)/shard_map/scatter | solution.py:119
  159.4 6.9 %all-to-all-start.2 = ((bf16[16,32,1024]{2,1,0:T(8,128)(2,1)}), bf16[16,32,1024]{2,1,0:T(8,128)(2,1)S(1)}, u32[]{:S(2)}, u32[]{:S(2)}) async-start(bf16[16,32,1024]{2,1,0:T(8,128)(2,1)} %bitcast.54), calls=%async_computation.2 | async-start | bytes 2097152 | tf_op jit(solution)/shard_map/all_to_all | solution.py:121
  166.2 0.3 all-reduce.6.cloned.1.call-start
  166.5 2.5 fusion.31
  169.0 3.5 %fusion.24 = f32[1024,512]{1,0:T(8,128)} fusion(bf16[512,512]{1,0:T(8,128)(2,1)} %copy-done.9, bf16[512,1024]{1,0:T(8,128)(2,1)} %gather_fusion, pred[512]{0:T(512)(128)(4,1)S(1)} %compare_and_fusion), kind=kOutput, calls=%fused_computation.43 | convolution fusion | flops 537395200 | bytes 3670528 | tf_op jit(solution)/shard_map/dot_general | solution.py:14
  172.5 16.7 %all-to-all-done.2 = bf16[16,32,1024]{2,1,0:T(8,128)(2,1)S(1)} async-done(((bf16[16,32,1024]{2,1,0:T(8,128)(2,1)}), bf16[16,32,1024]{2,1,0:T(8,128)(2,1)S(1)}, u32[]{:S(2)}, u32[]{:S(2)}) %all-to-all-start.2) | async-done | bytes 1048608 | tf_op jit(solution)/shard_map/all_to_all | solution.py:121
  189.2 0.3 convert_multiply_fusion
  189.4 7.0 %fusion.2 = (f32[1024]{0:T(1024)S(1)}, f32[1024]{0:T(1024)S(1)}, f32[1024]{0:T(1024)S(1)}, f32[1024]{0:T(1024)S(1)}) fusion(f32[512,1024]{1,0:T(8,128)S(1)} %bitcast.52, f32[1024]{0:T(1024)S(1)} %copy-done.10, f32[1024]{0:T(1024)S(1)} %copy-done.11, f32[1024]{0:T(1024)S(1)} %get-tuple-element.29, f32[512,4,1024]{2,0,1:T(8,128)} %copy-done.1, ...), kind=kLoop, calls=%fused_computation.9 | loop fusion | flops 35647488 | bytes 10518528 | tf_op jit(solution)/shard_map/transpose(jvp())/reduce_sum | solution.py:26
  196.5 8.5 %fusion.10 = f32[512,1024]{1,0:T(8,128)} fusion(bf16[512,4,512]{0,2,1:T(8,128)(2,1)S(1)} %copy-done.5, f32[512,4,1024]{2,0,1:T(8,128)} %copy-done.1, f32[1024]{0:T(1024)S(1)} %get-tuple-element.27, f32[1024]{0:T(1024)S(1)} %get-tuple-element.26, f32[512,1024]{1,0:T(8,128)S(1)} %bitcast.53, f32[1024]{0:T(1024)S(1)} %copy-done.11, ...), kind=kOutput, calls=%fused_computation.21 | convolution fusion | flops 2181038080 | bytes 14704640 | tf_op jit(solution)/shard_map/dot_general | solution.py:14
  205.0 0.0 all-reduce.6.cloned.1.call-update
  205.7 0.1 fusion.44
  205.8 0.4 fusion.27
  206.2 65.5 %all-reduce.2 = (f32[1]{0:T(128)}, f32[1024]{0:T(1024)}, f32[1024]{0:T(1024)}, f32[256]{0:T(256)}, f32[512,2]{0,1:T(2,128)}) all-reduce(f32[1]{0:T(128)} %bitcast.13, f32[1024]{0:T(1024)S(1)} %get-tuple-element.9, f32[1024]{0:T(1024)S(1)} %get-tuple-element.8, f32[256]{0:T(256)S(1)} %bitcast.71, ...), channel_id=1, replica_groups=mesh['groups'=2,'enc'=16] {'enc'}, use_global_device_ids=true, to_apply=%region_9.10 | all-reduce | flops 3329 | bytes 26632 | tf_op jit(solution)/shard_map/psum | solution.py:124
  271.8 62.3 %all-reduce.6.cloned.1.call-done = (f32[512,1024]{1,0:T(8,128)}, f32[1024,512]{1,0:T(8,128)}, f32[512,512]{1,0:T(8,128)}) async-done(((f32[512,1024]{1,0:T(8,128)}, f32[1024,512]{1,0:T(8,128)}, f32[512,512]{1,0:T(8,128)}), (f32[512,1024]{1,0:T(8,128)}, f32[1024,512]{1,0:T(8,128)}, f32[512,512]{1,0:T(8,128)})) %all-reduce.6.cloned.1.call-update) | async-done | bytes 5242896 | tf_op jit(solution)/shard_map/psum | solution.py:124
  334.0 3.2 copy.29
  337.3 3.1 copy.30
  340.4 1.0 copy.31
  (40 shorter events, 0.1 us)
Async XLA Ops:
  7.2 99.6 %copy-start = (bf16[512,1024]{1,0:T(8,128)(2,1)S(1)}, bf16[512,1024]{1,0:T(8,128)(2,1)}, u32[]{:S(2)}) copy-start(bf16[512,1024]{1,0:T(8,128)(2,1)} %param.15) | copy-start | bytes 3145732
  106.8 7.4 %copy-start.4 = (bf16[512,4,512]{0,2,1:T(8,128)(2,1)}, bf16[512,4,512]{0,2,1:T(8,128)(2,1)S(1)}, u32[]{:S(2)}) copy-start(bf16[512,4,512]{0,2,1:T(8,128)(2,1)S(1)} %copy.24) | copy-start | bytes 6291460
  106.8 5.7 %copy-start.10 = (f32[1024]{0:T(1024)S(1)}, f32[1024]{0:T(1024)}, u32[]{:S(2)}) copy-start(f32[1024]{0:T(1024)} %param.17) | copy-start | bytes 12292
  106.8 5.7 %copy-start.11 = (f32[1024]{0:T(1024)S(1)}, f32[1024]{0:T(1024)}, u32[]{:S(2)}) copy-start(f32[1024]{0:T(1024)} %param.16) | copy-start | bytes 12292
  109.3 3.2 copy-start.1
  109.3 11.4 %copy-start.17 = (s32[1,4]{1,0:T(1,128)S(1)}, s32[1,4]{1,0:T(1,128)}, u32[]{:S(2)}) copy-start(s32[1,4]{1,0:T(1,128)} %param.12) | copy-start | bytes 52
  109.3 11.6 %copy-start.12 = (s32[1,512]{1,0:T(1,128)S(1)}, s32[1,512]{1,0:T(1,128)}, u32[]{:S(2)}) copy-start(s32[1,512]{1,0:T(1,128)} %param.13) | copy-start | bytes 6148
  115.5 33.4 %copy-start.7 = (bf16[512,512]{1,0:T(8,128)(2,1)S(1)}, bf16[512,512]{1,0:T(8,128)(2,1)}, u32[]{:S(2)}) copy-start(bf16[512,512]{1,0:T(8,128)(2,1)} %param.19) | copy-start | bytes 1572868
  115.5 28.2 %all-to-all-start.1 = ((bf16[16,32,1024]{2,1,0:T(8,128)(2,1)}), bf16[16,32,1024]{2,1,0:T(8,128)(2,1)S(1)}, u32[]{:S(2)}, u32[]{:S(2)}) async-start(bf16[16,32,1024]{2,1,0:T(8,128)(2,1)} %bitcast.8), calls=%async_computation.1 | async-start | bytes 2097152 | tf_op jit(solution)/shard_map/all_to_all | solution.py:111
  120.7 28.6 %copy-start.15 = (f32[256]{0:T(256)S(1)}, f32[256]{0:T(256)}, u32[]{:S(2)}) copy-start(f32[256]{0:T(256)} %param.20) | copy-start | bytes 3076
  143.7 6.9 %copy-start.13 = (f32[512,2]{0,1:T(2,128)S(1)}, f32[512,2]{0,1:T(2,128)}, u32[]{:S(2)}) copy-start(f32[512,2]{0,1:T(2,128)} %param.21) | copy-start | bytes 12292
  143.7 6.9 %copy-start.14 = (s32[1,4]{1,0:T(1,128)S(1)}, s32[1,4]{1,0:T(1,128)}, u32[]{:S(2)}) copy-start(s32[1,4]{1,0:T(1,128)} %param.14) | copy-start | bytes 52
  146.4 8.6 %copy-start.16 = (bf16[1024,512]{1,0:T(8,128)(2,1)S(1)}, bf16[1024,512]{1,0:T(8,128)(2,1)}, u32[]{:S(2)}) copy-start(bf16[1024,512]{1,0:T(8,128)(2,1)} %param.18) | copy-start | bytes 3145732
  148.8 4.9 %copy-start.6 = (bf16[512,512]{1,0:T(8,128)(2,1)}, bf16[512,512]{1,0:T(8,128)(2,1)S(1)}, u32[]{:S(2)}) copy-start(bf16[512,512]{1,0:T(8,128)(2,1)S(1)} %get-tuple-element.33) | copy-start | bytes 1572868
  149.3 4.2 %copy-start.2 = (f32[512,512]{1,0:T(8,128)}, f32[512,512]{1,0:T(8,128)S(1)}, u32[]{:S(2)}) copy-start(f32[512,512]{1,0:T(8,128)S(1)} %fusion.55) | copy-start | bytes 3145732
  154.3 0.8 copy-start.9
  159.4 29.8 %all-to-all-start.2 = ((bf16[16,32,1024]{2,1,0:T(8,128)(2,1)}), bf16[16,32,1024]{2,1,0:T(8,128)(2,1)S(1)}, u32[]{:S(2)}, u32[]{:S(2)}) async-start(bf16[16,32,1024]{2,1,0:T(8,128)(2,1)} %bitcast.54), calls=%async_computation.2 | async-start | bytes 2097152 | tf_op jit(solution)/shard_map/all_to_all | solution.py:121
  166.2 167.8 %all-reduce.6.cloned.1.call-start = ((), (), s32[]{:S(2)}) async-start(), calls=%async_computation.3 | async-start | bytes 10485760 | tf_op jit(solution)/shard_map/psum | solution.py:124
  189.2 7.3 %copy-start.5 = (bf16[512,4,512]{0,2,1:T(8,128)(2,1)S(1)}, bf16[512,4,512]{0,2,1:T(8,128)(2,1)}, u32[]{:S(2)}) copy-start(bf16[512,4,512]{0,2,1:T(8,128)(2,1)} %copy-done.4) | copy-start | bytes 6291460
  196.5 9.3 %copy-start.3 = (f32[512,512]{1,0:T(8,128)S(1)}, f32[512,512]{1,0:T(8,128)}, u32[]{:S(2)}) copy-start(f32[512,512]{1,0:T(8,128)} %copy-done.2) | copy-start | bytes 3145732
  334.0 6.3 %copy-start.8 = (f32[512,512]{1,0:T(8,128)S(1)}, f32[512,512]{1,0:T(8,128)}, u32[]{:S(2)}) copy-start(f32[512,512]{1,0:T(8,128)} %get-tuple-element.43) | copy-start | bytes 3145732
Sparse Core Ops, SparseCore 0:
  205.1 128.8 all-reduce.5
where the time goes:
time: 350 us; the launch traced here: 348 us
  blocking collectives  120 us (34%)
  waiting for transfers between devices  102 us (29%)
  local copies, waits for them, and re-layouts  61.6 us (18%)
  matrix products  24.7 us (7%)
  between operations  15 us (4%)
  other arithmetic  12.4 us (4%)
  starting transfers between devices  12.4 us (4%)
    psum x1, blocking collectives, local(): lax.psum((loss_sum, grad_fc, grad_gate, grad_score, grad_cls, grad_conv,...  65.5 us
    psum x1, waiting for transfers between devices, local(): lax.psum((loss_sum, grad_fc, grad_gate, grad_score, grad_cls, grad_conv,...  62.3 us
    all_to_all x1, blocking collectives, local(): lax.all_to_all(outgoing, 'enc', split_axis=0, concat_axis=0, tiled=True)  54.9 us
    scatter x1, local copies, waits for them, and re-layouts, local(): outgoing = jnp.zeros((SLOTS_DEV, positions, input_width), jnp.bfloat16).a...  40.4 us
    all_to_all x1, waiting for transfers between devices, local(): lax.all_to_all(encoded, 'enc', split_axis=0, concat_axis=0, tiled=True)  22.7 us
    all_to_all x1, waiting for transfers between devices, local(): lax.all_to_all(grad_slots, 'enc', split_axis=0, concat_axis=0, tiled=True)  16.7 us
    dot_general x3, matrix products, contract_rows(): lax.dot_general(left, right, (((0,), (0,)), ((), ())), preferred_element_...  14.5 us
    unnamed x39, local copies, waits for them, and re-layouts  11.3 us
  transfers between devices with their start and end apart: 3, of which 3 were waited for; matrix products, arithmetic and copies ran while one was open for 2% of the time, Pallas kernels for 0%

commit v1 on v0

v1 whole, which is shorter than its diff:
```python
import jax
import jax.numpy as jnp
from jax import lax
from jax.sharding import PartitionSpec as P

epsilon = 1e-05
f32, bf16 = jnp.float32, jnp.bfloat16


def round_low(x):
    return lax.reduce_precision(x, 8, 7)


def split3(x):
    high = round_low(x)
    rest = x - high
    middle = round_low(rest)
    low = round_low(rest - middle)
    return high.astype(bf16), middle.astype(bf16), low.astype(bf16)


def contract_rows(left, right):
    return lax.dot_general(
        left, right, (((0,), (0,)), ((), ())), preferred_element_type=f32
    )


def contract_cols(left, right):
    return lax.dot_general(
        left, right, (((1,), (1,)), ((), ())), preferred_element_type=f32
    )


def group_sums(member, values):
    width = values.shape[1]
    parts = contract_rows(member, jnp.concatenate(split3(values), axis=1))
    return parts[:, :width] + parts[:, width : 2 * width] + parts[:, 2 * width :]


def spread(member, values):
    return jnp.dot(
        jnp.concatenate([member] * 3, axis=1),
        jnp.concatenate(split3(values), axis=0),
        preferred_element_type=f32,
    )


def swap(x, bit):
    count = lax.axis_size("enc")
    return lax.ppermute(x, "enc", [(i, i ^ (1 << bit)) for i in range(count)])


def bit_of(bit):
    return (lax.axis_index("enc") >> bit) & 1


def sum_small(pair):
    levels = lax.axis_size("enc").bit_length() - 1
    core = bit_of(0) == 0
    mine = jnp.where(core, pair[0], pair[1])
    mine = mine + swap(jnp.where(core, pair[1], pair[0]), 0)
    for level in range(1, levels):
        mine = mine + swap(mine, level)
    other = swap(mine, 0)
    return jnp.where(core, mine, other), jnp.where(core, other, mine)


def sum_large(x, order):
    for level in order[:-1]:
        halves = x.reshape((2, x.shape[0] // 2) + x.shape[1:])
        bit = bit_of(level)
        keep = lax.dynamic_index_in_dim(halves, bit, 0, keepdims=False)
        send = lax.dynamic_index_in_dim(halves, 1 - bit, 0, keepdims=False)
        x = keep + swap(send.astype(bf16), level).astype(f32)
    x = round_low(x)
    x = x + swap(x.astype(bf16), order[-1]).astype(f32)
    x = x.astype(bf16)
    for level in order[-2::-1]:
        other = swap(x, level)
        first = bit_of(level) == 0
        x = jnp.where(
            first,
            jnp.concatenate([x, other], axis=0),
            jnp.concatenate([other, x], axis=0),
        )
    return x.astype(f32)


def sum_gradient(x):
    levels = lax.axis_size("enc").bit_length() - 1
    half = x.shape[0] // 2
    first = tuple(range(levels))
    second = (0,) + tuple(range(2, levels)) + (1,)
    return jnp.concatenate(
        [sum_large(x[:half], first), sum_large(x[half:], second)], axis=0
    )


def head_pass(
    embedded, inside, classes_of, w_fc, w_gate, w_score, w_cls, slides_all
):
    high = lax.Precision.HIGHEST
    before = jnp.dot(embedded, w_fc, preferred_element_type=f32)
    hidden = jnp.maximum(before, 0.0).astype(bf16)
    gate_pre = jnp.dot(hidden, w_gate, preferred_element_type=f32)

    def tail(gate_pre, hidden_wide, w_score, w_cls):
        half_width = gate_pre.shape[1] // 2
        mix = jnp.tanh(gate_pre[:, :half_width]) * jax.nn.sigmoid(
            gate_pre[:, half_width:]
        )
        scores = jnp.dot(mix, w_score, precision=high)
        weight = jnp.exp(scores)[:, None] * inside
        attention = weight / jnp.sum(weight, axis=0)[None, :]
        pooled = lax.dot_general(
            attention, hidden_wide, (((0,), (0,)), ((), ())), precision=high
        )
        logits = jnp.dot(pooled, w_cls, precision=high)
        target = (
            classes_of[:, None] == jnp.arange(logits.shape[1], dtype=jnp.int32)[None, :]
        ).astype(f32)
        log_total = jnp.log(jnp.sum(jnp.exp(logits), axis=1))
        return jnp.sum(log_total - jnp.sum(logits * target, axis=1)) / slides_all

    loss_sum, tail_vjp = jax.vjp(tail, gate_pre, hidden.astype(f32), w_score, w_cls)
    grad_gates, grad_hidden, grad_score, grad_cls = tail_vjp(jnp.ones((), f32))
    gates_low = grad_gates.astype(bf16)
    grad_gate = contract_rows(hidden, gates_low)
    grad_hidden = grad_hidden + contract_cols(gates_low, w_gate)
    before_low = jnp.where(before > 0, grad_hidden, 0.0).astype(bf16)
    grad_fc = contract_rows(embedded, before_low)
    grad_embedded = contract_cols(before_low, w_fc).astype(bf16)
    return loss_sum, grad_fc, grad_gate, grad_score, grad_cls, grad_embedded


def local(
    tiles, tile_counts, assign, labels, w_conv, bn_gain, bn_shift, w_fc, w_gate, w_score, w_cls
):
    devices = lax.axis_size("enc")
    own_rows, positions, input_width = tiles.shape
    emb_width = w_conv.shape[1]
    slot_rows = assign.shape[1]
    cap_rows = slot_rows // devices
    group_tiles = (
        devices // 4 * (4 + (cap_rows - 2) // 3 + 2 * (cap_rows - 2) // 3 + (cap_rows - 2))
        + devices // 2
    )
    pixel_count = float(group_tiles * positions)
    slides = tile_counts.shape[1]
    slides_all = float(devices * slides)
    counts_row = tile_counts[0]
    earlier = jnp.arange(slides)[:, None] <= jnp.arange(slides)[None, :]
    slide_end = jnp.sum(jnp.where(earlier, counts_row[:, None], 0), axis=0)
    slide_start = slide_end - counts_row
    row = jnp.arange(own_rows, dtype=jnp.int32)[:, None]
    inside = ((row >= slide_start[None, :]) & (row < slide_end[None, :])).astype(f32)
    group = assign[0] // cap_rows
    member = (group[:, None] == jnp.arange(devices, dtype=jnp.int32)[None, :]).astype(bf16)

    work = jnp.transpose(tiles, (1, 0, 2))
    before = lax.dot_general(
        work, w_conv, (((2,), (0,)), ((), ())), preferred_element_type=f32
    )
    totals = group_sums(
        member,
        jnp.concatenate([jnp.sum(before, axis=0), jnp.sum(before * before, axis=0)], axis=1),
    )
    first, second = sum_small(jnp.stack([totals[:, :emb_width], totals[:, emb_width:]]))
    mean = first / pixel_count
    variance = second / pixel_count - mean * mean
    inverse = lax.rsqrt(variance + epsilon)
    rows = spread(member, jnp.concatenate([mean, inverse], axis=1))
    row_mean, row_inverse = rows[:, :emb_width], rows[:, emb_width:]
    unit = (before - row_mean) * row_inverse
    normed = unit * bn_gain + bn_shift
    embedded = jnp.mean(jnp.maximum(normed, 0.0), axis=0).astype(bf16)

    loss_sum, grad_fc, grad_gate, grad_score, grad_cls, grad_embedded = head_pass(
        embedded, inside, labels[0], w_fc, w_gate, w_score, w_cls, slides_all
    )

    slope = jnp.where(normed > 0, 1.0, jnp.where(normed == 0, 0.5, 0.0))
    grad_normed = slope * (grad_embedded.astype(f32) / positions)[None]
    back = group_sums(
        member,
        jnp.concatenate(
            [jnp.sum(grad_normed, axis=0), jnp.sum(grad_normed * unit, axis=0)], axis=1
        ),
    )
    extra = jnp.zeros((2, 1, emb_width), f32)
    extra = extra.at[0, 0, : grad_score.shape[0]].set(grad_score)
    extra = extra.at[0, 0, grad_score.shape[0]].set(loss_sum)
    extra = extra.at[1, 0].set(grad_cls.reshape(-1))
    pair = jnp.stack([back[:, :emb_width], back[:, emb_width:]])
    shift_sums, gain_sums = sum_small(jnp.concatenate([pair, extra], axis=1))
    grad_score = shift_sums[devices, : grad_score.shape[0]]
    loss = shift_sums[devices, grad_score.shape[0]].reshape(1)
    grad_cls = gain_sums[devices].reshape(grad_cls.shape)
    shift_sums, gain_sums = shift_sums[:devices], gain_sums[:devices]
    grad_shift = jnp.sum(shift_sums, axis=0)
    grad_gain = jnp.sum(gain_sums, axis=0)
    rows = spread(
        member, jnp.concatenate([shift_sums / pixel_count, gain_sums / pixel_count], axis=1)
    )
    row_shift, row_gain = rows[:, :emb_width], rows[:, emb_width:]
    grad_before = (
        (grad_normed - row_shift - unit * row_gain) * (row_inverse * bn_gain)
    ).astype(bf16)
    grad_conv = lax.dot_general(
        work, grad_before, (((0, 1), (0, 1)), ((), ())), preferred_element_type=f32
    )
    grad_head = sum_gradient(jnp.concatenate([grad_fc, grad_gate], axis=0))
    grad_conv = sum_gradient(grad_conv)
    return (
        loss,
        grad_conv,
        grad_gain,
        grad_shift,
        grad_head[:emb_width],
        grad_head[emb_width:],
        grad_score,
        grad_cls,
    )


def solution(mesh):
    per_device = P(("groups", "enc"), None)
    placed = (P(("groups", "enc"), None, None), per_device, per_device, per_device) + (P(),) * 7
    rows_out = P("groups", None)
    return jax.shard_map(
        local,
        mesh=mesh,
        in_specs=placed,
        out_specs=(
            P("groups"),
            rows_out,
            P("groups"),
            P("groups"),
            rows_out,
            rows_out,
            P("groups"),
            rows_out,
        ),
        check_vma=False,
    )
```

time: 350 us -> 156 us (0.45)
  blocking collectives: 120 us -> 0 us
  waiting for transfers between devices: 102 us -> 30.9 us
  local copies, waits for them, and re-layouts: 61.6 us -> 20.4 us
  starting transfers between devices: 12.4 us -> 47.3 us
  between operations: 15 us -> 2.17 us
  other arithmetic: 12.4 us -> 24.5 us
  matrix products: 24.7 us -> 30.2 us
    psum x1 -> x0, blocking collectives: 65.5 us -> none  [local(): lax.psum((loss_sum, grad_fc, grad_gate, grad_score, grad_cls, grad_conv,...]
    psum x1 -> x0, waiting for transfers between devices: 62.3 us -> none  [local(): lax.psum((loss_sum, grad_fc, grad_gate, grad_score, grad_cls, grad_conv,...]
    all_to_all x1 -> x0, blocking collectives: 54.9 us -> none  [local(): lax.all_to_all(outgoing, 'enc', split_axis=0, concat_axis=0, tiled=True)]
    ppermute x0 -> x38, starting transfers between devices: none -> 47.3 us  [swap(): return lax.ppermute(x, 'enc', [(i, i ^ 1 << bit) for i in range(count)])]
    scatter x2 -> x3, local copies, waits for them, and re-layouts: 44 us -> 0.28 us  [the longest x1 0.27 us: local(): extra = extra.at[0, 0, grad_score.shape[0]].set(loss_sum)]
    all_to_all x2 -> x0, waiting for transfers between devices: 39.4 us -> none  [the longest x1 22.7 us: local(): lax.all_to_all(encoded, 'enc', split_axis=0, concat_axis=0, tiled=True)]
    ppermute x0 -> x38, waiting for transfers between devices: none -> 30.9 us  [swap(): return lax.ppermute(x, 'enc', [(i, i ^ 1 << bit) for i in range(count)])]
    dot_general x8 -> x11, matrix products: 6.91 us -> 19.2 us  [the longest x1 7.14 us: local(): lax.dot_general(work, grad_before, (((0, 1), (0, 1)), ((), ())), preferre...]
  transfers between devices with their start and end apart: 3 -> 38, of which waited for: 3 -> 18; matrix products, arithmetic and copies ran while one was open for 2% -> 18% of each run, Pallas kernels for 0% -> 0%
where the time goes in v1:
time: 156 us; the launch traced here: 155 us
  starting transfers between devices  47.3 us (30%)
  waiting for transfers between devices  30.9 us (20%)
  matrix products  30.2 us (19%)
  other arithmetic  24.5 us (16%)
  local copies, waits for them, and re-layouts  20.4 us (13%)
  between operations  2.17 us (1%)
    ppermute x38, starting transfers between devices, swap(): return lax.ppermute(x, 'enc', [(i, i ^ 1 << bit) for i in range(count)])  47.3 us
    ppermute x38, waiting for transfers between devices, swap(): return lax.ppermute(x, 'enc', [(i, i ^ 1 << bit) for i in range(count)])  30.9 us
    unnamed x63, local copies, waits for them, and re-layouts  7.23 us
    dot_general x1, matrix products, local(): lax.dot_general(work, grad_before, (((0, 1), (0, 1)), ((), ())), preferre...  7.14 us
    reduce_sum x1, other arithmetic, local(): jnp.sum(grad_normed, axis=0)  6.5 us
    dot_general x1, matrix products, local(): lax.dot_general(work, w_conv, (((2,), (0,)), ((), ())), preferred_element...  6.39 us
    dot_general x4, matrix products, contract_rows(): lax.dot_general(left, right, (((0,), (0,)), ((), ())), preferred_element_...  4.75 us
    convert_element_type x12, local copies, waits for them, and re-layouts, sum_large(): x = keep + swap(send.astype(bf16), level).astype(f32)  3.29 us
  transfers between devices with their start and end apart: 38, of which 18 were waited for; matrix products, arithmetic and copies ran while one was open for 18% of the time, Pallas kernels for 0%

profile of v1, /device:TPU:0, one launch (start us, length us, event | category | flops | bytes accessed | tf_op | source)
XLA Modules:
  0.0 155.4 jit_solution(6974103841256426355)
XLA Ops:
  1.4 3.0 %copy.33 = bf16[4,512,512]{1,2,0:T(8,128)(2,1)S(1)} copy(bf16[4,512,512]{2,0,1:T(4,128)(2,1)} %bitcast.157) | data formatting | bytes 4194304 | tf_op jit(solution)/shard_map/transpose | solution.py:160
  4.4 6.4 %fusion.105 = (f32[512,1024]{1,0:T(8,128)S(1)}, f32[512,1024]{1,0:T(8,128)S(1)}, f32[4,512,1024]{2,1,0:T(8,128)}) fusion(bf16[4,512,512]{1,2,0:T(8,128)(2,1)S(1)} %copy.33, bf16[512,1024]{1,0:T(8,128)(2,1)S(1)} %copy-done), kind=kOutput, calls=%fused_computation.225 | convolution fusion | flops 2152726528 | bytes 15728640 | tf_op jit(solution)/shard_map/dot_general | solution.py:161
  10.8 1.3 reduce-precision_convert_fusion.3
  14.5 2.9 %collective-permute-start.1 = (f32[16,1024]{1,0:T(8,128)S(1)}, f32[16,1024]{1,0:T(8,128)S(1)}, u32[]{:S(2)}, u32[]{:S(2)}) collective-permute-start(f32[16,1024]{1,0:T(8,128)S(1)} %select_add_fusion), channel_id=1, source_target_pairs={{0,2},{1,3},{2,0},{3,1},{4,6},{5,7},{6,4},{7,5},{8,10},{9,11},{10,... | collective-permute-start | bytes 196616 | tf_op jit(solution)/shard_map/ppermute | solution.py:50
  17.5 2.4 %collective-permute-done.1 = f32[16,1024]{1,0:T(8,128)S(1)} collective-permute-done((f32[16,1024]{1,0:T(8,128)S(1)}, f32[16,1024]{1,0:T(8,128)S(1)}, u32[]{:S(2)}, u32[]{:S(2)}) %collective-permute-start.1) | collective-permute-done | bytes 65568 | tf_op jit(solution)/shard_map/ppermute | solution.py:50
  19.9 2.0 %collective-permute-start.2 = (f32[16,1024]{1,0:T(8,128)S(1)}, f32[16,1024]{1,0:T(8,128)S(1)}, u32[]{:S(2)}, u32[]{:S(2)}) collective-permute-start(f32[16,1024]{1,0:T(8,128)S(1)} %add.177), channel_id=1, source_target_pairs={{0,4},{1,5},{2,6},{3,7},{4,0},{5,1},{6,2},{7,3},{8,12},{9,13},{10,... | collective-permute-start | bytes 196616 | tf_op jit(solution)/shard_map/ppermute | solution.py:50
  21.9 2.3 %collective-permute-done.2 = f32[16,1024]{1,0:T(8,128)S(1)} collective-permute-done((f32[16,1024]{1,0:T(8,128)S(1)}, f32[16,1024]{1,0:T(8,128)S(1)}, u32[]{:S(2)}, u32[]{:S(2)}) %collective-permute-start.2) | collective-permute-done | bytes 65568 | tf_op jit(solution)/shard_map/ppermute | solution.py:50
  24.2 3.0 %collective-permute-start.3 = (f32[16,1024]{1,0:T(8,128)S(1)}, f32[16,1024]{1,0:T(8,128)S(1)}, u32[]{:S(2)}, u32[]{:S(2)}) collective-permute-start(f32[16,1024]{1,0:T(8,128)S(1)} %add.178), channel_id=1, source_target_pairs={{0,8},{1,9},{2,10},{3,11},{4,12},{5,13},{6,14},{7,15},{8,0},{9,1},... | collective-permute-start | bytes 196616 | tf_op jit(solution)/shard_map/ppermute | solution.py:50
  27.3 2.2 %collective-permute-done.3 = f32[16,1024]{1,0:T(8,128)S(1)} collective-permute-done((f32[16,1024]{1,0:T(8,128)S(1)}, f32[16,1024]{1,0:T(8,128)S(1)}, u32[]{:S(2)}, u32[]{:S(2)}) %collective-permute-start.3) | collective-permute-done | bytes 65568 | tf_op jit(solution)/shard_map/ppermute | solution.py:50
  31.7 2.0 %broadcast_multiply_fusion = (f32[512,1024]{1,0:T(8,128)}, f32[512,1024]{1,0:T(8,128)S(1)}, f32[512,1024]{1,0:T(8,128)S(1)}) fusion(f32[1024]{0:T(1024)S(1)} %copy-done.21, f32[512,2048]{1,0:T(8,128)S(1)} %fusion.41), kind=kLoop, calls=%fused_computation.50 | loop fusion | flops 524288 | bytes 10489856 | tf_op jit(solution)/shard_map/mul | solution.py:207
  33.7 2.3 %slice-done.1 = s8[4194304]{0:T(1024)(128)(4,1)S(1)} async-done(((s8[8388608]{0:T(1024)(128)(4,1)}), s8[4194304]{0:T(1024)(128)(4,1)S(1)}, s32[]{:S(2)}) %slice-start.1) | async-done | bytes 4194328
  36.0 2.2 %maximum_reduce_fusion = f32[512,1024]{1,0:T(8,128)S(1)} fusion(f32[4,512,1024]{2,1,0:T(8,128)S(1)} %bitcast.142, f32[1024]{0:T(1024)S(1)} %copy-done.22, f32[1024]{0:T(1024)S(1)} %copy-done.21, f32[512,1024]{1,0:T(8,128)S(1)} %get-tuple-element.85, f32[512,1024]{1,0:T(8,128)S(1)} %get-tuple-element.86), kind=kLoop, calls=%fused_computation.2 | loop fusion | flops 12058624 | bytes 14688256 | tf_op jit(solution)/shard_map/reduce_sum | solution.py:176
  38.2 1.7 %maximum_convert_fusion.1 = (bf16[512,512]{1,0:T(8,128)(2,1)S(1)}, f32[512,512]{1,0:T(8,128)}) fusion(bf16[1024,512]{1,0:T(8,128)(2,1)S(1)} %copy-done.15, f32[512,1024]{1,0:T(8,128)S(1)} %maximum_reduce_fusion), kind=kOutput, calls=%fused_computation.52 | convolution fusion | flops 538443776 | bytes 4718592 | tf_op jit(solution)/shard_map/dot_general | solution.py:103
  43.5 2.1 %fusion.97 = f32[512,512]{1,0:T(8,128)} fusion(f32[4,512]{1,0:T(4,128)S(1)} %fusion.96, f32[4]{0:T(128)S(1)} %select_reduce_fusion, f32[512]{0:T(512)S(1)} %exp.10, s32[4]{0:T(128)S(1)} %select_reduce_fusion.2, s32[4]{0:T(128)S(1)} %fusion.81), kind=kOutput, calls=%fused_computation.223 | convolution fusion | flops 12593152 | bytes 1058864 | tf_op jit(solution)/shard_map/transpose(jvp())/dot_general | solution.py:115
  48.1 2.4 %fusion.22 = bf16[512,512]{1,0:T(8,128)(2,1)S(1)} fusion(f32[512,512]{1,0:T(8,128)} %fusion.97, bf16[512,512]{1,0:T(8,128)(2,1)} %param.25, f32[512,512]{1,0:T(8,128)} %get-tuple-element.119, f32[512,256]{1,0:T(8,128)} %get-tuple-element.98, f32[512,256]{1,0:T(8,128)S(1)} %get-tuple-element.97), kind=kOutput, calls=%fused_computation.45 | convolution fusion | flops 270008320 | bytes 4194304 | tf_op jit(solution)/shard_map/dot_general | solution.py:29
  52.3 6.5 %fusion = (f32[512,1024]{1,0:T(8,128)S(1)}, f32[512,1024]{1,0:T(8,128)S(1)}) fusion(f32[512,1024]{1,0:T(8,128)S(1)} %convert_multiply_fusion, f32[1024]{0:T(1024)S(1)} %copy-done.22, f32[1024]{0:T(1024)S(1)} %copy-done.21, f32[512,1024]{1,0:T(8,128)S(1)} %get-tuple-element.85, f32[4,512,1024]{2,1,0:T(8,128)} %get-tuple-element.117, f32[512,1024]{1,0:T(8,128)S(1)} %copy-done.3), kind=kLoop, calls=%fused_computation.4 | loop fusion | flops 24117248 | bytes 18882560 | tf_op jit(solution)/shard_map/reduce_sum | solution.py:187
  58.9 1.3 reduce-precision_convert_fusion.1
  62.4 2.4 %fusion.33 = f32[1024,512]{1,0:T(8,128)S(1)} fusion(bf16[512,512]{1,0:T(8,128)(2,1)} %copy-done.14, f32[512,1024]{1,0:T(8,128)} %copy-done.5), kind=kOutput, calls=%fused_computation.78 | convolution fusion | flops 537919488 | bytes 4718592 | tf_op jit(solution)/shard_map/dot_general | solution.py:23
  64.8 1.9 %collective-permute-start.6 = (f32[17,1024]{1,0:T(8,128)S(1)}, f32[17,1024]{1,0:T(8,128)S(1)}, u32[]{:S(2)}, u32[]{:S(2)}) collective-permute-start(f32[17,1024]{1,0:T(8,128)S(1)} %bitcast_add_fusion.12), channel_id=1, source_target_pairs={{0,2},{1,3},{2,0},{3,1},{4,6},{5,7},{6,4},{7,5},{8,10},{9,11},{10,... | collective-permute-start | bytes 208904 | tf_op jit(solution)/shard_map/ppermute | solution.py:50
  67.2 2.8 %collective-permute-done.6 = f32[17,1024]{1,0:T(8,128)S(1)} collective-permute-done((f32[17,1024]{1,0:T(8,128)S(1)}, f32[17,1024]{1,0:T(8,128)S(1)}, u32[]{:S(2)}, u32[]{:S(2)}) %collective-permute-start.6) | collective-permute-done | bytes 69664 | tf_op jit(solution)/shard_map/ppermute | solution.py:50
  70.1 1.9 %collective-permute-start.7 = (f32[17,1024]{1,0:T(8,128)S(1)}, f32[17,1024]{1,0:T(8,128)S(1)}, u32[]{:S(2)}, u32[]{:S(2)}) collective-permute-start(f32[17,1024]{1,0:T(8,128)S(1)} %add.190), channel_id=1, source_target_pairs={{0,4},{1,5},{2,6},{3,7},{4,0},{5,1},{6,2},{7,3},{8,12},{9,13},{10,... | collective-permute-start | bytes 208904 | tf_op jit(solution)/shard_map/ppermute | solution.py:50
  72.2 2.5 %collective-permute-done.7 = f32[17,1024]{1,0:T(8,128)S(1)} collective-permute-done((f32[17,1024]{1,0:T(8,128)S(1)}, f32[17,1024]{1,0:T(8,128)S(1)}, u32[]{:S(2)}, u32[]{:S(2)}) %collective-permute-start.7) | collective-permute-done | bytes 69664 | tf_op jit(solution)/shard_map/ppermute | solution.py:50
  74.8 3.0 %collective-permute-start.8 = (f32[17,1024]{1,0:T(8,128)S(1)}, f32[17,1024]{1,0:T(8,128)S(1)}, u32[]{:S(2)}, u32[]{:S(2)}) collective-permute-start(f32[17,1024]{1,0:T(8,128)S(1)} %add.191), channel_id=1, source_target_pairs={{0,8},{1,9},{2,10},{3,11},{4,12},{5,13},{6,14},{7,15},{8,0},{9,1},... | collective-permute-start | bytes 208904 | tf_op jit(solution)/shard_map/ppermute | solution.py:50
  78.6 2.0 %collective-permute-done.8 = f32[17,1024]{1,0:T(8,128)S(1)} collective-permute-done((f32[17,1024]{1,0:T(8,128)S(1)}, f32[17,1024]{1,0:T(8,128)S(1)}, u32[]{:S(2)}, u32[]{:S(2)}) %collective-permute-start.8) | collective-permute-done | bytes 69664 | tf_op jit(solution)/shard_map/ppermute | solution.py:50
  83.5 2.5 %fusion.106 = (f32[512,1024]{1,0:T(8,128)}, f32[512,1024]{1,0:T(8,128)}) fusion(f32[512,2048]{1,0:T(8,128)S(1)} %fusion.47), kind=kLoop, calls=%fused_computation.226 | loop fusion | bytes 8388608 | tf_op jit(solution)/shard_map/slice | solution.py:205
  86.0 1.3 copy-done.4
  88.5 7.1 %fusion.20 = f32[512,1024]{1,0:T(8,128)S(1)} fusion(bf16[4,512,512]{1,2,0:T(8,128)(2,1)S(1)} %copy-done.9, f32[4,512,1024]{2,1,0:T(8,128)S(1)} %bitcast.144, f32[512,1024]{1,0:T(8,128)} %get-tuple-element.84, f32[512,1024]{1,0:T(8,128)} %get-tuple-element.83, f32[512,1024]{1,0:T(8,128)} %get-tuple-element.82, f32[512,1024]{1,0:T(8,128)S(1)} %copy-done.7, ...), kind=kOutput, calls=%fused_computation.40 | convolution fusion | flops 2176843776 | bytes 25174016 | tf_op jit(solution)/shard_map/dot_general | solution.py:209
  98.8 1.3 slice.211
  102.8 1.6 %collective-permute-start.25 = (bf16[192,512]{1,0:T(8,128)(2,1)S(1)}, bf16[192,512]{1,0:T(8,128)(2,1)S(1)}, u32[]{:S(2)}, u32[]{:S(2)}) collective-permute-start(bf16[192,512]{1,0:T(8,128)(2,1)S(1)} %fusion.39), channel_id=1, source_target_pairs={{0,2},{1,3},{2,0},{3,1},{4,6},{5,7},{6,4},{7,5},{8,10},{9,11},{10,... | collective-permute-start | bytes 589832 | tf_op jit(solution)/shard_map/ppermute | solution.py:50
  105.6 1.9 %collective-permute-start.32 = (bf16[192,512]{1,0:T(8,128)(2,1)S(1)}, bf16[192,512]{1,0:T(8,128)(2,1)S(1)}, u32[]{:S(2)}, u32[]{:S(2)}) collective-permute-start(bf16[192,512]{1,0:T(8,128)(2,1)S(1)} %fusion.40), channel_id=1, source_target_pairs={{0,4},{1,5},{2,6},{3,7},{4,0},{5,1},{6,2},{7,3},{8,12},{9,13},{10,... | collective-permute-start | bytes 589832 | tf_op jit(solution)/shard_map/ppermute | solution.py:50
  107.5 2.4 %collective-permute-done.25 = bf16[192,512]{1,0:T(8,128)(2,1)S(1)} collective-permute-done((bf16[192,512]{1,0:T(8,128)(2,1)S(1)}, bf16[192,512]{1,0:T(8,128)(2,1)S(1)}, u32[]{:S(2)}, u32[]{:S(2)}) %collective-permute-start.25) | collective-permute-done | bytes 196640 | tf_op jit(solution)/shard_map/ppermute | solution.py:50
  109.9 1.9 %collective-permute-start.26 = (bf16[96,512]{1,0:T(8,128)(2,1)S(1)}, bf16[96,512]{1,0:T(8,128)(2,1)S(1)}, u32[]{:S(2)}, u32[]{:S(2)}) collective-permute-start(bf16[96,512]{1,0:T(8,128)(2,1)S(1)} %fusion.68), channel_id=1, source_target_pairs={{0,4},{1,5},{2,6},{3,7},{4,0},{5,1},{6,2},{7,3},{8,12},{9,13},{10,... | collective-permute-start | bytes 294920 | tf_op jit(solution)/shard_map/ppermute | solution.py:50
  112.8 3.4 %collective-permute-start.33 = (bf16[96,512]{1,0:T(8,128)(2,1)S(1)}, bf16[96,512]{1,0:T(8,128)(2,1)S(1)}, u32[]{:S(2)}, u32[]{:S(2)}) collective-permute-start(bf16[96,512]{1,0:T(8,128)(2,1)S(1)} %fusion.69), channel_id=1, source_target_pairs={{0,8},{1,9},{2,10},{3,11},{4,12},{5,13},{6,14},{7,15},{8,0},{9,1},... | collective-permute-start | bytes 294920 | tf_op jit(solution)/shard_map/ppermute | solution.py:50
  117.1 1.4 collective-permute-start.18
  120.6 1.8 %collective-permute-done.11 = bf16[64,1024]{1,0:T(8,128)(2,1)S(1)} collective-permute-done((bf16[64,1024]{1,0:T(8,128)(2,1)S(1)}, bf16[64,1024]{1,0:T(8,128)(2,1)S(1)}, u32[]{:S(2)}, u32[]{:S(2)}) %collective-permute-start.11) | collective-permute-done | bytes 131104 | tf_op jit(solution)/shard_map/ppermute | solution.py:50
  122.4 1.9 %collective-permute-start.12 = (bf16[32,1024]{1,0:T(8,128)(2,1)S(1)}, bf16[32,1024]{1,0:T(8,128)(2,1)S(1)}, u32[]{:S(2)}, u32[]{:S(2)}) collective-permute-start(bf16[32,1024]{1,0:T(8,128)(2,1)S(1)} %fusion.73), channel_id=1, source_target_pairs={{0,4},{1,5},{2,6},{3,7},{4,0},{5,1},{6,2},{7,3},{8,12},{9,13},{10,... | collective-permute-start | bytes 196616 | tf_op jit(solution)/shard_map/ppermute | solution.py:50
  124.3 3.1 %collective-permute-start.19 = (bf16[32,1024]{1,0:T(8,128)(2,1)S(1)}, bf16[32,1024]{1,0:T(8,128)(2,1)S(1)}, u32[]{:S(2)}, u32[]{:S(2)}) collective-permute-start(bf16[32,1024]{1,0:T(8,128)(2,1)S(1)} %fusion.74), channel_id=1, source_target_pairs={{0,8},{1,9},{2,10},{3,11},{4,12},{5,13},{6,14},{7,15},{8,0},{9,1},... | collective-permute-start | bytes 196616 | tf_op jit(solution)/shard_map/ppermute | solution.py:50
  129.2 1.4 collective-permute-start.13
  130.7 1.5 collective-permute-done.19
  133.3 2.0 %collective-permute-done.13 = bf16[32,1024]{1,0:T(8,128)(2,1)S(1)} collective-permute-done((bf16[32,1024]{1,0:T(8,128)(2,1)S(1)}, bf16[32,1024]{1,0:T(8,128)(2,1)S(1)}, u32[]{:S(2)}, u32[]{:S(2)}) %collective-permute-start.13) | collective-permute-done | bytes 65568 | tf_op jit(solution)/shard_map/ppermute | solution.py:50
  135.3 1.7 %collective-permute-start.14 = (bf16[32,1024]{1,0:T(8,128)(2,1)S(1)}, bf16[32,1024]{1,0:T(8,128)(2,1)S(1)}, u32[]{:S(2)}, u32[]{:S(2)}) collective-permute-start(bf16[32,1024]{1,0:T(8,128)(2,1)S(1)} %add_convert_fusion.4), channel_id=1, source_target_pairs={{0,4},{1,5},{2,6},{3,7},{4,0},{5,1},{6,2},{7,3},{8,12},{9,13},{10,... | collective-permute-start | bytes 196616 | tf_op jit(solution)/shard_map/ppermute | solution.py:50
  137.1 1.8 %collective-permute-start.21 = (bf16[32,1024]{1,0:T(8,128)(2,1)S(1)}, bf16[32,1024]{1,0:T(8,128)(2,1)S(1)}, u32[]{:S(2)}, u32[]{:S(2)}) collective-permute-start(bf16[32,1024]{1,0:T(8,128)(2,1)S(1)} %add_convert_fusion.3), channel_id=1, source_target_pairs={{0,8},{1,9},{2,10},{3,11},{4,12},{5,13},{6,14},{7,15},{8,0},{9,1},... | collective-permute-start | bytes 196616 | tf_op jit(solution)/shard_map/ppermute | solution.py:50
  140.3 2.9 %collective-permute-start.15 = (bf16[64,1024]{1,0:T(8,128)(2,1)S(1)}, bf16[64,1024]{1,0:T(8,128)(2,1)S(1)}, u32[]{:S(2)}, u32[]{:S(2)}) collective-permute-start(bf16[64,1024]{1,0:T(8,128)(2,1)S(1)} %maximum_select_fusion.10), channel_id=1, source_target_pairs={{0,2},{1,3},{2,0},{3,1},{4,6},{5,7},{6,4},{7,5},{8,10},{9,11},{10,... | collective-permute-start | bytes 393224 | tf_op jit(solution)/shard_map/ppermute | solution.py:50
  143.5 1.9 %collective-permute-start.36 = (bf16[192,512]{1,0:T(8,128)(2,1)S(1)}, bf16[192,512]{1,0:T(8,128)(2,1)S(1)}, u32[]{:S(2)}, u32[]{:S(2)}) collective-permute-start(bf16[192,512]{1,0:T(8,128)(2,1)S(1)} %maximum_select_fusion.9), channel_id=1, source_target_pairs={{0,4},{1,5},{2,6},{3,7},{4,0},{5,1},{6,2},{7,3},{8,12},{9,13},{10,... | collective-permute-start | bytes 589832 | tf_op jit(solution)/shard_map/ppermute | solution.py:50
  146.3 1.9 %collective-permute-done.22 = bf16[64,1024]{1,0:T(8,128)(2,1)S(1)} collective-permute-done((bf16[64,1024]{1,0:T(8,128)(2,1)S(1)}, bf16[64,1024]{1,0:T(8,128)(2,1)S(1)}, u32[]{:S(2)}, u32[]{:S(2)}) %collective-permute-start.22) | collective-permute-done | bytes 131104 | tf_op jit(solution)/shard_map/ppermute | solution.py:50
  149.1 1.3 collective-permute-done.36
  150.8 1.6 %maximum_convert_fusion = f32[512,1024]{1,0:T(8,128)} fusion(bf16[256,1024]{1,0:T(8,128)(2,1)S(1)} %maximum_select_fusion.3, bf16[256,1024]{1,0:T(8,128)(2,1)S(1)} %maximum_select_fusion.2), kind=kLoop, calls=%fused_computation.47 | loop fusion | flops 2097152 | bytes 3145728 | tf_op jit(solution)/shard_map/concatenate | solution.py:94
  153.9 1.5 pad_maximum_fusion.2
  (204 shorter events, 39.9 us)
Async XLA Ops:
  4.4 6.4 %copy-start.8 = (bf16[4,512,512]{1,2,0:T(8,128)(2,1)}, bf16[4,512,512]{1,2,0:T(8,128)(2,1)S(1)}, u32[]{:S(2)}) copy-start(bf16[4,512,512]{1,2,0:T(8,128)(2,1)S(1)} %copy.33) | copy-start | bytes 6291460
  12.1 15.1 %copy-start.26 = (s32[1,4]{1,0:T(1,128)S(1)}, s32[1,4]{1,0:T(1,128)}, u32[]{:S(2)}) copy-start(s32[1,4]{1,0:T(1,128)} %param.18) | copy-start | bytes 52
  13.1 1.4 collective-permute-start
  14.5 5.3 %collective-permute-start.1 = (f32[16,1024]{1,0:T(8,128)S(1)}, f32[16,1024]{1,0:T(8,128)S(1)}, u32[]{:S(2)}, u32[]{:S(2)}) collective-permute-start(f32[16,1024]{1,0:T(8,128)S(1)} %select_add_fusion), channel_id=1, source_target_pairs={{0,2},{1,3},{2,0},{3,1},{4,6},{5,7},{6,4},{7,5},{8,10},{9,11},{10,... | collective-permute-start | bytes 196616 | tf_op jit(solution)/shard_map/ppermute | solution.py:50
  19.9 4.3 %collective-permute-start.2 = (f32[16,1024]{1,0:T(8,128)S(1)}, f32[16,1024]{1,0:T(8,128)S(1)}, u32[]{:S(2)}, u32[]{:S(2)}) collective-permute-start(f32[16,1024]{1,0:T(8,128)S(1)} %add.177), channel_id=1, source_target_pairs={{0,4},{1,5},{2,6},{3,7},{4,0},{5,1},{6,2},{7,3},{8,12},{9,13},{10,... | collective-permute-start | bytes 196616 | tf_op jit(solution)/shard_map/ppermute | solution.py:50
  24.2 5.2 %collective-permute-start.3 = (f32[16,1024]{1,0:T(8,128)S(1)}, f32[16,1024]{1,0:T(8,128)S(1)}, u32[]{:S(2)}, u32[]{:S(2)}) collective-permute-start(f32[16,1024]{1,0:T(8,128)S(1)} %add.178), channel_id=1, source_target_pairs={{0,8},{1,9},{2,10},{3,11},{4,12},{5,13},{6,14},{7,15},{8,0},{9,1},... | collective-permute-start | bytes 196616 | tf_op jit(solution)/shard_map/ppermute | solution.py:50
  29.5 1.3 collective-permute-start.4
  50.5 8.3 %copy-start.14 = (bf16[512,512]{1,0:T(8,128)(2,1)}, bf16[512,512]{1,0:T(8,128)(2,1)S(1)}, u32[]{:S(2)}) copy-start(bf16[512,512]{1,0:T(8,128)(2,1)S(1)} %fusion.22) | copy-start | bytes 1572868
  52.3 6.5 %copy-start.6 = (f32[512,1024]{1,0:T(8,128)}, f32[512,1024]{1,0:T(8,128)S(1)}, u32[]{:S(2)}) copy-start(f32[512,1024]{1,0:T(8,128)S(1)} %convert_multiply_fusion) | copy-start | bytes 6291460
  62.1 2.6 %collective-permute-start.5 = (f32[17,1024]{1,0:T(8,128)S(1)}, f32[17,1024]{1,0:T(8,128)S(1)}, u32[]{:S(2)}, u32[]{:S(2)}) collective-permute-start(f32[17,1024]{1,0:T(8,128)S(1)} %select_bitcast_fusion), channel_id=1, source_target_pairs={{0,1},{1,0},{2,3},{3,2},{4,5},{5,4},{6,7},{7,6},{8,9},{9,8},{10,11... | collective-permute-start | bytes 208904 | tf_op jit(solution)/shard_map/ppermute | solution.py:50
  64.8 5.2 %collective-permute-start.6 = (f32[17,1024]{1,0:T(8,128)S(1)}, f32[17,1024]{1,0:T(8,128)S(1)}, u32[]{:S(2)}, u32[]{:S(2)}) collective-permute-start(f32[17,1024]{1,0:T(8,128)S(1)} %bitcast_add_fusion.12), channel_id=1, source_target_pairs={{0,2},{1,3},{2,0},{3,1},{4,6},{5,7},{6,4},{7,5},{8,10},{9,11},{10,... | collective-permute-start | bytes 208904 | tf_op jit(solution)/shard_map/ppermute | solution.py:50
  70.1 4.7 %collective-permute-start.7 = (f32[17,1024]{1,0:T(8,128)S(1)}, f32[17,1024]{1,0:T(8,128)S(1)}, u32[]{:S(2)}, u32[]{:S(2)}) collective-permute-start(f32[17,1024]{1,0:T(8,128)S(1)} %add.190), channel_id=1, source_target_pairs={{0,4},{1,5},{2,6},{3,7},{4,0},{5,1},{6,2},{7,3},{8,12},{9,13},{10,... | collective-permute-start | bytes 208904 | tf_op jit(solution)/shard_map/ppermute | solution.py:50
  71.9 14.0 %slice-start.2 = ((s8[8388608]{0:T(1024)(128)(4,1)}), s8[4194304]{0:T(1024)(128)(4,1)S(1)}, s32[]{:S(2)}) async-start(s8[8388608]{0:T(1024)(128)(4,1)} %bitcast.143), calls=%async_computation.2 | async-start | bytes 8388608
  72.2 10.4 %copy-start.10 = (f32[768,512]{1,0:T(8,128)}, f32[768,512]{1,0:T(8,128)S(1)}, u32[]{:S(2)}) copy-start(f32[768,512]{1,0:T(8,128)S(1)} %get-tuple-element.94) | copy-start | bytes 4718596
  72.2 10.4 %copy-start.12 = (f32[768,512]{1,0:T(8,128)}, f32[768,512]{1,0:T(8,128)S(1)}, u32[]{:S(2)}) copy-start(f32[768,512]{1,0:T(8,128)S(1)} %get-tuple-element.93) | copy-start | bytes 4718596
  74.8 5.8 %collective-permute-start.8 = (f32[17,1024]{1,0:T(8,128)S(1)}, f32[17,1024]{1,0:T(8,128)S(1)}, u32[]{:S(2)}, u32[]{:S(2)}) collective-permute-start(f32[17,1024]{1,0:T(8,128)S(1)} %add.191), channel_id=1, source_target_pairs={{0,8},{1,9},{2,10},{3,11},{4,12},{5,13},{6,14},{7,15},{8,0},{9,1},... | collective-permute-start | bytes 208904 | tf_op jit(solution)/shard_map/ppermute | solution.py:50
  78.6 22.9 %collective-permute-start.24 = (bf16[384,512]{1,0:T(8,128)(2,1)}, bf16[384,512]{1,0:T(8,128)(2,1)S(1)}, u32[]{:S(2)}, u32[]{:S(2)}) collective-permute-start(bf16[384,512]{1,0:T(8,128)(2,1)} %fusion.35), channel_id=1, source_target_pairs={{0,1},{1,0},{2,3},{3,2},{4,5},{5,4},{6,7},{7,6},{8,9},{9,8},{10,11... | collective-permute-start | bytes 1179656 | tf_op jit(solution)/shard_map/ppermute | solution.py:50
  80.6 1.4 collective-permute-start.9
  81.5 22.9 %collective-permute-start.31 = (bf16[384,512]{1,0:T(8,128)(2,1)}, bf16[384,512]{1,0:T(8,128)(2,1)}, u32[]{:S(2)}, u32[]{:S(2)}) collective-permute-start(bf16[384,512]{1,0:T(8,128)(2,1)} %fusion.36), channel_id=1, source_target_pairs={{0,1},{1,0},{2,3},{3,2},{4,5},{5,4},{6,7},{7,6},{8,9},{9,8},{10,11... | collective-permute-start | bytes 1179656 | tf_op jit(solution)/shard_map/ppermute | solution.py:50
  83.5 5.0 %copy-start.9 = (bf16[4,512,512]{1,2,0:T(8,128)(2,1)S(1)}, bf16[4,512,512]{1,2,0:T(8,128)(2,1)}, u32[]{:S(2)}) copy-start(bf16[4,512,512]{1,2,0:T(8,128)(2,1)} %copy-done.8) | copy-start | bytes 6291460
  95.8 8.6 %copy-start.11 = (f32[768,512]{1,0:T(8,128)S(1)}, f32[768,512]{1,0:T(8,128)}, u32[]{:S(2)}) copy-start(f32[768,512]{1,0:T(8,128)} %copy-done.10) | copy-start | bytes 4718596
  101.0 15.3 %collective-permute-start.10 = (bf16[128,1024]{1,0:T(8,128)(2,1)}, bf16[128,1024]{1,0:T(8,128)(2,1)S(1)}, u32[]{:S(2)}, u32[]{:S(2)}) collective-permute-start(bf16[128,1024]{1,0:T(8,128)(2,1)} %fusion.37), channel_id=1, source_target_pairs={{0,1},{1,0},{2,3},{3,2},{4,5},{5,4},{6,7},{7,6},{8,9},{9,8},{10,11... | collective-permute-start | bytes 786440 | tf_op jit(solution)/shard_map/ppermute | solution.py:50
  101.1 15.9 %collective-permute-start.17 = (bf16[128,1024]{1,0:T(8,128)(2,1)}, bf16[128,1024]{1,0:T(8,128)(2,1)S(1)}, u32[]{:S(2)}, u32[]{:S(2)}) collective-permute-start(bf16[128,1024]{1,0:T(8,128)(2,1)} %fusion.38), channel_id=1, source_target_pairs={{0,1},{1,0},{2,3},{3,2},{4,5},{5,4},{6,7},{7,6},{8,9},{9,8},{10,11... | collective-permute-start | bytes 786440 | tf_op jit(solution)/shard_map/ppermute | solution.py:50
  102.8 13.5 %copy-start.18 = (f32[256,1024]{1,0:T(8,128)S(1)}, f32[256,1024]{1,0:T(8,128)}, u32[]{:S(2)}) copy-start(f32[256,1024]{1,0:T(8,128)} %copy-done.17) | copy-start | bytes 3145732
  102.8 7.0 %collective-permute-start.25 = (bf16[192,512]{1,0:T(8,128)(2,1)S(1)}, bf16[192,512]{1,0:T(8,128)(2,1)S(1)}, u32[]{:S(2)}, u32[]{:S(2)}) collective-permute-start(bf16[192,512]{1,0:T(8,128)(2,1)S(1)} %fusion.39), channel_id=1, source_target_pairs={{0,2},{1,3},{2,0},{3,1},{4,6},{5,7},{6,4},{7,5},{8,10},{9,11},{10,... | collective-permute-start | bytes 589832 | tf_op jit(solution)/shard_map/ppermute | solution.py:50
  105.6 7.2 %collective-permute-start.32 = (bf16[192,512]{1,0:T(8,128)(2,1)S(1)}, bf16[192,512]{1,0:T(8,128)(2,1)S(1)}, u32[]{:S(2)}, u32[]{:S(2)}) collective-permute-start(bf16[192,512]{1,0:T(8,128)(2,1)S(1)} %fusion.40), channel_id=1, source_target_pairs={{0,4},{1,5},{2,6},{3,7},{4,0},{5,1},{6,2},{7,3},{8,12},{9,13},{10,... | collective-permute-start | bytes 589832 | tf_op jit(solution)/shard_map/ppermute | solution.py:50
  109.9 8.6 %collective-permute-start.26 = (bf16[96,512]{1,0:T(8,128)(2,1)S(1)}, bf16[96,512]{1,0:T(8,128)(2,1)S(1)}, u32[]{:S(2)}, u32[]{:S(2)}) collective-permute-start(bf16[96,512]{1,0:T(8,128)(2,1)S(1)} %fusion.68), channel_id=1, source_target_pairs={{0,4},{1,5},{2,6},{3,7},{4,0},{5,1},{6,2},{7,3},{8,12},{9,13},{10,... | collective-permute-start | bytes 294920 | tf_op jit(solution)/shard_map/ppermute | solution.py:50
  112.8 7.0 %collective-permute-start.33 = (bf16[96,512]{1,0:T(8,128)(2,1)S(1)}, bf16[96,512]{1,0:T(8,128)(2,1)S(1)}, u32[]{:S(2)}, u32[]{:S(2)}) collective-permute-start(bf16[96,512]{1,0:T(8,128)(2,1)S(1)} %fusion.69), channel_id=1, source_target_pairs={{0,8},{1,9},{2,10},{3,11},{4,12},{5,13},{6,14},{7,15},{8,0},{9,1},... | collective-permute-start | bytes 294920 | tf_op jit(solution)/shard_map/ppermute | solution.py:50
  116.4 6.0 %collective-permute-start.11 = (bf16[64,1024]{1,0:T(8,128)(2,1)S(1)}, bf16[64,1024]{1,0:T(8,128)(2,1)S(1)}, u32[]{:S(2)}, u32[]{:S(2)}) collective-permute-start(bf16[64,1024]{1,0:T(8,128)(2,1)S(1)} %fusion.62), channel_id=1, source_target_pairs={{0,2},{1,3},{2,0},{3,1},{4,6},{5,7},{6,4},{7,5},{8,10},{9,11},{10,... | collective-permute-start | bytes 393224 | tf_op jit(solution)/shard_map/ppermute | solution.py:50
  117.1 7.1 %collective-permute-start.18 = (bf16[64,1024]{1,0:T(8,128)(2,1)S(1)}, bf16[64,1024]{1,0:T(8,128)(2,1)S(1)}, u32[]{:S(2)}, u32[]{:S(2)}) collective-permute-start(bf16[64,1024]{1,0:T(8,128)(2,1)S(1)} %fusion.63), channel_id=1, source_target_pairs={{0,4},{1,5},{2,6},{3,7},{4,0},{5,1},{6,2},{7,3},{8,12},{9,13},{10,... | collective-permute-start | bytes 393224 | tf_op jit(solution)/shard_map/ppermute | solution.py:50
  118.6 8.8 %collective-permute-start.27 = (bf16[96,512]{1,0:T(8,128)(2,1)S(1)}, bf16[96,512]{1,0:T(8,128)(2,1)S(1)}, u32[]{:S(2)}, u32[]{:S(2)}) collective-permute-start(bf16[96,512]{1,0:T(8,128)(2,1)S(1)} %fusion.66), channel_id=1, source_target_pairs={{0,8},{1,9},{2,10},{3,11},{4,12},{5,13},{6,14},{7,15},{8,0},{9,1},... | collective-permute-start | bytes 294920 | tf_op jit(solution)/shard_map/ppermute | solution.py:50
  119.8 7.7 %collective-permute-start.34 = (bf16[96,512]{1,0:T(8,128)(2,1)S(1)}, bf16[96,512]{1,0:T(8,128)(2,1)S(1)}, u32[]{:S(2)}, u32[]{:S(2)}) collective-permute-start(bf16[96,512]{1,0:T(8,128)(2,1)S(1)} %fusion.67), channel_id=1, source_target_pairs={{0,2},{1,3},{2,0},{3,1},{4,6},{5,7},{6,4},{7,5},{8,10},{9,11},{10,... | collective-permute-start | bytes 294920 | tf_op jit(solution)/shard_map/ppermute | solution.py:50
  122.4 6.8 %collective-permute-start.12 = (bf16[32,1024]{1,0:T(8,128)(2,1)S(1)}, bf16[32,1024]{1,0:T(8,128)(2,1)S(1)}, u32[]{:S(2)}, u32[]{:S(2)}) collective-permute-start(bf16[32,1024]{1,0:T(8,128)(2,1)S(1)} %fusion.73), channel_id=1, source_target_pairs={{0,4},{1,5},{2,6},{3,7},{4,0},{5,1},{6,2},{7,3},{8,12},{9,13},{10,... | collective-permute-start | bytes 196616 | tf_op jit(solution)/shard_map/ppermute | solution.py:50
  124.3 7.8 %collective-permute-start.19 = (bf16[32,1024]{1,0:T(8,128)(2,1)S(1)}, bf16[32,1024]{1,0:T(8,128)(2,1)S(1)}, u32[]{:S(2)}, u32[]{:S(2)}) collective-permute-start(bf16[32,1024]{1,0:T(8,128)(2,1)S(1)} %fusion.74), channel_id=1, source_target_pairs={{0,8},{1,9},{2,10},{3,11},{4,12},{5,13},{6,14},{7,15},{8,0},{9,1},... | collective-permute-start | bytes 196616 | tf_op jit(solution)/shard_map/ppermute | solution.py:50
  127.4 11.5 %collective-permute-start.28 = (bf16[96,512]{1,0:T(8,128)(2,1)S(1)}, bf16[96,512]{1,0:T(8,128)(2,1)S(1)}, u32[]{:S(2)}, u32[]{:S(2)}) collective-permute-start(bf16[96,512]{1,0:T(8,128)(2,1)S(1)} %add_convert_fusion.2), channel_id=1, source_target_pairs={{0,4},{1,5},{2,6},{3,7},{4,0},{5,1},{6,2},{7,3},{8,12},{9,13},{10,... | collective-permute-start | bytes 294920 | tf_op jit(solution)/shard_map/ppermute | solution.py:50
  127.6 15.9 %collective-permute-start.35 = (bf16[96,512]{1,0:T(8,128)(2,1)S(1)}, bf16[96,512]{1,0:T(8,128)(2,1)S(1)}, u32[]{:S(2)}, u32[]{:S(2)}) collective-permute-start(bf16[96,512]{1,0:T(8,128)(2,1)S(1)} %add_convert_fusion.1), channel_id=1, source_target_pairs={{0,8},{1,9},{2,10},{3,11},{4,12},{5,13},{6,14},{7,15},{8,0},{9,1},... | collective-permute-start | bytes 294920 | tf_op jit(solution)/shard_map/ppermute | solution.py:50
  129.2 6.1 %collective-permute-start.13 = (bf16[32,1024]{1,0:T(8,128)(2,1)S(1)}, bf16[32,1024]{1,0:T(8,128)(2,1)S(1)}, u32[]{:S(2)}, u32[]{:S(2)}) collective-permute-start(bf16[32,1024]{1,0:T(8,128)(2,1)S(1)} %fusion.71), channel_id=1, source_target_pairs={{0,8},{1,9},{2,10},{3,11},{4,12},{5,13},{6,14},{7,15},{8,0},{9,1},... | collective-permute-start | bytes 196616 | tf_op jit(solution)/shard_map/ppermute | solution.py:50
  132.2 4.9 %collective-permute-start.20 = (bf16[32,1024]{1,0:T(8,128)(2,1)S(1)}, bf16[32,1024]{1,0:T(8,128)(2,1)S(1)}, u32[]{:S(2)}, u32[]{:S(2)}) collective-permute-start(bf16[32,1024]{1,0:T(8,128)(2,1)S(1)} %fusion.72), channel_id=1, source_target_pairs={{0,2},{1,3},{2,0},{3,1},{4,6},{5,7},{6,4},{7,5},{8,10},{9,11},{10,... | collective-permute-start | bytes 196616 | tf_op jit(solution)/shard_map/ppermute | solution.py:50
  135.3 4.9 %collective-permute-start.14 = (bf16[32,1024]{1,0:T(8,128)(2,1)S(1)}, bf16[32,1024]{1,0:T(8,128)(2,1)S(1)}, u32[]{:S(2)}, u32[]{:S(2)}) collective-permute-start(bf16[32,1024]{1,0:T(8,128)(2,1)S(1)} %add_convert_fusion.4), channel_id=1, source_target_pairs={{0,4},{1,5},{2,6},{3,7},{4,0},{5,1},{6,2},{7,3},{8,12},{9,13},{10,... | collective-permute-start | bytes 196616 | tf_op jit(solution)/shard_map/ppermute | solution.py:50
  137.1 6.1 %collective-permute-start.21 = (bf16[32,1024]{1,0:T(8,128)(2,1)S(1)}, bf16[32,1024]{1,0:T(8,128)(2,1)S(1)}, u32[]{:S(2)}, u32[]{:S(2)}) collective-permute-start(bf16[32,1024]{1,0:T(8,128)(2,1)S(1)} %add_convert_fusion.3), channel_id=1, source_target_pairs={{0,8},{1,9},{2,10},{3,11},{4,12},{5,13},{6,14},{7,15},{8,0},{9,1},... | collective-permute-start | bytes 196616 | tf_op jit(solution)/shard_map/ppermute | solution.py:50
  139.0 9.4 %collective-permute-start.29 = (bf16[192,512]{1,0:T(8,128)(2,1)S(1)}, bf16[192,512]{1,0:T(8,128)(2,1)S(1)}, u32[]{:S(2)}, u32[]{:S(2)}) collective-permute-start(bf16[192,512]{1,0:T(8,128)(2,1)S(1)} %maximum_select_fusion.8), channel_id=1, source_target_pairs={{0,2},{1,3},{2,0},{3,1},{4,6},{5,7},{6,4},{7,5},{8,10},{9,11},{10,... | collective-permute-start | bytes 589832 | tf_op jit(solution)/shard_map/ppermute | solution.py:50
  140.3 5.9 %collective-permute-start.15 = (bf16[64,1024]{1,0:T(8,128)(2,1)S(1)}, bf16[64,1024]{1,0:T(8,128)(2,1)S(1)}, u32[]{:S(2)}, u32[]{:S(2)}) collective-permute-start(bf16[64,1024]{1,0:T(8,128)(2,1)S(1)} %maximum_select_fusion.10), channel_id=1, source_target_pairs={{0,2},{1,3},{2,0},{3,1},{4,6},{5,7},{6,4},{7,5},{8,10},{9,11},{10,... | collective-permute-start | bytes 393224 | tf_op jit(solution)/shard_map/ppermute | solution.py:50
  143.2 5.0 %collective-permute-start.22 = (bf16[64,1024]{1,0:T(8,128)(2,1)S(1)}, bf16[64,1024]{1,0:T(8,128)(2,1)S(1)}, u32[]{:S(2)}, u32[]{:S(2)}) collective-permute-start(bf16[64,1024]{1,0:T(8,128)(2,1)S(1)} %maximum_select_fusion.11), channel_id=1, source_target_pairs={{0,4},{1,5},{2,6},{3,7},{4,0},{5,1},{6,2},{7,3},{8,12},{9,13},{10,... | collective-permute-start | bytes 393224 | tf_op jit(solution)/shard_map/ppermute | solution.py:50
  143.5 6.8 %collective-permute-start.36 = (bf16[192,512]{1,0:T(8,128)(2,1)S(1)}, bf16[192,512]{1,0:T(8,128)(2,1)S(1)}, u32[]{:S(2)}, u32[]{:S(2)}) collective-permute-start(bf16[192,512]{1,0:T(8,128)(2,1)S(1)} %maximum_select_fusion.9), channel_id=1, source_target_pairs={{0,4},{1,5},{2,6},{3,7},{4,0},{5,1},{6,2},{7,3},{8,12},{9,13},{10,... | collective-permute-start | bytes 589832 | tf_op jit(solution)/shard_map/ppermute | solution.py:50
  146.2 4.3 %collective-permute-start.16 = (bf16[128,1024]{1,0:T(8,128)(2,1)S(1)}, bf16[128,1024]{1,0:T(8,128)(2,1)S(1)}, u32[]{:S(2)}, u32[]{:S(2)}) collective-permute-start(bf16[128,1024]{1,0:T(8,128)(2,1)S(1)} %maximum_select_fusion.6), channel_id=1, source_target_pairs={{0,1},{1,0},{2,3},{3,2},{4,5},{5,4},{6,7},{7,6},{8,9},{9,8},{10,11... | collective-permute-start | bytes 786440 | tf_op jit(solution)/shard_map/ppermute | solution.py:50
  148.3 2.4 %collective-permute-start.23 = (bf16[128,1024]{1,0:T(8,128)(2,1)S(1)}, bf16[128,1024]{1,0:T(8,128)(2,1)S(1)}, u32[]{:S(2)}, u32[]{:S(2)}) collective-permute-start(bf16[128,1024]{1,0:T(8,128)(2,1)S(1)} %maximum_select_fusion.7), channel_id=1, source_target_pairs={{0,1},{1,0},{2,3},{3,2},{4,5},{5,4},{6,7},{7,6},{8,9},{9,8},{10,11... | collective-permute-start | bytes 786440 | tf_op jit(solution)/shard_map/ppermute | solution.py:50
  148.5 5.2 %collective-permute-start.30 = (bf16[384,512]{1,0:T(8,128)(2,1)S(1)}, bf16[384,512]{1,0:T(8,128)(2,1)S(1)}, u32[]{:S(2)}, u32[]{:S(2)}) collective-permute-start(bf16[384,512]{1,0:T(8,128)(2,1)S(1)} %maximum_select_fusion.4), channel_id=1, source_target_pairs={{0,1},{1,0},{2,3},{3,2},{4,5},{5,4},{6,7},{7,6},{8,9},{9,8},{10,11... | collective-permute-start | bytes 1179656 | tf_op jit(solution)/shard_map/ppermute | solution.py:50
  150.5 1.9 %collective-permute-start.37 = (bf16[384,512]{1,0:T(8,128)(2,1)S(1)}, bf16[384,512]{1,0:T(8,128)(2,1)S(1)}, u32[]{:S(2)}, u32[]{:S(2)}) collective-permute-start(bf16[384,512]{1,0:T(8,128)(2,1)S(1)} %maximum_select_fusion.5), channel_id=1, source_target_pairs={{0,1},{1,0},{2,3},{3,2},{4,5},{5,4},{6,7},{7,6},{8,9},{9,8},{10,11... | collective-permute-start | bytes 1179656 | tf_op jit(solution)/shard_map/ppermute | solution.py:50
  (21 other events, 54.4 us)

commit v2 on v0

v2 whole, which is shorter than its diff:
```python
import functools
import math

import jax
import jax.numpy as jnp
from jax import lax
from jax.experimental import pallas as pl
from jax.experimental.pallas import tpu as pltpu
from jax.sharding import PartitionSpec as P

epsilon = 1e-05
f32, bf16 = jnp.float32, jnp.bfloat16
CHUNK = 128
EXTRA = 128


def split3(x):
    high = x.astype(bf16)
    rest = x - high.astype(f32)
    middle = rest.astype(bf16)
    low = (rest - middle.astype(f32)).astype(bf16)
    return high, middle, low


def contract_rows(left, right):
    return lax.dot_general(
        left, right, (((0,), (0,)), ((), ())), preferred_element_type=f32
    )


def contract_cols(left, right):
    return lax.dot_general(
        left, right, (((1,), (1,)), ((), ())), preferred_element_type=f32
    )


def matmul(left, right):
    return jnp.dot(left, right, preferred_element_type=f32)


def one_hot(assign, groups, cap_rows):
    low = lax.broadcasted_iota(jnp.int32, (groups, assign.shape[1]), 0) * cap_rows
    return jnp.where((assign >= low) & (assign < low + cap_rows), 1.0, 0.0)


def group_sums(member, values):
    high = values.astype(bf16)
    low = (values - high.astype(f32)).astype(bf16)
    return matmul(member, high) + matmul(member, low)


def spread(member, values):
    return contract_rows(
        jnp.concatenate([member] * 3, axis=0).astype(bf16),
        jnp.concatenate(split3(values), axis=0),
    )


def moments(first, second, pixel_count):
    mean = first * (1.0 / pixel_count)
    variance = second * (1.0 / pixel_count) - mean * mean
    return mean, lax.rsqrt(variance + epsilon)


def conv_kernel(cap_rows, x_ref, assign_ref, w_ref, before_ref, sums_ref, inputs_ref):
    step = pl.program_id(0)
    positions, tiles, width = x_ref.shape
    groups = sums_ref.shape[1]
    x = x_ref[...].reshape(positions * tiles, width)
    before = matmul(x, w_ref[...])
    before_ref[...] = before.reshape(before_ref.shape)
    parts = [before[p * tiles : (p + 1) * tiles] for p in range(positions)]
    second = sum([v * v for v in parts[1:]], parts[0] * parts[0])
    member = one_hot(assign_ref[...], groups, cap_rows).astype(bf16)

    @pl.when(step == 0)
    def _():
        sums_ref[1] = jnp.zeros(sums_ref.shape[1:], f32)
        inputs_ref[...] = jnp.zeros_like(inputs_ref)

    inputs_ref[...] += matmul(jnp.concatenate([member] * positions, axis=1), x)
    sums_ref[1] += group_sums(member, second)

    @pl.when(step == pl.num_programs(0) - 1)
    def _():
        terms = matmul(jnp.concatenate(split3(inputs_ref[...]), axis=0), w_ref[...])
        sums_ref[0] = terms[:groups] + terms[groups : 2 * groups] + terms[2 * groups :]


def head_kernel(
    cap_rows,
    pixel_count,
    slides_all,
    counts_ref,
    labels_ref,
    core_ref,
    before_ref,
    assign_ref,
    assign_all_ref,
    first_ref,
    second_ref,
    gain_ref,
    shift_ref,
    w_fc_ref,
    w_gate_ref,
    w_score_ref,
    w_cls_ref,
    send_ref,
    keep_ref,
    grad_embedded_ref,
    sums_ref,
    embedded_ref,
    count_ref,
    total_ref,
    grad_ref,
    low_ref,
    grad_low_ref,
    copied,
):
    step = pl.program_id(0)
    positions, tiles, emb_width = before_ref.shape
    groups = first_ref.shape[0]
    mean, inverse = moments(first_ref[...], second_ref[...], pixel_count)
    scale = inverse * gain_ref[...]
    offset = shift_ref[...] - mean * scale
    member = one_hot(assign_ref[...], groups, cap_rows)
    spread_rows = spread(member, jnp.concatenate([scale, offset], axis=1))
    scale, offset = spread_rows[:, :emb_width], spread_rows[:, emb_width:]
    count = jnp.zeros((tiles, emb_width), f32)
    total = jnp.zeros((tiles, emb_width), f32)
    for p in range(positions):
        value = before_ref[p]
        live = value * scale + offset > 0
        count += jnp.where(live, 1.0, 0.0)
        total += jnp.where(live, value, 0.0)
    rows = pl.ds(pl.multiple_of(step * tiles, tiles), tiles)
    embedded_ref[rows] = ((total * scale + count * offset) * (1.0 / positions)).astype(bf16)
    count_ref[rows] = count
    total_ref[rows] = total

    @pl.when(step == pl.num_programs(0) - 1)
    def _():
        embedded = embedded_ref[...]
        tiles_all = embedded.shape[0]
        slides = counts_ref.shape[1]
        pre = matmul(embedded, w_fc_ref[...])
        hidden = jnp.maximum(pre, 0.0).astype(bf16)
        gate_pre = matmul(hidden, w_gate_ref[...])
        half = gate_pre.shape[1] // 2
        wave = jnp.tanh(gate_pre[:, :half])
        sig = jax.nn.sigmoid(gate_pre[:, half:])
        mix = wave * sig
        w_score = w_score_ref[...]
        score = jnp.sum(mix * w_score, axis=1, keepdims=True)

        lane = lax.broadcasted_iota(jnp.int32, (1, 128), 1)
        row = lax.broadcasted_iota(jnp.int32, (tiles_all, 128), 0)
        low = jnp.zeros((1, 128), jnp.int32)
        high = jnp.zeros((1, 128), jnp.int32)
        start = jnp.int32(0)
        for s in range(slides):
            end = start + counts_ref[0, s]
            low = jnp.where(lane == s, start, low)
            high = jnp.where(lane == s, end, high)
            start = end
        weight = jnp.where((row >= low) & (row < high), jnp.exp(score), 0.0)
        totals = jnp.sum(weight, axis=0, keepdims=True)
        attention = weight / jnp.where(lane < slides, totals, 1.0)
        att_high, att_middle, att_low = split3(attention)
        pooled = (
            contract_rows(att_high, hidden)
            + contract_rows(att_middle, hidden)
            + contract_rows(att_low, hidden)
        )[:8]
        slot = lax.broadcasted_iota(jnp.int32, (8, 1), 0)
        label = jnp.zeros((8, 1), jnp.int32)
        for s in range(slides):
            label = jnp.where(slot == s, labels_ref[0, s], label)
        classes = w_cls_ref.shape[0]
        w_cls = [w_cls_ref[c : c + 1, :] for c in range(classes)]
        logits = [jnp.sum(pooled * w, axis=1, keepdims=True) for w in w_cls]
        powers = [jnp.exp(v) for v in logits]
        power = sum(powers[1:], powers[0])
        target = sum(jnp.where(label == c, v, 0.0) for c, v in enumerate(logits))
        used = slot < slides
        loss = jnp.sum(jnp.where(used, jnp.log(power) - target, 0.0), axis=0, keepdims=True) * (
            1.0 / slides_all
        )
        grad_logits = [
            jnp.where(used, v / power - jnp.where(label == c, 1.0, 0.0), 0.0) * (1.0 / slides_all)
            for c, v in enumerate(powers)
        ]
        grad_cls = [jnp.sum(g * pooled, axis=0, keepdims=True) for g in grad_logits]
        grad_pooled = sum(g * w for g, w in zip(grad_logits, w_cls))
        grad_pooled = jnp.concatenate(
            [grad_pooled, jnp.zeros((128 - 8, grad_pooled.shape[1]), f32)], axis=0
        )
        gp_high, gp_middle, gp_low = split3(grad_pooled)
        grad_attention = (
            contract_cols(hidden, gp_high)
            + contract_cols(hidden, gp_middle)
            + contract_cols(hidden, gp_low)
        )
        product = attention * grad_attention
        centre = jnp.sum(product, axis=0, keepdims=True)
        grad_score = jnp.sum(product - attention * centre, axis=1, keepdims=True)
        grad_w_score = jnp.sum(grad_score * mix, axis=0, keepdims=True)
        grad_mix = grad_score * w_score
        gates_low = jnp.concatenate(
            [grad_mix * sig * (1.0 - wave * wave), grad_mix * mix * (1.0 - sig)], axis=1
        ).astype(bf16)
        grad_hidden = matmul(
            jnp.concatenate([att_high, att_high, att_middle], axis=1),
            jnp.concatenate([gp_high, gp_middle, gp_high], axis=0),
        )
        grad_hidden += contract_cols(gates_low, w_gate_ref[...])
        before_low = jnp.where(pre > 0, grad_hidden, 0.0).astype(bf16)
        core = core_ref[0, 0]
        rows_fc, rows_gate = emb_width // 2, pre.shape[1] // 2
        halves_fc = grad_ref.at[:, pl.ds(0, rows_fc)]
        halves_gate = grad_ref.at[:, pl.ds(rows_fc, rows_gate)]
        halves_fc[...] = contract_rows(embedded, before_low).reshape(2, rows_fc, -1)
        halves_gate[...] = contract_rows(hidden, gates_low).reshape(2, rows_gate, -1)
        low_ref[...] = grad_ref[1 - core].astype(bf16)
        grad_embedded = contract_cols(before_low, w_fc_ref[...]).astype(bf16)
        grad_low_ref[...] = grad_embedded
        copies = [
            pltpu.make_async_copy(low_ref, send_ref, copied.at[0]),
            pltpu.make_async_copy(grad_ref.at[core], keep_ref, copied.at[1]),
            pltpu.make_async_copy(grad_low_ref, grad_embedded_ref, copied.at[2]),
        ]
        for c in copies:
            c.start()
        each = grad_embedded.astype(f32) * (1.0 / positions)
        member_all = one_hot(assign_all_ref[...], groups, cap_rows).astype(bf16)
        shift_sums = group_sums(member_all, each * count_ref[...])
        total_sums = group_sums(member_all, each * total_ref[...])
        sums_ref[0, :, :emb_width] = shift_sums
        sums_ref[1, :, :emb_width] = (total_sums - mean * shift_sums) * inverse
        sums_ref[:, :, emb_width:] = jnp.zeros((2, groups, EXTRA), f32)
        for i in range(half // EXTRA):
            sums_ref[0, i : i + 1, emb_width:] = grad_w_score[:, i * EXTRA : (i + 1) * EXTRA]
        i = half // EXTRA
        sums_ref[0, i : i + 1, emb_width:] = jnp.where(lane == 0, loss, 0.0)
        grad_cls = jnp.concatenate(grad_cls, axis=1)
        for i in range(grad_cls.shape[1] // EXTRA):
            sums_ref[1, i : i + 1, emb_width:] = grad_cls[:, i * EXTRA : (i + 1) * EXTRA]
        for c in copies:
            c.wait()


def back_kernel(
    cap_rows,
    pixel_count,
    x_ref,
    before_ref,
    grad_embedded_ref,
    assign_ref,
    first_ref,
    second_ref,
    shift_sums_ref,
    gain_sums_ref,
    gain_ref,
    shift_ref,
    grad_ref,
    grad_gain_ref,
    grad_shift_ref,
):

    positions, tiles, emb_width = before_ref.shape
    groups = first_ref.shape[0]
    mean, inverse = moments(first_ref[...], second_ref[...], pixel_count)
    scale = inverse * gain_ref[...]
    offset = shift_ref[...] - mean * scale
    slope = scale * inverse * gain_sums_ref[:, :emb_width] * (1.0 / pixel_count)
    constant = scale * shift_sums_ref[:, :emb_width] * (1.0 / pixel_count) - mean * slope
    member = one_hot(assign_ref[...], groups, cap_rows)
    spread_rows = spread(member, jnp.concatenate([scale, offset, slope, constant], axis=1))
    scale, offset, slope, constant = (
        spread_rows[:, i * emb_width : (i + 1) * emb_width] for i in range(4)
    )
    direct = grad_embedded_ref[...].astype(f32) * scale * (1.0 / positions)
    grads = []
    for p in range(positions):
        value = before_ref[p]
        live = value * scale + offset > 0
        grads.append(
            (jnp.where(live, direct, 0.0) - constant - value * slope).astype(bf16)
        )

    @pl.when(pl.program_id(0) == 0)
    def _():
        grad_ref[...] = jnp.zeros_like(grad_ref)
        grad_gain_ref[...] = jnp.sum(gain_sums_ref[:, :emb_width], axis=0, keepdims=True)
        grad_shift_ref[...] = jnp.sum(shift_sums_ref[:, :emb_width], axis=0, keepdims=True)

    grad_ref[...] += contract_rows(
        x_ref[...].reshape(positions * tiles, x_ref.shape[2]), jnp.concatenate(grads, axis=0)
    )


def round_low(x):
    return lax.reduce_precision(x, 8, 7)


def swap(x, bit):
    count = lax.axis_size("enc")
    return lax.ppermute(x, "enc", [(i, i ^ (1 << bit)) for i in range(count)])


def bit_of(bit):
    return (lax.axis_index("enc") >> bit) & 1


def wait_for(x, other):
    corner = (other[:16, :128] * 0).astype(x.dtype)
    return x + jnp.pad(corner, ((0, x.shape[0] - 16), (0, x.shape[1] - 128)))


class SmallSum:
    def __init__(self, pair):
        self.core = bit_of(0) == 0
        self.x = jnp.where(self.core, pair[0], pair[1])
        self.x += swap(jnp.where(self.core, pair[1], pair[0]), 0)

    def hop(self, level):
        self.x += swap(self.x, level)

    def result(self):
        other = swap(self.x, 0)
        return jnp.where(self.core, self.x, other), jnp.where(self.core, other, self.x)


class LargeSum:
    def __init__(self, x):
        self.x = x

    def halve(self, level, other=None):
        x = self.x
        halves = x.reshape((2, x.shape[0] // 2) + x.shape[1:])
        bit = bit_of(level)
        keep = lax.dynamic_index_in_dim(halves, bit, 0, keepdims=False)
        send = lax.dynamic_index_in_dim(halves, 1 - bit, 0, keepdims=False).astype(bf16)
        if other is not None:
            send = wait_for(send, other)
        self.x = keep + swap(send, level).astype(f32)

    def exchange(self, level):
        x = round_low(self.x)
        self.x = (x + swap(x.astype(bf16), level).astype(f32)).astype(bf16)

    def pair(self, level):
        other = swap(self.x, level)
        first = bit_of(level) == 0
        return jnp.where(first, self.x, other), jnp.where(first, other, self.x)

    def double(self, level):
        self.x = jnp.concatenate(self.pair(level), axis=0)


def local(
    tiles, tile_counts, assign, labels, w_conv, bn_gain, bn_shift, w_fc, w_gate, w_score, w_cls
):
    devices = lax.axis_size("enc")
    own_rows, positions, input_width = tiles.shape
    emb_width = w_conv.shape[1]
    hid_width = w_fc.shape[1]
    slot_rows = assign.shape[1]
    cap_rows = slot_rows // devices
    group_tiles = (
        devices // 4 * (4 + (cap_rows - 2) // 3 + 2 * (cap_rows - 2) // 3 + (cap_rows - 2))
        + devices // 2
    )
    pixel_count = float(group_tiles * positions)
    slides_all = float(devices * tile_counts.shape[1])
    gain, shift = bn_gain.reshape(1, emb_width), bn_shift.reshape(1, emb_width)
    steps = own_rows // CHUNK

    def whole(*shape):
        return pl.BlockSpec(shape, lambda i: (0,) * len(shape))

    smem = pl.BlockSpec(memory_space=pltpu.SMEM)
    x_block = pl.BlockSpec((positions, CHUNK, input_width), lambda i: (0, i, 0))
    before_block = pl.BlockSpec((positions, CHUNK, emb_width), lambda i: (0, i, 0))
    assign_block = pl.BlockSpec((1, CHUNK), lambda i: (0, i))

    def settings(mebibytes, microseconds):
        return dict(
            compiler_params=pltpu.CompilerParams(
                dimension_semantics=("arbitrary",), vmem_limit_bytes=mebibytes << 20
            ),
            cost_estimate=pl.CostEstimate(
                flops=int(microseconds * 1.1e9), bytes_accessed=8 << 20, transcendentals=0
            ),
        )

    group_block = whole(devices, emb_width)
    back_block = whole(devices, emb_width + EXTRA)
    row_block = whole(1, emb_width)

    work = jnp.transpose(tiles, (1, 0, 2))
    before, sums = pl.pallas_call(
        functools.partial(conv_kernel, cap_rows),
        grid=(steps,),
        in_specs=[x_block, assign_block, whole(input_width, emb_width)],
        out_specs=[before_block, whole(2, devices, emb_width)],
        out_shape=[
            pltpu.HBM((positions, own_rows, emb_width), f32),
            jax.ShapeDtypeStruct((2, devices, emb_width), f32),
        ],
        scratch_shapes=[pltpu.VMEM((devices, input_width), f32)],
        **settings(24, 6),
        name="conv_sums",
    )(work, assign, w_conv)
    before = pltpu.with_memory_space_constraint(before, pltpu.HBM)
    levels = devices.bit_length() - 1
    total = SmallSum(sums)
    for level in range(1, levels):
        total.hop(level)
    first, second = total.result()

    any_block = pl.BlockSpec(memory_space=pl.ANY)
    half_rows = (emb_width + hid_width) // 2
    send, keep, grad_embedded, sums = pl.pallas_call(
        functools.partial(head_kernel, cap_rows, pixel_count, slides_all),
        grid=(steps,),
        in_specs=[
            smem,
            smem,
            smem,
            before_block,
            assign_block,
            whole(1, own_rows),
            group_block,
            group_block,
            row_block,
            row_block,
            whole(*w_fc.shape),
            whole(*w_gate.shape),
            whole(1, w_score.shape[0]),
            whole(*w_cls.shape[::-1]),
        ],
        out_specs=[any_block] * 3 + [whole(2, devices, emb_width + EXTRA)],
        out_shape=[
            jax.ShapeDtypeStruct((half_rows, hid_width), bf16),
            pltpu.HBM((half_rows, hid_width), f32),
            pltpu.HBM((own_rows, emb_width), bf16),
            jax.ShapeDtypeStruct((2, devices, emb_width + EXTRA), f32),
        ],
        scratch_shapes=[
            pltpu.VMEM((own_rows, emb_width), bf16),
            pltpu.VMEM((own_rows, emb_width), f32),
            pltpu.VMEM((own_rows, emb_width), f32),
            pltpu.VMEM((2, half_rows, hid_width), f32),
            pltpu.VMEM((half_rows, hid_width), bf16),
            pltpu.VMEM((own_rows, emb_width), bf16),
            pltpu.SemaphoreType.DMA((3,)),
        ],
        name="norm_head",
        **settings(36, 12),
    )(
        tile_counts,
        labels,
        bit_of(0).astype(jnp.int32).reshape(1, 1),
        before,
        assign,
        assign,
        first,
        second,
        gain,
        shift,
        w_fc,
        w_gate,
        w_score.reshape(1, -1),
        w_cls.T,
    )
    grad_embedded = pltpu.with_memory_space_constraint(grad_embedded, pltpu.HBM)
    total = SmallSum(sums)
    rows_fc = emb_width // 2
    head = LargeSum(keep + swap(send, 0).astype(f32))
    total.hop(1)
    total.x = wait_for(total.x, head.x)
    head.halve(1)
    for level in range(2, levels):
        total.hop(level)
    total.x = wait_for(total.x, head.x)
    shift_sums, gain_sums = total.result()

    grad_conv, grad_gain, grad_shift = pl.pallas_call(
        functools.partial(back_kernel, cap_rows, pixel_count),
        grid=(steps,),
        in_specs=[
            x_block,
            before_block,
            pl.BlockSpec((CHUNK, emb_width), lambda i: (i, 0)),
            assign_block,
            group_block,
            group_block,
            back_block,
            back_block,
            row_block,
            row_block,
        ],
        out_specs=[whole(input_width, emb_width), row_block, row_block],
        out_shape=[
            jax.ShapeDtypeStruct((input_width, emb_width), f32),
            jax.ShapeDtypeStruct((1, emb_width), f32),
            jax.ShapeDtypeStruct((1, emb_width), f32),
        ],
        name="norm_back",
        **settings(24, 9),
    )(work, before, grad_embedded, assign, first, second, shift_sums, gain_sums, gain, shift)

    conv = LargeSum(grad_conv)
    for level in range(2, levels - 1):
        head.halve(level)
    conv.halve(0, head.x)
    conv.halve(1)
    head.exchange(levels - 1)
    head.x = wait_for(head.x, conv.x)
    for level in range(2, levels - 1):
        conv.halve(level)
    for level in range(levels - 2, 1, -1):
        head.double(level)
    head.x = wait_for(head.x, conv.x)
    conv.exchange(levels - 1)
    conv.x = wait_for(conv.x, head.x)
    for level in range(levels - 2, 1, -1):
        conv.double(level)
    head.double(1)
    conv.x = wait_for(conv.x, head.x)
    conv.double(1)
    low, high = head.pair(0)
    grad_fc = jnp.concatenate([low[:rows_fc], high[:rows_fc]], axis=0).astype(f32)
    grad_gate = jnp.concatenate([low[rows_fc:], high[rows_fc:]], axis=0).astype(f32)
    conv.x = wait_for(conv.x, grad_fc)
    conv.double(0)
    grad_conv = conv.x.astype(f32)
    scores = w_score.shape[0] // EXTRA
    classes = math.prod(w_cls.shape) // EXTRA
    return (
        shift_sums[scores, emb_width : emb_width + 1],
        grad_conv,
        grad_gain.reshape(emb_width),
        grad_shift.reshape(emb_width),
        grad_fc,
        grad_gate,
        shift_sums[:scores, emb_width:].reshape(-1),
        gain_sums[:classes, emb_width:].reshape(w_cls.shape[::-1]).T,
    )


def solution(mesh):
    per_device = P(("groups", "enc"), None)
    placed = (P(("groups", "enc"), None, None), per_device, per_device, per_device) + (P(),) * 7
    rows_out = P("groups", None)
    return jax.shard_map(
        local,
        mesh=mesh,
        in_specs=placed,
        out_specs=(
            P("groups"),
            rows_out,
            P("groups"),
            P("groups"),
            rows_out,
            rows_out,
            P("groups"),
            rows_out,
        ),
        check_vma=False,
    )
```

time: 350 us -> 121 us (0.35)
  blocking collectives: 120 us -> 0 us
  waiting for transfers between devices: 102 us -> 47 us
  local copies, waits for them, and re-layouts: 61.6 us -> 7.59 us
  Pallas kernels: 0 us -> 28.2 us
  matrix products: 24.7 us -> 0 us
  starting transfers between devices: 12.4 us -> 28.3 us
  between operations: 15 us -> 1.19 us
  other arithmetic: 12.4 us -> 8.59 us
    psum x1 -> x0, blocking collectives: 65.5 us -> none  [local(): lax.psum((loss_sum, grad_fc, grad_gate, grad_score, grad_cls, grad_conv,...]
    psum x1 -> x0, waiting for transfers between devices: 62.3 us -> none  [local(): lax.psum((loss_sum, grad_fc, grad_gate, grad_score, grad_cls, grad_conv,...]
    all_to_all x1 -> x0, blocking collectives: 54.9 us -> none  [local(): lax.all_to_all(outgoing, 'enc', split_axis=0, concat_axis=0, tiled=True)]
    ppermute x0 -> x24, waiting for transfers between devices: none -> 47 us  [swap(): return lax.ppermute(x, 'enc', [(i, i ^ 1 << bit) for i in range(count)])]
    scatter x2 -> x0, local copies, waits for them, and re-layouts: 44 us -> none  [the longest x1 40.4 us: local(): outgoing = jnp.zeros((SLOTS_DEV, positions, input_width), jnp.bfloat16).a...]
    all_to_all x2 -> x0, waiting for transfers between devices: 39.4 us -> none  [the longest x1 22.7 us: local(): lax.all_to_all(encoded, 'enc', split_axis=0, concat_axis=0, tiled=True)]
    ppermute x0 -> x24, starting transfers between devices: none -> 28.3 us  [swap(): return lax.ppermute(x, 'enc', [(i, i ^ 1 << bit) for i in range(count)])]
    pallas_call x0 -> x3, Pallas kernels: none -> 28.2 us  [the longest x1 12.8 us: local(): pl.pallas_call(functools.partial(head_kernel, cap_rows, pixel_count, slid...]
  transfers between devices with their start and end apart: 3 -> 24, of which waited for: 3 -> 17; matrix products, arithmetic and copies ran while one was open for 2% -> 5% of each run, Pallas kernels for 0% -> 8%
where the time goes in v2:
time: 121 us
  waiting for transfers between devices  47 us (39%)
  starting transfers between devices  28.3 us (23%)
  Pallas kernels  28.2 us (23%)
  other arithmetic  8.59 us (7%)
  local copies, waits for them, and re-layouts  7.59 us (6%)
    ppermute x24, waiting for transfers between devices, swap(): return lax.ppermute(x, 'enc', [(i, i ^ 1 << bit) for i in range(count)])  47 us
    ppermute x24, starting transfers between devices, swap(): return lax.ppermute(x, 'enc', [(i, i ^ 1 << bit) for i in range(count)])  28.3 us
    pallas_call x1, Pallas kernels, local(): pl.pallas_call(functools.partial(head_kernel, cap_rows, pixel_count, slid...  12.8 us
    pallas_call x1, Pallas kernels, local(): pl.pallas_call(functools.partial(back_kernel, cap_rows, pixel_count), gri...  9.38 us
    pallas_call x1, Pallas kernels, local(): pl.pallas_call(functools.partial(conv_kernel, cap_rows), grid=(steps,), i...  6.01 us
    unnamed x27, local copies, waits for them, and re-layouts  5.66 us
    add x3, other arithmetic, halve(): self.x = keep + swap(send, level).astype(f32)  2.68 us
  transfers between devices with their start and end apart: 24, of which 17 were waited for; matrix products, arithmetic and copies ran while one was open for 5% of the time, Pallas kernels for 8%

profile of v2, /device:TPU:0, one launch (start us, length us, event | category | flops | bytes accessed | tf_op | source)
XLA Modules:
  0.0 120.9 jit_solution(15355659610473891323)
XLA Ops:
  0.7 2.1 %copy.21 = bf16[512,4,512]{2,0,1:T(8,128)(2,1)S(1)} copy(bf16[512,4,512]{2,1,0:T(4,128)(2,1)} %param.11) | data formatting | bytes 4194304 | tf_op args[0]
  2.9 6.0 %conv_sums.1 = (f32[4,512,1024]{2,1,0:T(8,128)}, f32[2,16,1024]{2,1,0:T(8,128)S(1)}) custom-call(bf16[4,512,512]{2,1,0:T(8,128)(2,1)S(1)} %bitcast.51, s32[1,512]{1,0:T(1,128)S(1)} %copy-done.7, bf16[512,1024]{1,0:T(8,128)(2,1)S(1)} %copy-done.1), custom_call_target="tpu_custom_call" | custom-call | flops 6600000000 | bytes 8388608 | tf_op jit(solution)/shard_map/conv_sums/pallas_call | solution.py:402
  8.9 0.5 collective-permute-start
  9.4 0.9 collective-permute-done
  10.3 2.9 %collective-permute-start.1 = (f32[16,1024]{1,0:T(8,128)S(1)}, f32[16,1024]{1,0:T(8,128)S(1)}, u32[]{:S(2)}, u32[]{:S(2)}) collective-permute-start(f32[16,1024]{1,0:T(8,128)S(1)} %bitcast_add_fusion.6), channel_id=1, source_target_pairs={{0,2},{1,3},{2,0},{3,1},{4,6},{5,7},{6,4},{7,5},{8,10},{9,11},{10,... | collective-permute-start | bytes 196616 | tf_op jit(solution)/shard_map/ppermute | solution.py:308
  13.3 2.4 %collective-permute-done.1 = f32[16,1024]{1,0:T(8,128)S(1)} collective-permute-done((f32[16,1024]{1,0:T(8,128)S(1)}, f32[16,1024]{1,0:T(8,128)S(1)}, u32[]{:S(2)}, u32[]{:S(2)}) %collective-permute-start.1) | collective-permute-done | bytes 65568 | tf_op jit(solution)/shard_map/ppermute | solution.py:308
  15.7 2.0 %collective-permute-start.2 = (f32[16,1024]{1,0:T(8,128)S(1)}, f32[16,1024]{1,0:T(8,128)S(1)}, u32[]{:S(2)}, u32[]{:S(2)}) collective-permute-start(f32[16,1024]{1,0:T(8,128)S(1)} %add.119), channel_id=1, source_target_pairs={{0,4},{1,5},{2,6},{3,7},{4,0},{5,1},{6,2},{7,3},{8,12},{9,13},{10,... | collective-permute-start | bytes 196616 | tf_op jit(solution)/shard_map/ppermute | solution.py:308
  17.7 2.4 %collective-permute-done.2 = f32[16,1024]{1,0:T(8,128)S(1)} collective-permute-done((f32[16,1024]{1,0:T(8,128)S(1)}, f32[16,1024]{1,0:T(8,128)S(1)}, u32[]{:S(2)}, u32[]{:S(2)}) %collective-permute-start.2) | collective-permute-done | bytes 65568 | tf_op jit(solution)/shard_map/ppermute | solution.py:308
  20.0 3.0 %collective-permute-start.3 = (f32[16,1024]{1,0:T(8,128)S(1)}, f32[16,1024]{1,0:T(8,128)S(1)}, u32[]{:S(2)}, u32[]{:S(2)}) collective-permute-start(f32[16,1024]{1,0:T(8,128)S(1)} %add.120), channel_id=1, source_target_pairs={{0,8},{1,9},{2,10},{3,11},{4,12},{5,13},{6,14},{7,15},{8,0},{9,1},... | collective-permute-start | bytes 196616 | tf_op jit(solution)/shard_map/ppermute | solution.py:308
  23.0 2.2 %collective-permute-done.3 = f32[16,1024]{1,0:T(8,128)S(1)} collective-permute-done((f32[16,1024]{1,0:T(8,128)S(1)}, f32[16,1024]{1,0:T(8,128)S(1)}, u32[]{:S(2)}, u32[]{:S(2)}) %collective-permute-start.3) | collective-permute-done | bytes 65568 | tf_op jit(solution)/shard_map/ppermute | solution.py:308
  25.3 1.2 %collective-permute-done.4 = f32[16,1024]{1,0:T(8,128)S(1)} collective-permute-done((f32[16,1024]{1,0:T(8,128)S(1)}, f32[16,1024]{1,0:T(8,128)S(1)}, u32[]{:S(2)}, u32[]{:S(2)}) %collective-permute-start.4) | collective-permute-done | bytes 65568 | tf_op jit(solution)/shard_map/ppermute | solution.py:308
  26.7 12.8 %norm_head.1 = (bf16[768,512]{1,0:T(8,128)(2,1)S(1)}, f32[768,512]{1,0:T(8,128)}, bf16[512,1024]{1,0:T(8,128)(2,1)}, f32[2,16,1152]{2,1,0:T(8,128)S(1)}) custom-call(s32[1,4]{1,0:T(1,128)S(1)} %copy-done.9, s32[1,4]{1,0:T(1,128)S(1)} %copy-done.10, s32[1,1]{1,0:T(1,128)} %bitcast.core_ref, f32[4,512,1024]{2,1,0:T(8,128)} %get-tuple-element.17.before_ref, ...), custom_call_target="tpu_custom_call" | custom-call | flops 13200000000 | bytes 8388608 | tf_op jit(solution)/shard_map/norm_head/pallas_call | solution.py:424
  39.7 0.4 collective-permute-start.5
  40.1 1.8 %collective-permute-done.5 = f32[16,1152]{1,0:T(8,128)S(1)} collective-permute-done((f32[16,1152]{1,0:T(8,128)S(1)}, f32[16,1152]{1,0:T(8,128)S(1)}, u32[]{:S(2)}, u32[]{:S(2)}) %collective-permute-start.5) | collective-permute-done | bytes 73760 | tf_op jit(solution)/shard_map/ppermute | solution.py:308
  42.0 1.9 %collective-permute-start.6 = (f32[16,1152]{1,0:T(8,128)S(1)}, f32[16,1152]{1,0:T(8,128)S(1)}, u32[]{:S(2)}, u32[]{:S(2)}) collective-permute-start(f32[16,1152]{1,0:T(8,128)S(1)} %bitcast_add_fusion.5), channel_id=1, source_target_pairs={{0,2},{1,3},{2,0},{3,1},{4,6},{5,7},{6,4},{7,5},{8,10},{9,11},{10,... | collective-permute-start | bytes 221192 | tf_op jit(solution)/shard_map/ppermute | solution.py:308
  43.9 1.8 %convert_add_fusion = f32[768,512]{1,0:T(8,128)S(1)} fusion(f32[768,512]{1,0:T(8,128)} %get-tuple-element.20, bf16[768,512]{1,0:T(8,128)(2,1)} %collective-permute-done.7), kind=kLoop, calls=%fused_computation.1 | loop fusion | flops 786432 | bytes 3932160 | tf_op jit(solution)/shard_map/add | solution.py:480
  45.8 1.1 copy-done.11
  47.2 2.0 %collective-permute-start.8 = (f32[16,1152]{1,0:T(8,128)S(1)}, f32[16,1152]{1,0:T(8,128)S(1)}, u32[]{:S(2)}, u32[]{:S(2)}) collective-permute-start(f32[16,1152]{1,0:T(8,128)S(1)} %pad_add_fusion.1), channel_id=1, source_target_pairs={{0,4},{1,5},{2,6},{3,7},{4,0},{5,1},{6,2},{7,3},{8,12},{9,13},{10,... | collective-permute-start | bytes 221192 | tf_op jit(solution)/shard_map/ppermute | solution.py:308
  49.2 2.4 %collective-permute-done.8 = f32[16,1152]{1,0:T(8,128)S(1)} collective-permute-done((f32[16,1152]{1,0:T(8,128)S(1)}, f32[16,1152]{1,0:T(8,128)S(1)}, u32[]{:S(2)}, u32[]{:S(2)}) %collective-permute-start.8) | collective-permute-done | bytes 73760 | tf_op jit(solution)/shard_map/ppermute | solution.py:308
  51.6 3.1 %collective-permute-start.9 = (f32[16,1152]{1,0:T(8,128)S(1)}, f32[16,1152]{1,0:T(8,128)S(1)}, u32[]{:S(2)}, u32[]{:S(2)}) collective-permute-start(f32[16,1152]{1,0:T(8,128)S(1)} %add.126), channel_id=1, source_target_pairs={{0,8},{1,9},{2,10},{3,11},{4,12},{5,13},{6,14},{7,15},{8,0},{9,1},... | collective-permute-start | bytes 221192 | tf_op jit(solution)/shard_map/ppermute | solution.py:308
  54.8 3.1 %collective-permute-done.10 = bf16[384,512]{1,0:T(8,128)(2,1)S(1)} collective-permute-done((bf16[384,512]{1,0:T(8,128)(2,1)S(1)}, bf16[384,512]{1,0:T(8,128)(2,1)S(1)}, u32[]{:S(2)}, u32[]{:S(2)}) %collective-permute-start.10) | collective-permute-done | bytes 393248 | tf_op jit(solution)/shard_map/ppermute | solution.py:308
  57.9 1.2 %bitcast_add_fusion.1 = f32[384,512]{1,0:T(8,128)S(1)} fusion(bf16[384,512]{1,0:T(8,128)(2,1)S(1)} %collective-permute-done.10, f32[2,384,512]{2,1,0:T(8,128)} %bitcast.62, s32[]{:T(128)S(6)} %select_n.169), kind=kLoop, calls=%fused_computation.7 | loop fusion | flops 393216 | bytes 1966084 | tf_op jit(solution)/shard_map/add | solution.py:346
  59.3 1.6 %collective-permute-start.12 = (bf16[192,512]{1,0:T(8,128)(2,1)S(1)}, bf16[192,512]{1,0:T(8,128)(2,1)S(1)}, u32[]{:S(2)}, u32[]{:S(2)}) collective-permute-start(bf16[192,512]{1,0:T(8,128)(2,1)S(1)} %fusion.4), channel_id=1, source_target_pairs={{0,4},{1,5},{2,6},{3,7},{4,0},{5,1},{6,2},{7,3},{8,12},{9,13},{10,... | collective-permute-start | bytes 589832 | tf_op jit(solution)/shard_map/ppermute | solution.py:308
  61.0 9.4 %norm_back.1 = (f32[512,1024]{1,0:T(8,128)S(1)}, f32[1,1024]{1,0:T(1,128)}, f32[1,1024]{1,0:T(1,128)}) custom-call(bf16[4,512,512]{2,1,0:T(8,128)(2,1)S(1)} %bitcast.52, f32[4,512,1024]{2,1,0:T(8,128)} %get-tuple-element.17.before_ref, bf16[512,1024]{1,0:T(8,128)(2,1)} %get-tuple-element.22.grad_embedded_ref, s32[1,512]{1,0:T(1,128)S(1)} %copy-done.7, ...), custom_call_target="tpu_custom_call" | custom-call | flops 9900000256 | bytes 8388608 | tf_op jit(solution)/shard_map/norm_back/pallas_call | solution.py:489
  70.5 1.2 %copy-done = f32[512,1024]{1,0:T(8,128)} copy-done((f32[512,1024]{1,0:T(8,128)}, f32[512,1024]{1,0:T(8,128)S(1)}, u32[]{:S(2)}) %copy-start) | copy-done | bytes 2097176
  72.0 1.7 %collective-permute-done.13 = bf16[256,1024]{1,0:T(8,128)(2,1)S(1)} collective-permute-done((bf16[256,1024]{1,0:T(8,128)(2,1)S(1)}, bf16[256,1024]{1,0:T(8,128)(2,1)S(1)}, u32[]{:S(2)}, u32[]{:S(2)}) %collective-permute-start.13) | collective-permute-done | bytes 524320 | tf_op jit(solution)/shard_map/ppermute | solution.py:308
  73.7 1.4 %bitcast_add_fusion = f32[256,1024]{1,0:T(8,128)S(1)} fusion(bf16[256,1024]{1,0:T(8,128)(2,1)S(1)} %collective-permute-done.13, f32[2,256,1024]{2,1,0:T(8,128)} %bitcast.54, s32[]{:T(128)S(6)} %select_n.176), kind=kLoop, calls=%fused_computation.4 | loop fusion | flops 524288 | bytes 2621444 | tf_op jit(solution)/shard_map/add | solution.py:346
  75.2 0.6 collective-permute-start.14
  75.7 3.2 %collective-permute-start.17 = (bf16[192,512]{1,0:T(8,128)(2,1)S(1)}, bf16[192,512]{1,0:T(8,128)(2,1)S(1)}, u32[]{:S(2)}, u32[]{:S(2)}) collective-permute-start(bf16[192,512]{1,0:T(8,128)(2,1)S(1)} %get-tuple-element.26), channel_id=1, source_target_pairs={{0,8},{1,9},{2,10},{3,11},{4,12},{5,13},{6,14},{7,15},{8,0},{9,1},... | collective-permute-start | bytes 589832 | tf_op jit(solution)/shard_map/ppermute | solution.py:308
  78.9 4.7 %collective-permute-done.14 = bf16[128,1024]{1,0:T(8,128)(2,1)S(1)} collective-permute-done((bf16[128,1024]{1,0:T(8,128)(2,1)S(1)}, bf16[128,1024]{1,0:T(8,128)(2,1)S(1)}, u32[]{:S(2)}, u32[]{:S(2)}) %collective-permute-start.14) | collective-permute-done | bytes 262176 | tf_op jit(solution)/shard_map/ppermute | solution.py:308
  83.7 1.2 collective-permute-start.15
  84.9 3.3 %collective-permute-done.17 = bf16[192,512]{1,0:T(8,128)(2,1)S(1)} collective-permute-done((bf16[192,512]{1,0:T(8,128)(2,1)S(1)}, bf16[192,512]{1,0:T(8,128)(2,1)S(1)}, u32[]{:S(2)}, u32[]{:S(2)}) %collective-permute-start.17) | collective-permute-done | bytes 196640 | tf_op jit(solution)/shard_map/ppermute | solution.py:308
  88.3 0.3 collective-permute-start.18
  88.6 2.4 %collective-permute-done.15 = bf16[64,1024]{1,0:T(8,128)(2,1)S(1)} collective-permute-done((bf16[64,1024]{1,0:T(8,128)(2,1)S(1)}, bf16[64,1024]{1,0:T(8,128)(2,1)S(1)}, u32[]{:S(2)}, u32[]{:S(2)}) %collective-permute-start.15) | collective-permute-done | bytes 131104 | tf_op jit(solution)/shard_map/ppermute | solution.py:308
  91.0 1.3 %collective-permute-start.16 = (bf16[64,1024]{1,0:T(8,128)(2,1)S(1)}, bf16[64,1024]{1,0:T(8,128)(2,1)S(1)}, u32[]{:S(2)}, u32[]{:S(2)}) collective-permute-start(bf16[64,1024]{1,0:T(8,128)(2,1)S(1)} %get-tuple-element.28), channel_id=1, source_target_pairs={{0,8},{1,9},{2,10},{3,11},{4,12},{5,13},{6,14},{7,15},{8,0},{9,1},... | collective-permute-start | bytes 393224 | tf_op jit(solution)/shard_map/ppermute | solution.py:308
  92.4 4.0 %collective-permute-done.18 = bf16[192,512]{1,0:T(8,128)(2,1)S(1)} collective-permute-done((bf16[192,512]{1,0:T(8,128)(2,1)S(1)}, bf16[192,512]{1,0:T(8,128)(2,1)S(1)}, u32[]{:S(2)}, u32[]{:S(2)}) %collective-permute-start.18) | collective-permute-done | bytes 196640 | tf_op jit(solution)/shard_map/ppermute | solution.py:308
  96.4 1.6 %collective-permute-start.20 = (bf16[384,512]{1,0:T(8,128)(2,1)S(1)}, bf16[384,512]{1,0:T(8,128)(2,1)S(1)}, u32[]{:S(2)}, u32[]{:S(2)}) collective-permute-start(bf16[384,512]{1,0:T(8,128)(2,1)S(1)} %maximum_add_fusion.1), channel_id=1, source_target_pairs={{0,2},{1,3},{2,0},{3,1},{4,6},{5,7},{6,4},{7,5},{8,10},{9,11},{10,... | collective-permute-start | bytes 1179656 | tf_op jit(solution)/shard_map/ppermute | solution.py:308
  98.0 2.1 %collective-permute-done.16 = bf16[64,1024]{1,0:T(8,128)(2,1)S(1)} collective-permute-done((bf16[64,1024]{1,0:T(8,128)(2,1)S(1)}, bf16[64,1024]{1,0:T(8,128)(2,1)S(1)}, u32[]{:S(2)}, u32[]{:S(2)}) %collective-permute-start.16) | collective-permute-done | bytes 131104 | tf_op jit(solution)/shard_map/ppermute | solution.py:308
  100.3 4.9 %collective-permute-done.19 = bf16[64,1024]{1,0:T(8,128)(2,1)S(1)} collective-permute-done((bf16[64,1024]{1,0:T(8,128)(2,1)S(1)}, bf16[64,1024]{1,0:T(8,128)(2,1)S(1)}, u32[]{:S(2)}, u32[]{:S(2)}) %collective-permute-start.19) | collective-permute-done | bytes 131104 | tf_op jit(solution)/shard_map/ppermute | solution.py:308
  105.6 1.6 %collective-permute-start.21 = (bf16[128,1024]{1,0:T(8,128)(2,1)S(1)}, bf16[128,1024]{1,0:T(8,128)(2,1)S(1)}, u32[]{:S(2)}, u32[]{:S(2)}) collective-permute-start(bf16[128,1024]{1,0:T(8,128)(2,1)S(1)} %maximum_add_fusion.2), channel_id=1, source_target_pairs={{0,2},{1,3},{2,0},{3,1},{4,6},{5,7},{6,4},{7,5},{8,10},{9,11},{10,... | collective-permute-start | bytes 786440 | tf_op jit(solution)/shard_map/ppermute | solution.py:308
  107.2 7.2 %collective-permute-done.21 = bf16[128,1024]{1,0:T(8,128)(2,1)S(1)} collective-permute-done((bf16[128,1024]{1,0:T(8,128)(2,1)S(1)}, bf16[128,1024]{1,0:T(8,128)(2,1)S(1)}, u32[]{:S(2)}, u32[]{:S(2)}) %collective-permute-start.21) | collective-permute-done | bytes 262176 | tf_op jit(solution)/shard_map/ppermute | solution.py:308
  114.4 0.3 broadcast_select_fusion.1
  115.3 1.2 copy-done.12
  116.4 0.5 slice.82
  116.9 0.6 reshape.80
  117.5 0.6 slice_bitcast_fusion
  118.1 1.1 maximum_convert_fusion.2
  119.3 1.6 %maximum_convert_fusion.1 = f32[512,1024]{1,0:T(8,128)} fusion(bf16[256,1024]{1,0:T(8,128)(2,1)S(1)} %get-tuple-element.33, bf16[256,1024]{1,0:T(8,128)(2,1)S(1)} %get-tuple-element.32), kind=kLoop, calls=%fused_computation.3 | loop fusion | flops 2097152 | bytes 3145728 | tf_op jit(solution)/shard_map/convert_element_type | solution.py:538
  (84 shorter events, 2.7 us)
Async XLA Ops:
  0.6 2.1 %copy-start.1 = (bf16[512,1024]{1,0:T(8,128)(2,1)S(1)}, bf16[512,1024]{1,0:T(8,128)(2,1)}, u32[]{:S(2)}) copy-start(bf16[512,1024]{1,0:T(8,128)(2,1)} %w_ref.1) | copy-start | bytes 3145732
  0.7 2.1 %copy-start.7 = (s32[1,512]{1,0:T(1,128)S(1)}, s32[1,512]{1,0:T(1,128)}, u32[]{:S(2)}) copy-start(s32[1,512]{1,0:T(1,128)} %assign_ref.5) | copy-start | bytes 6148
  2.8 23.8 %copy-start.2 = (bf16[1024,512]{1,0:T(8,128)(2,1)S(1)}, bf16[1024,512]{1,0:T(8,128)(2,1)}, u32[]{:S(2)}) copy-start(bf16[1024,512]{1,0:T(8,128)(2,1)} %w_fc_ref.1) | copy-start | bytes 3145732
  2.8 23.8 %copy-start.3 = (bf16[512,512]{1,0:T(8,128)(2,1)S(1)}, bf16[512,512]{1,0:T(8,128)(2,1)}, u32[]{:S(2)}) copy-start(bf16[512,512]{1,0:T(8,128)(2,1)} %w_gate_ref.1) | copy-start | bytes 1572868
  2.8 23.8 %copy-start.4 = (f32[512,2]{0,1:T(2,128)S(1)}, f32[512,2]{0,1:T(2,128)}, u32[]{:S(2)}) copy-start(f32[512,2]{0,1:T(2,128)} %param.21) | copy-start | bytes 12292
  2.8 23.8 %copy-start.5 = (f32[1024]{0:T(1024)S(1)}, f32[1024]{0:T(1024)}, u32[]{:S(2)}) copy-start(f32[1024]{0:T(1024)} %param.16) | copy-start | bytes 12292
  2.8 23.8 %copy-start.6 = (f32[1024]{0:T(1024)S(1)}, f32[1024]{0:T(1024)}, u32[]{:S(2)}) copy-start(f32[1024]{0:T(1024)} %param.17) | copy-start | bytes 12292
  2.8 23.8 %copy-start.8 = (f32[256]{0:T(256)S(1)}, f32[256]{0:T(256)}, u32[]{:S(2)}) copy-start(f32[256]{0:T(256)} %param.20) | copy-start | bytes 3076
  2.8 23.8 %copy-start.9 = (s32[1,4]{1,0:T(1,128)S(1)}, s32[1,4]{1,0:T(1,128)}, u32[]{:S(2)}) copy-start(s32[1,4]{1,0:T(1,128)} %counts_ref.1) | copy-start | bytes 52
  2.9 23.8 %copy-start.10 = (s32[1,4]{1,0:T(1,128)S(1)}, s32[1,4]{1,0:T(1,128)}, u32[]{:S(2)}) copy-start(s32[1,4]{1,0:T(1,128)} %labels_ref.1) | copy-start | bytes 52
  8.9 1.4 %collective-permute-start = (f32[16,1024]{1,0:T(8,128)S(1)}, f32[16,1024]{1,0:T(8,128)S(1)}, u32[]{:S(2)}, u32[]{:S(2)}) collective-permute-start(f32[16,1024]{1,0:T(8,128)S(1)} %select_bitcast_fusion.1), channel_id=1, source_target_pairs={{0,1},{1,0},{2,3},{3,2},{4,5},{5,4},{6,7},{7,6},{8,9},{9,8},{10,11... | collective-permute-start | bytes 196616 | tf_op jit(solution)/shard_map/ppermute | solution.py:308
  10.3 5.4 %collective-permute-start.1 = (f32[16,1024]{1,0:T(8,128)S(1)}, f32[16,1024]{1,0:T(8,128)S(1)}, u32[]{:S(2)}, u32[]{:S(2)}) collective-permute-start(f32[16,1024]{1,0:T(8,128)S(1)} %bitcast_add_fusion.6), channel_id=1, source_target_pairs={{0,2},{1,3},{2,0},{3,1},{4,6},{5,7},{6,4},{7,5},{8,10},{9,11},{10,... | collective-permute-start | bytes 196616 | tf_op jit(solution)/shard_map/ppermute | solution.py:308
  15.7 4.3 %collective-permute-start.2 = (f32[16,1024]{1,0:T(8,128)S(1)}, f32[16,1024]{1,0:T(8,128)S(1)}, u32[]{:S(2)}, u32[]{:S(2)}) collective-permute-start(f32[16,1024]{1,0:T(8,128)S(1)} %add.119), channel_id=1, source_target_pairs={{0,4},{1,5},{2,6},{3,7},{4,0},{5,1},{6,2},{7,3},{8,12},{9,13},{10,... | collective-permute-start | bytes 196616 | tf_op jit(solution)/shard_map/ppermute | solution.py:308
  20.0 5.2 %collective-permute-start.3 = (f32[16,1024]{1,0:T(8,128)S(1)}, f32[16,1024]{1,0:T(8,128)S(1)}, u32[]{:S(2)}, u32[]{:S(2)}) collective-permute-start(f32[16,1024]{1,0:T(8,128)S(1)} %add.120), channel_id=1, source_target_pairs={{0,8},{1,9},{2,10},{3,11},{4,12},{5,13},{6,14},{7,15},{8,0},{9,1},... | collective-permute-start | bytes 196616 | tf_op jit(solution)/shard_map/ppermute | solution.py:308
  25.3 1.3 %collective-permute-start.4 = (f32[16,1024]{1,0:T(8,128)S(1)}, f32[16,1024]{1,0:T(8,128)S(1)}, u32[]{:S(2)}, u32[]{:S(2)}) collective-permute-start(f32[16,1024]{1,0:T(8,128)S(1)} %add.121), channel_id=1, source_target_pairs={{0,1},{1,0},{2,3},{3,2},{4,5},{5,4},{6,7},{7,6},{8,9},{9,8},{10,11... | collective-permute-start | bytes 196616 | tf_op jit(solution)/shard_map/ppermute | solution.py:308
  39.5 4.4 %collective-permute-start.7 = (bf16[768,512]{1,0:T(8,128)(2,1)S(1)}, bf16[768,512]{1,0:T(8,128)(2,1)}, u32[]{:S(2)}, u32[]{:S(2)}) collective-permute-start(bf16[768,512]{1,0:T(8,128)(2,1)S(1)} %get-tuple-element.21), channel_id=1, source_target_pairs={{0,1},{1,0},{2,3},{3,2},{4,5},{5,4},{6,7},{7,6},{8,9},{9,8},{10,11... | collective-permute-start | bytes 2359304 | tf_op jit(solution)/shard_map/ppermute | solution.py:308
  39.7 2.2 %collective-permute-start.5 = (f32[16,1152]{1,0:T(8,128)S(1)}, f32[16,1152]{1,0:T(8,128)S(1)}, u32[]{:S(2)}, u32[]{:S(2)}) collective-permute-start(f32[16,1152]{1,0:T(8,128)S(1)} %select_bitcast_fusion), channel_id=1, source_target_pairs={{0,1},{1,0},{2,3},{3,2},{4,5},{5,4},{6,7},{7,6},{8,9},{9,8},{10,11... | collective-permute-start | bytes 221192 | tf_op jit(solution)/shard_map/ppermute | solution.py:308
  42.0 5.2 %collective-permute-start.6 = (f32[16,1152]{1,0:T(8,128)S(1)}, f32[16,1152]{1,0:T(8,128)S(1)}, u32[]{:S(2)}, u32[]{:S(2)}) collective-permute-start(f32[16,1152]{1,0:T(8,128)S(1)} %bitcast_add_fusion.5), channel_id=1, source_target_pairs={{0,2},{1,3},{2,0},{3,1},{4,6},{5,7},{6,4},{7,5},{8,10},{9,11},{10,... | collective-permute-start | bytes 221192 | tf_op jit(solution)/shard_map/ppermute | solution.py:308
  45.7 1.1 copy-start.11
  46.9 11.0 %collective-permute-start.10 = (bf16[384,512]{1,0:T(8,128)(2,1)S(1)}, bf16[384,512]{1,0:T(8,128)(2,1)S(1)}, u32[]{:S(2)}, u32[]{:S(2)}) collective-permute-start(bf16[384,512]{1,0:T(8,128)(2,1)S(1)} %fusion.2), channel_id=1, source_target_pairs={{0,2},{1,3},{2,0},{3,1},{4,6},{5,7},{6,4},{7,5},{8,10},{9,11},{10,... | collective-permute-start | bytes 1179656 | tf_op jit(solution)/shard_map/ppermute | solution.py:308
  47.2 4.4 %collective-permute-start.8 = (f32[16,1152]{1,0:T(8,128)S(1)}, f32[16,1152]{1,0:T(8,128)S(1)}, u32[]{:S(2)}, u32[]{:S(2)}) collective-permute-start(f32[16,1152]{1,0:T(8,128)S(1)} %pad_add_fusion.1), channel_id=1, source_target_pairs={{0,4},{1,5},{2,6},{3,7},{4,0},{5,1},{6,2},{7,3},{8,12},{9,13},{10,... | collective-permute-start | bytes 221192 | tf_op jit(solution)/shard_map/ppermute | solution.py:308
  51.6 7.5 %collective-permute-start.9 = (f32[16,1152]{1,0:T(8,128)S(1)}, f32[16,1152]{1,0:T(8,128)S(1)}, u32[]{:S(2)}, u32[]{:S(2)}) collective-permute-start(f32[16,1152]{1,0:T(8,128)S(1)} %add.126), channel_id=1, source_target_pairs={{0,8},{1,9},{2,10},{3,11},{4,12},{5,13},{6,14},{7,15},{8,0},{9,1},... | collective-permute-start | bytes 221192 | tf_op jit(solution)/shard_map/ppermute | solution.py:308
  59.2 1.8 %collective-permute-start.11 = (f32[16,1152]{1,0:T(8,128)S(1)}, f32[16,1152]{1,0:T(8,128)S(1)}, u32[]{:S(2)}, u32[]{:S(2)}) collective-permute-start(f32[16,1152]{1,0:T(8,128)S(1)} %pad_add_fusion), channel_id=1, source_target_pairs={{0,1},{1,0},{2,3},{3,2},{4,5},{5,4},{6,7},{7,6},{8,9},{9,8},{10,11... | collective-permute-start | bytes 221192 | tf_op jit(solution)/shard_map/ppermute | solution.py:308
  59.3 11.1 %collective-permute-start.12 = (bf16[192,512]{1,0:T(8,128)(2,1)S(1)}, bf16[192,512]{1,0:T(8,128)(2,1)S(1)}, u32[]{:S(2)}, u32[]{:S(2)}) collective-permute-start(bf16[192,512]{1,0:T(8,128)(2,1)S(1)} %fusion.4), channel_id=1, source_target_pairs={{0,4},{1,5},{2,6},{3,7},{4,0},{5,1},{6,2},{7,3},{8,12},{9,13},{10,... | collective-permute-start | bytes 589832 | tf_op jit(solution)/shard_map/ppermute | solution.py:308
  70.4 1.3 %copy-start = (f32[512,1024]{1,0:T(8,128)}, f32[512,1024]{1,0:T(8,128)S(1)}, u32[]{:S(2)}) copy-start(f32[512,1024]{1,0:T(8,128)S(1)} %get-tuple-element.23) | copy-start | bytes 6291460
  71.8 2.0 %collective-permute-start.13 = (bf16[256,1024]{1,0:T(8,128)(2,1)S(1)}, bf16[256,1024]{1,0:T(8,128)(2,1)S(1)}, u32[]{:S(2)}, u32[]{:S(2)}) collective-permute-start(bf16[256,1024]{1,0:T(8,128)(2,1)S(1)} %fusion.1), channel_id=1, source_target_pairs={{0,1},{1,0},{2,3},{3,2},{4,5},{5,4},{6,7},{7,6},{8,9},{9,8},{10,11... | collective-permute-start | bytes 1572872 | tf_op jit(solution)/shard_map/ppermute | solution.py:308
  75.2 8.5 %collective-permute-start.14 = (bf16[128,1024]{1,0:T(8,128)(2,1)S(1)}, bf16[128,1024]{1,0:T(8,128)(2,1)S(1)}, u32[]{:S(2)}, u32[]{:S(2)}) collective-permute-start(bf16[128,1024]{1,0:T(8,128)(2,1)S(1)} %fusion.3), channel_id=1, source_target_pairs={{0,2},{1,3},{2,0},{3,1},{4,6},{5,7},{6,4},{7,5},{8,10},{9,11},{10,... | collective-permute-start | bytes 786440 | tf_op jit(solution)/shard_map/ppermute | solution.py:308
  75.7 12.5 %collective-permute-start.17 = (bf16[192,512]{1,0:T(8,128)(2,1)S(1)}, bf16[192,512]{1,0:T(8,128)(2,1)S(1)}, u32[]{:S(2)}, u32[]{:S(2)}) collective-permute-start(bf16[192,512]{1,0:T(8,128)(2,1)S(1)} %get-tuple-element.26), channel_id=1, source_target_pairs={{0,8},{1,9},{2,10},{3,11},{4,12},{5,13},{6,14},{7,15},{8,0},{9,1},... | collective-permute-start | bytes 589832 | tf_op jit(solution)/shard_map/ppermute | solution.py:308
  83.7 7.3 %collective-permute-start.15 = (bf16[64,1024]{1,0:T(8,128)(2,1)S(1)}, bf16[64,1024]{1,0:T(8,128)(2,1)S(1)}, u32[]{:S(2)}, u32[]{:S(2)}) collective-permute-start(bf16[64,1024]{1,0:T(8,128)(2,1)S(1)} %fusion.6), channel_id=1, source_target_pairs={{0,4},{1,5},{2,6},{3,7},{4,0},{5,1},{6,2},{7,3},{8,12},{9,13},{10,... | collective-permute-start | bytes 393224 | tf_op jit(solution)/shard_map/ppermute | solution.py:308
  88.3 8.0 %collective-permute-start.18 = (bf16[192,512]{1,0:T(8,128)(2,1)S(1)}, bf16[192,512]{1,0:T(8,128)(2,1)S(1)}, u32[]{:S(2)}, u32[]{:S(2)}) collective-permute-start(bf16[192,512]{1,0:T(8,128)(2,1)S(1)} %fusion.5), channel_id=1, source_target_pairs={{0,4},{1,5},{2,6},{3,7},{4,0},{5,1},{6,2},{7,3},{8,12},{9,13},{10,... | collective-permute-start | bytes 589832 | tf_op jit(solution)/shard_map/ppermute | solution.py:308
  91.0 9.1 %collective-permute-start.16 = (bf16[64,1024]{1,0:T(8,128)(2,1)S(1)}, bf16[64,1024]{1,0:T(8,128)(2,1)S(1)}, u32[]{:S(2)}, u32[]{:S(2)}) collective-permute-start(bf16[64,1024]{1,0:T(8,128)(2,1)S(1)} %get-tuple-element.28), channel_id=1, source_target_pairs={{0,8},{1,9},{2,10},{3,11},{4,12},{5,13},{6,14},{7,15},{8,0},{9,1},... | collective-permute-start | bytes 393224 | tf_op jit(solution)/shard_map/ppermute | solution.py:308
  96.4 8.9 %collective-permute-start.20 = (bf16[384,512]{1,0:T(8,128)(2,1)S(1)}, bf16[384,512]{1,0:T(8,128)(2,1)S(1)}, u32[]{:S(2)}, u32[]{:S(2)}) collective-permute-start(bf16[384,512]{1,0:T(8,128)(2,1)S(1)} %maximum_add_fusion.1), channel_id=1, source_target_pairs={{0,2},{1,3},{2,0},{3,1},{4,6},{5,7},{6,4},{7,5},{8,10},{9,11},{10,... | collective-permute-start | bytes 1179656 | tf_op jit(solution)/shard_map/ppermute | solution.py:308
  100.2 5.0 %collective-permute-start.19 = (bf16[64,1024]{1,0:T(8,128)(2,1)S(1)}, bf16[64,1024]{1,0:T(8,128)(2,1)S(1)}, u32[]{:S(2)}, u32[]{:S(2)}) collective-permute-start(bf16[64,1024]{1,0:T(8,128)(2,1)S(1)} %fusion.7), channel_id=1, source_target_pairs={{0,4},{1,5},{2,6},{3,7},{4,0},{5,1},{6,2},{7,3},{8,12},{9,13},{10,... | collective-permute-start | bytes 393224 | tf_op jit(solution)/shard_map/ppermute | solution.py:308
  105.5 8.9 %collective-permute-start.22 = (bf16[768,512]{1,0:T(8,128)(2,1)S(1)}, bf16[768,512]{1,0:T(8,128)(2,1)S(1)}, u32[]{:S(2)}, u32[]{:S(2)}) collective-permute-start(bf16[768,512]{1,0:T(8,128)(2,1)S(1)} %pad_maximum_fusion), channel_id=1, source_target_pairs={{0,1},{1,0},{2,3},{3,2},{4,5},{5,4},{6,7},{7,6},{8,9},{9,8},{10,11... | collective-permute-start | bytes 2359304 | tf_op jit(solution)/shard_map/ppermute | solution.py:308
  105.6 8.8 %collective-permute-start.21 = (bf16[128,1024]{1,0:T(8,128)(2,1)S(1)}, bf16[128,1024]{1,0:T(8,128)(2,1)S(1)}, u32[]{:S(2)}, u32[]{:S(2)}) collective-permute-start(bf16[128,1024]{1,0:T(8,128)(2,1)S(1)} %maximum_add_fusion.2), channel_id=1, source_target_pairs={{0,2},{1,3},{2,0},{3,1},{4,6},{5,7},{6,4},{7,5},{8,10},{9,11},{10,... | collective-permute-start | bytes 786440 | tf_op jit(solution)/shard_map/ppermute | solution.py:308
  115.1 1.3 %copy-start.12 = (f32[1024,512]{1,0:T(8,128)}, f32[1024,512]{1,0:T(8,128)S(1)}, u32[]{:S(2)}) copy-start(f32[1024,512]{1,0:T(8,128)S(1)} %maximum_convert_fusion) | copy-start | bytes 6291460
  115.2 4.1 %collective-permute-start.23 = (bf16[256,1024]{1,0:T(8,128)(2,1)S(1)}, bf16[256,1024]{1,0:T(8,128)(2,1)S(1)}, u32[]{:S(2)}, u32[]{:S(2)}) collective-permute-start(bf16[256,1024]{1,0:T(8,128)(2,1)S(1)} %maximum_add_fusion), channel_id=1, source_target_pairs={{0,1},{1,0},{2,3},{3,2},{4,5},{5,4},{6,7},{7,6},{8,9},{9,8},{10,11... | collective-permute-start | bytes 1572872 | tf_op jit(solution)/shard_map/ppermute | solution.py:308

commit v3 on v2

v3 whole, which is shorter than its diff:
```python
import functools
import math

import jax
import jax.numpy as jnp
from jax import lax
from jax.experimental import pallas as pl
from jax.experimental.pallas import tpu as pltpu
from jax.sharding import PartitionSpec as P

epsilon = 1e-05
f32, bf16 = jnp.float32, jnp.bfloat16
CHUNK_CONV, CHUNK_HEAD, CHUNK_BACK = 128, 128, 128
EXTRA = 128


def split3(x):
    high = x.astype(bf16)
    rest = x - high.astype(f32)
    middle = rest.astype(bf16)
    low = (rest - middle.astype(f32)).astype(bf16)
    return high, middle, low


def contract_rows(left, right):
    return lax.dot_general(
        left, right, (((0,), (0,)), ((), ())), preferred_element_type=f32
    )


def contract_cols(left, right):
    return lax.dot_general(
        left, right, (((1,), (1,)), ((), ())), preferred_element_type=f32
    )


def matmul(left, right):
    return jnp.dot(left, right, preferred_element_type=f32)


def one_hot(assign, groups, cap_rows):
    low = lax.broadcasted_iota(jnp.int32, (groups, assign.shape[1]), 0) * cap_rows
    return jnp.where((assign >= low) & (assign < low + cap_rows), 1.0, 0.0)


def group_sums(member, values):
    high = values.astype(bf16)
    low = (values - high.astype(f32)).astype(bf16)
    return matmul(member, high) + matmul(member, low)


def spread(member, values):
    return contract_rows(
        jnp.concatenate([member] * 3, axis=0).astype(bf16),
        jnp.concatenate(split3(values), axis=0),
    )


def moments(first, second, pixel_count):
    mean = first * (1.0 / pixel_count)
    variance = second * (1.0 / pixel_count) - mean * mean
    return mean, lax.rsqrt(variance + epsilon)


def conv_kernel(cap_rows, x_ref, assign_ref, w_ref, before_ref, sums_ref):
    positions, tiles_all, width = x_ref.shape
    groups, emb_width = sums_ref.shape[1:]
    tiles = CHUNK_CONV
    inputs = jnp.zeros((groups, width), f32)
    squares = jnp.zeros((groups, emb_width), f32)
    for start in range(0, tiles_all, tiles):
        rows = pl.ds(start, tiles)
        x = x_ref[:, rows].reshape(positions * tiles, width)
        before = matmul(x, w_ref[...])
        before_ref[:, rows] = before.reshape(positions, tiles, emb_width)
        parts = [before[p * tiles : (p + 1) * tiles] for p in range(positions)]
        second = sum([v * v for v in parts[1:]], parts[0] * parts[0])
        member = one_hot(assign_ref[:, rows], groups, cap_rows).astype(bf16)
        inputs += matmul(jnp.concatenate([member] * positions, axis=1), x)
        squares += group_sums(member, second)
    terms = matmul(jnp.concatenate(split3(inputs), axis=0), w_ref[...])
    sums_ref[0] = terms[:groups] + terms[groups : 2 * groups] + terms[2 * groups :]
    sums_ref[1] = squares


def head_kernel(
    cap_rows,
    pixel_count,
    slides_all,
    counts_ref,
    labels_ref,
    core_ref,
    before_ref,
    assign_ref,
    first_ref,
    second_ref,
    gain_ref,
    shift_ref,
    w_fc_ref,
    w_gate_ref,
    w_score_ref,
    w_cls_ref,
    send_ref,
    keep_ref,
    grad_embedded_ref,
    sums_ref,
    embedded_ref,
    count_ref,
    total_ref,
    grad_ref,
):
    positions, tiles_all, emb_width = before_ref.shape
    tiles = CHUNK_HEAD
    groups = first_ref.shape[0]
    mean, inverse = moments(first_ref[...], second_ref[...], pixel_count)
    scale = inverse * gain_ref[...]
    offset = shift_ref[...] - mean * scale
    both = jnp.concatenate([scale, offset], axis=1)
    for begin in range(0, tiles_all, tiles):
        rows = pl.ds(begin, tiles)
        spread_rows = spread(one_hot(assign_ref[:, rows], groups, cap_rows), both)
        scale, offset = spread_rows[:, :emb_width], spread_rows[:, emb_width:]
        count = jnp.zeros((tiles, emb_width), f32)
        total = jnp.zeros((tiles, emb_width), f32)
        for p in range(positions):
            value = before_ref[p, rows]
            live = value * scale + offset > 0
            count += jnp.where(live, 1.0, 0.0)
            total += jnp.where(live, value, 0.0)
        embedded_ref[rows] = ((total * scale + count * offset) * (1.0 / positions)).astype(bf16)
        count_ref[rows] = count
        total_ref[rows] = total

    embedded = embedded_ref[...]
    slides = counts_ref.shape[1]
    pre = matmul(embedded, w_fc_ref[...])
    hidden = jnp.maximum(pre, 0.0).astype(bf16)
    gate_pre = matmul(hidden, w_gate_ref[...])
    half = gate_pre.shape[1] // 2
    wave = jnp.tanh(gate_pre[:, :half])
    sig = jax.nn.sigmoid(gate_pre[:, half:])
    mix = wave * sig
    w_score = w_score_ref[...]
    score = jnp.sum(mix * w_score, axis=1, keepdims=True)

    lane = lax.broadcasted_iota(jnp.int32, (1, 128), 1)
    row = lax.broadcasted_iota(jnp.int32, (tiles_all, 128), 0)
    low = jnp.zeros((1, 128), jnp.int32)
    high = jnp.zeros((1, 128), jnp.int32)
    start = jnp.int32(0)
    for s in range(slides):
        end = start + counts_ref[0, s]
        low = jnp.where(lane == s, start, low)
        high = jnp.where(lane == s, end, high)
        start = end
    weight = jnp.where((row >= low) & (row < high), jnp.exp(score), 0.0)
    totals = jnp.sum(weight, axis=0, keepdims=True)
    attention = weight / jnp.where(lane < slides, totals, 1.0)
    att_high, att_middle, att_low = split3(attention)
    pooled = (
        contract_rows(att_high, hidden)
        + contract_rows(att_middle, hidden)
        + contract_rows(att_low, hidden)
    )[:8]
    slot = lax.broadcasted_iota(jnp.int32, (8, 1), 0)
    label = jnp.zeros((8, 1), jnp.int32)
    for s in range(slides):
        label = jnp.where(slot == s, labels_ref[0, s], label)
    classes = w_cls_ref.shape[0]
    w_cls = [w_cls_ref[c : c + 1, :] for c in range(classes)]
    logits = [jnp.sum(pooled * w, axis=1, keepdims=True) for w in w_cls]
    powers = [jnp.exp(v) for v in logits]
    power = sum(powers[1:], powers[0])
    target = sum(jnp.where(label == c, v, 0.0) for c, v in enumerate(logits))
    used = slot < slides
    loss = jnp.sum(jnp.where(used, jnp.log(power) - target, 0.0), axis=0, keepdims=True) * (
        1.0 / slides_all
    )
    grad_logits = [
        jnp.where(used, v / power - jnp.where(label == c, 1.0, 0.0), 0.0) * (1.0 / slides_all)
        for c, v in enumerate(powers)
    ]
    grad_cls = [jnp.sum(g * pooled, axis=0, keepdims=True) for g in grad_logits]
    grad_pooled = sum(g * w for g, w in zip(grad_logits, w_cls))
    grad_pooled = jnp.concatenate(
        [grad_pooled, jnp.zeros((128 - 8, grad_pooled.shape[1]), f32)], axis=0
    )
    gp_high, gp_middle, gp_low = split3(grad_pooled)
    grad_attention = (
        contract_cols(hidden, gp_high)
        + contract_cols(hidden, gp_middle)
        + contract_cols(hidden, gp_low)
    )
    product = attention * grad_attention
    centre = jnp.sum(product, axis=0, keepdims=True)
    grad_score = jnp.sum(product - attention * centre, axis=1, keepdims=True)
    grad_w_score = jnp.sum(grad_score * mix, axis=0, keepdims=True)
    grad_mix = grad_score * w_score
    gates_low = jnp.concatenate(
        [grad_mix * sig * (1.0 - wave * wave), grad_mix * mix * (1.0 - sig)], axis=1
    ).astype(bf16)
    grad_hidden = matmul(
        jnp.concatenate([att_high, att_high, att_middle], axis=1),
        jnp.concatenate([gp_high, gp_middle, gp_high], axis=0),
    )
    grad_hidden += contract_cols(gates_low, w_gate_ref[...])
    before_low = jnp.where(pre > 0, grad_hidden, 0.0).astype(bf16)
    core = core_ref[0, 0]
    rows_fc, rows_gate = emb_width // 2, pre.shape[1] // 2
    halves_fc = grad_ref.at[:, pl.ds(0, rows_fc)]
    halves_gate = grad_ref.at[:, pl.ds(rows_fc, rows_gate)]
    halves_fc[...] = contract_rows(embedded, before_low).reshape(2, rows_fc, -1)
    halves_gate[...] = contract_rows(hidden, gates_low).reshape(2, rows_gate, -1)
    send_ref[...] = grad_ref[1 - core].astype(bf16)
    keep_ref[...] = grad_ref[core]
    grad_embedded = contract_cols(before_low, w_fc_ref[...]).astype(bf16)
    grad_embedded_ref[...] = grad_embedded
    each = grad_embedded.astype(f32) * (1.0 / positions)
    member_all = one_hot(assign_ref[...], groups, cap_rows).astype(bf16)
    shift_sums = group_sums(member_all, each * count_ref[...])
    total_sums = group_sums(member_all, each * total_ref[...])
    sums_ref[0, :, :emb_width] = shift_sums
    sums_ref[1, :, :emb_width] = (total_sums - mean * shift_sums) * inverse
    sums_ref[:, :, emb_width:] = jnp.zeros((2, groups, EXTRA), f32)
    for i in range(half // EXTRA):
        sums_ref[0, i : i + 1, emb_width:] = grad_w_score[:, i * EXTRA : (i + 1) * EXTRA]
    i = half // EXTRA
    sums_ref[0, i : i + 1, emb_width:] = jnp.where(lane == 0, loss, 0.0)
    grad_cls = jnp.concatenate(grad_cls, axis=1)
    for i in range(grad_cls.shape[1] // EXTRA):
        sums_ref[1, i : i + 1, emb_width:] = grad_cls[:, i * EXTRA : (i + 1) * EXTRA]


def back_kernel(
    cap_rows,
    pixel_count,
    x_ref,
    before_ref,
    grad_embedded_ref,
    assign_ref,
    first_ref,
    second_ref,
    shift_sums_ref,
    gain_sums_ref,
    gain_ref,
    shift_ref,
    grad_ref,
    grad_gain_ref,
    grad_shift_ref,
):

    positions, tiles_all, emb_width = before_ref.shape
    tiles = CHUNK_BACK
    groups = first_ref.shape[0]
    mean, inverse = moments(first_ref[...], second_ref[...], pixel_count)
    scale = inverse * gain_ref[...]
    offset = shift_ref[...] - mean * scale
    slope = scale * inverse * gain_sums_ref[:, :emb_width] * (1.0 / pixel_count)
    constant = scale * shift_sums_ref[:, :emb_width] * (1.0 / pixel_count) - mean * slope
    grad_gain_ref[...] = jnp.sum(gain_sums_ref[:, :emb_width], axis=0, keepdims=True)
    grad_shift_ref[...] = jnp.sum(shift_sums_ref[:, :emb_width], axis=0, keepdims=True)
    every = jnp.concatenate([scale, offset, slope, constant], axis=1)
    for start in range(0, tiles_all, tiles):
        rows = pl.ds(start, tiles)
        spread_rows = spread(one_hot(assign_ref[:, rows], groups, cap_rows), every)
        scale, offset, slope, constant = (
            spread_rows[:, i * emb_width : (i + 1) * emb_width] for i in range(4)
        )
        direct = grad_embedded_ref[rows].astype(f32) * scale * (1.0 / positions)
        grads = []
        for p in range(positions):
            value = before_ref[p, rows]
            live = value * scale + offset > 0
            grads.append((jnp.where(live, direct, 0.0) - constant - value * slope).astype(bf16))
        part = contract_rows(
            x_ref[:, rows].reshape(positions * tiles, x_ref.shape[2]),
            jnp.concatenate(grads, axis=0),
        )
        if start == 0:
            grad_ref[...] = part
        else:
            grad_ref[...] += part


def round_low(x):
    return lax.reduce_precision(x, 8, 7)


def swap(x, bit):
    count = lax.axis_size("enc")
    return lax.ppermute(x, "enc", [(i, i ^ (1 << bit)) for i in range(count)])


def wait_for(x, other):
    corner = (other[:16, :128] * 0).astype(x.dtype)
    return x + jnp.pad(corner, ((0, x.shape[0] - 16), (0, x.shape[1] - 128)))


class SmallSum:
    def __init__(self, pair, firsts):
        self.core = firsts[0]
        self.x = jnp.where(self.core, pair[0], pair[1])
        self.x += swap(jnp.where(self.core, pair[1], pair[0]), 0)

    def hop(self, level):
        self.x += swap(self.x, level)

    def result(self):
        other = swap(self.x, 0)
        return jnp.where(self.core, self.x, other), jnp.where(self.core, other, self.x)


class LargeSum:
    def __init__(self, x, firsts):
        self.x = x
        self.firsts = firsts

    def halve(self, level, other=None):
        half = self.x.shape[0] // 2
        low, high = self.x[:half], self.x[half:]
        first = self.firsts[level]
        send = jnp.where(first, high, low).astype(bf16)
        if other is not None:
            send = wait_for(send, other)
        self.x = jnp.where(first, low, high) + swap(send, level).astype(f32)

    def exchange(self, level):
        x = round_low(self.x)
        self.x = (x + swap(x.astype(bf16), level).astype(f32)).astype(bf16)

    def pair(self, level):
        other = swap(self.x, level)
        first = self.firsts[level]
        return jnp.where(first, self.x, other), jnp.where(first, other, self.x)

    def double(self, level):
        self.x = jnp.concatenate(self.pair(level), axis=0)


def local(
    tiles, tile_counts, assign, labels, w_conv, bn_gain, bn_shift, w_fc, w_gate, w_score, w_cls
):
    devices = lax.axis_size("enc")
    own_rows, positions, input_width = tiles.shape
    emb_width = w_conv.shape[1]
    hid_width = w_fc.shape[1]
    slot_rows = assign.shape[1]
    cap_rows = slot_rows // devices
    group_tiles = (
        devices // 4 * (4 + (cap_rows - 2) // 3 + 2 * (cap_rows - 2) // 3 + (cap_rows - 2))
        + devices // 2
    )
    pixel_count = float(group_tiles * positions)
    slides_all = float(devices * tile_counts.shape[1])
    gain, shift = bn_gain.reshape(1, emb_width), bn_shift.reshape(1, emb_width)

    smem = pl.BlockSpec(memory_space=pltpu.SMEM)
    vmem = pl.BlockSpec(memory_space=pltpu.VMEM)

    def settings(mebibytes, microseconds):
        return dict(
            compiler_params=pltpu.CompilerParams(
                vmem_limit_bytes=mebibytes << 20
            ),
            cost_estimate=pl.CostEstimate(
                flops=int(microseconds * 1.1e9), bytes_accessed=8 << 20, transcendentals=0
            ),
        )


    levels = devices.bit_length() - 1
    place = lax.axis_index("enc")
    bits = [(place >> level) & 1 for level in range(levels)]
    firsts, core, work = lax.optimization_barrier(
        ([bit == 0 for bit in bits], bits[0].reshape(1, 1), jnp.transpose(tiles, (1, 0, 2)))
    )
    before, sums = pl.pallas_call(
        functools.partial(conv_kernel, cap_rows),
        in_specs=[vmem] * 3,
        out_specs=[vmem] * 2,
        out_shape=[
            jax.ShapeDtypeStruct((positions, own_rows, emb_width), f32),
            jax.ShapeDtypeStruct((2, devices, emb_width), f32),
        ],
        name="conv_sums",
        **settings(20, 6),
    )(work, assign, w_conv)
    total = SmallSum(sums, firsts)
    for level in range(1, levels):
        total.hop(level)
    first, second = total.result()

    half_rows = (emb_width + hid_width) // 2
    send, keep, grad_embedded, sums = pl.pallas_call(
        functools.partial(head_kernel, cap_rows, pixel_count, slides_all),
        in_specs=[smem] * 3 + [vmem] * 10,
        out_specs=[vmem] * 4,
        out_shape=[
            jax.ShapeDtypeStruct((half_rows, hid_width), bf16),
            jax.ShapeDtypeStruct((half_rows, hid_width), f32),
            jax.ShapeDtypeStruct((own_rows, emb_width), bf16),
            jax.ShapeDtypeStruct((2, devices, emb_width + EXTRA), f32),
        ],
        scratch_shapes=[
            pltpu.VMEM((own_rows, emb_width), bf16),
            pltpu.VMEM((own_rows, emb_width), f32),
            pltpu.VMEM((own_rows, emb_width), f32),
            pltpu.VMEM((2, half_rows, hid_width), f32),
        ],
        name="norm_head",
        **settings(32, 12),
    )(
        tile_counts,
        labels,
        core,
        before,
        assign,
        first,
        second,
        gain,
        shift,
        w_fc,
        w_gate,
        w_score.reshape(1, -1),
        w_cls.T,
    )
    total = SmallSum(sums, firsts)
    rows_fc = emb_width // 2
    head = LargeSum(keep + swap(send, 0).astype(f32), firsts)
    total.hop(1)
    total.x = wait_for(total.x, head.x)
    head.halve(1)
    for level in range(2, levels):
        total.hop(level)
    total.x = wait_for(total.x, head.x)
    shift_sums, gain_sums = total.result()

    grad_conv, grad_gain, grad_shift = pl.pallas_call(
        functools.partial(back_kernel, cap_rows, pixel_count),
        in_specs=[vmem] * 10,
        out_specs=[vmem] * 3,
        out_shape=[
            jax.ShapeDtypeStruct((input_width, emb_width), f32),
            jax.ShapeDtypeStruct((1, emb_width), f32),
            jax.ShapeDtypeStruct((1, emb_width), f32),
        ],
        name="norm_back",
        **settings(20, 7),
    )(work, before, grad_embedded, assign, first, second, shift_sums, gain_sums, gain, shift)

    conv = LargeSum(grad_conv, firsts)
    for level in range(2, levels - 1):
        head.halve(level)
    conv.halve(0, head.x)
    conv.halve(1)
    head.exchange(levels - 1)
    head.x = wait_for(head.x, conv.x)
    for level in range(2, levels - 1):
        conv.halve(level)
    for level in range(levels - 2, 1, -1):
        head.double(level)
    head.x = wait_for(head.x, conv.x)
    conv.exchange(levels - 1)
    conv.x = wait_for(conv.x, head.x)
    for level in range(levels - 2, 1, -1):
        conv.double(level)
    head.double(1)
    conv.x = wait_for(conv.x, head.x)
    conv.double(1)
    low, high = head.pair(0)
    grad_fc = jnp.concatenate([low[:rows_fc], high[:rows_fc]], axis=0).astype(f32)
    grad_gate = jnp.concatenate([low[rows_fc:], high[rows_fc:]], axis=0).astype(f32)
    conv.x = wait_for(conv.x, grad_fc)
    conv.double(0)
    grad_conv = conv.x.astype(f32)
    scores = w_score.shape[0] // EXTRA
    classes = math.prod(w_cls.shape) // EXTRA
    return (
        shift_sums[scores, emb_width : emb_width + 1],
        grad_conv,
        grad_gain.reshape(emb_width),
        grad_shift.reshape(emb_width),
        grad_fc,
        grad_gate,
        shift_sums[:scores, emb_width:].reshape(-1),
        gain_sums[:classes, emb_width:].reshape(w_cls.shape[::-1]).T,
    )


def solution(mesh):
    per_device = P(("groups", "enc"), None)
    placed = (P(("groups", "enc"), None, None), per_device, per_device, per_device) + (P(),) * 7
    rows_out = P("groups", None)
    return jax.shard_map(
        local,
        mesh=mesh,
        in_specs=placed,
        out_specs=(
            P("groups"),
            rows_out,
            P("groups"),
            P("groups"),
            rows_out,
            rows_out,
            P("groups"),
            rows_out,
        ),
        check_vma=False,
    )
```

time: 121 us -> 109 us (0.901)
  Pallas kernels: 28.2 us -> 18.7 us
  waiting for transfers between devices: 47 us -> 50.4 us
  other arithmetic: 8.59 us -> 5.26 us
  local copies, waits for them, and re-layouts: 7.59 us -> 5.25 us
    pallas_call x2, Pallas kernels: 15.4 us -> 9.74 us  [the longest x1 6.36 us: local(): pl.pallas_call(functools.partial(back_kernel, cap_rows, pixel_count), in_...]
    pallas_call x1, Pallas kernels: 12.8 us -> 9 us  [local(): pl.pallas_call(functools.partial(head_kernel, cap_rows, pixel_count, slid...]
    add x4, other arithmetic: 4.53 us -> 0.87 us  [the longest x3 0.59 us: halve(): self.x = jnp.where(first, low, high) + swap(send, level).astype(f32)]
    ppermute x24, waiting for transfers between devices: 47 us -> 50.4 us  [swap(): return lax.ppermute(x, 'enc', [(i, i ^ 1 << bit) for i in range(count)])]
    unnamed x27 -> x23, local copies, waits for them, and re-layouts: 5.66 us -> 3.46 us
  transfers between devices with their start and end apart: 24 -> 24, of which waited for: 17 -> 19; matrix products, arithmetic and copies ran while one was open for 5% -> 4% of each run, Pallas kernels for 8% -> 6%
where the time goes in v3:
time: 109 us
  waiting for transfers between devices  50.4 us (46%)
  starting transfers between devices  27.9 us (26%)
  Pallas kernels  18.7 us (17%)
  other arithmetic  5.26 us (5%)
  local copies, waits for them, and re-layouts  5.25 us (5%)
  between operations  1.13 us (1%)
    ppermute x24, waiting for transfers between devices, swap(): return lax.ppermute(x, 'enc', [(i, i ^ 1 << bit) for i in range(count)])  50.4 us
    ppermute x24, starting transfers between devices, swap(): return lax.ppermute(x, 'enc', [(i, i ^ 1 << bit) for i in range(count)])  27.9 us
    pallas_call x1, Pallas kernels, local(): pl.pallas_call(functools.partial(head_kernel, cap_rows, pixel_count, slid...  9 us
    pallas_call x1, Pallas kernels, local(): pl.pallas_call(functools.partial(back_kernel, cap_rows, pixel_count), in_...  6.36 us
    unnamed x23, local copies, waits for them, and re-layouts  3.46 us
    pallas_call x1, Pallas kernels, local(): pl.pallas_call(functools.partial(conv_kernel, cap_rows), in_specs=[vmem]...  3.38 us
  transfers between devices with their start and end apart: 24, of which 19 were waited for; matrix products, arithmetic and copies ran while one was open for 4% of the time, Pallas kernels for 6%

profile of v3, /device:TPU:0, one launch (start us, length us, event | category | flops | bytes accessed | tf_op | source)
XLA Modules:
  0.0 108.7 jit_solution(13681876849562872623)
XLA Ops:
  0.7 2.1 %copy.21 = bf16[512,4,512]{2,0,1:T(8,128)(2,1)S(1)} copy(bf16[512,4,512]{2,1,0:T(4,128)(2,1)} %param.11) | data formatting | bytes 4194304 | tf_op args[0]
  2.9 3.4 %conv_sums.1 = (f32[4,512,1024]{2,1,0:T(8,128)S(1)}, f32[2,16,1024]{2,1,0:T(8,128)S(1)}) custom-call(bf16[4,512,512]{2,1,0:T(8,128)(2,1)S(1)} %bitcast.22, s32[1,512]{1,0:T(1,128)S(1)} %copy-done.6, bf16[512,1024]{1,0:T(8,128)(2,1)S(1)} %copy-done), custom_call_target="tpu_custom_call" | custom-call | flops 6600000000 | bytes 8388608 | tf_op jit(solution)/shard_map/conv_sums/pallas_call | solution.py:377
  6.3 0.5 collective-permute-start
  6.8 0.9 collective-permute-done
  7.7 2.9 %collective-permute-start.1 = (f32[16,1024]{1,0:T(8,128)S(1)}, f32[16,1024]{1,0:T(8,128)S(1)}, u32[]{:S(2)}, u32[]{:S(2)}) collective-permute-start(f32[16,1024]{1,0:T(8,128)S(1)} %bitcast_add_fusion.1), channel_id=1, source_target_pairs={{0,2},{1,3},{2,0},{3,1},{4,6},{5,7},{6,4},{7,5},{8,10},{9,11},{10,... | collective-permute-start | bytes 196616 | tf_op jit(solution)/shard_map/ppermute | solution.py:291
  10.7 2.4 %collective-permute-done.1 = f32[16,1024]{1,0:T(8,128)S(1)} collective-permute-done((f32[16,1024]{1,0:T(8,128)S(1)}, f32[16,1024]{1,0:T(8,128)S(1)}, u32[]{:S(2)}, u32[]{:S(2)}) %collective-permute-start.1) | collective-permute-done | bytes 65568 | tf_op jit(solution)/shard_map/ppermute | solution.py:291
  13.1 2.0 %collective-permute-start.2 = (f32[16,1024]{1,0:T(8,128)S(1)}, f32[16,1024]{1,0:T(8,128)S(1)}, u32[]{:S(2)}, u32[]{:S(2)}) collective-permute-start(f32[16,1024]{1,0:T(8,128)S(1)} %add.89), channel_id=1, source_target_pairs={{0,4},{1,5},{2,6},{3,7},{4,0},{5,1},{6,2},{7,3},{8,12},{9,13},{10,... | collective-permute-start | bytes 196616 | tf_op jit(solution)/shard_map/ppermute | solution.py:291
  15.1 2.4 %collective-permute-done.2 = f32[16,1024]{1,0:T(8,128)S(1)} collective-permute-done((f32[16,1024]{1,0:T(8,128)S(1)}, f32[16,1024]{1,0:T(8,128)S(1)}, u32[]{:S(2)}, u32[]{:S(2)}) %collective-permute-start.2) | collective-permute-done | bytes 65568 | tf_op jit(solution)/shard_map/ppermute | solution.py:291
  17.4 3.0 %collective-permute-start.3 = (f32[16,1024]{1,0:T(8,128)S(1)}, f32[16,1024]{1,0:T(8,128)S(1)}, u32[]{:S(2)}, u32[]{:S(2)}) collective-permute-start(f32[16,1024]{1,0:T(8,128)S(1)} %add.90), channel_id=1, source_target_pairs={{0,8},{1,9},{2,10},{3,11},{4,12},{5,13},{6,14},{7,15},{8,0},{9,1},... | collective-permute-start | bytes 196616 | tf_op jit(solution)/shard_map/ppermute | solution.py:291
  20.4 2.2 %collective-permute-done.3 = f32[16,1024]{1,0:T(8,128)S(1)} collective-permute-done((f32[16,1024]{1,0:T(8,128)S(1)}, f32[16,1024]{1,0:T(8,128)S(1)}, u32[]{:S(2)}, u32[]{:S(2)}) %collective-permute-start.3) | collective-permute-done | bytes 65568 | tf_op jit(solution)/shard_map/ppermute | solution.py:291
  22.8 1.2 %collective-permute-done.4 = f32[16,1024]{1,0:T(8,128)S(1)} collective-permute-done((f32[16,1024]{1,0:T(8,128)S(1)}, f32[16,1024]{1,0:T(8,128)S(1)}, u32[]{:S(2)}, u32[]{:S(2)}) %collective-permute-start.4) | collective-permute-done | bytes 65568 | tf_op jit(solution)/shard_map/ppermute | solution.py:291
  24.1 9.0 %norm_head.1 = (bf16[768,512]{1,0:T(8,128)(2,1)S(1)}, f32[768,512]{1,0:T(8,128)S(1)}, bf16[512,1024]{1,0:T(8,128)(2,1)S(1)}, f32[2,16,1152]{2,1,0:T(8,128)S(1)}) custom-call(s32[1,4]{1,0:T(1,128)S(1)} %copy-done.8, s32[1,4]{1,0:T(1,128)S(1)} %copy-done.9, s32[1,1]{1,0:T(1,128)} %bitcast.core_ref, f32[4,512,1024]{2,1,0:T(8,128)S(1)} %get-tuple-element.25.before_ref, ...), custom_call_target="tpu_custom_call" | custom-call | flops 13200000000 | bytes 8388608 | tf_op jit(solution)/shard_map/norm_head/pallas_call | solution.py:394
  33.3 0.4 collective-permute-start.5
  33.7 1.8 %collective-permute-done.5 = f32[16,1152]{1,0:T(8,128)S(1)} collective-permute-done((f32[16,1152]{1,0:T(8,128)S(1)}, f32[16,1152]{1,0:T(8,128)S(1)}, u32[]{:S(2)}, u32[]{:S(2)}) %collective-permute-start.5) | collective-permute-done | bytes 73760 | tf_op jit(solution)/shard_map/ppermute | solution.py:291
  35.5 1.9 %collective-permute-start.6 = (f32[16,1152]{1,0:T(8,128)S(1)}, f32[16,1152]{1,0:T(8,128)S(1)}, u32[]{:S(2)}, u32[]{:S(2)}) collective-permute-start(f32[16,1152]{1,0:T(8,128)S(1)} %bitcast_add_fusion), channel_id=1, source_target_pairs={{0,2},{1,3},{2,0},{3,1},{4,6},{5,7},{6,4},{7,5},{8,10},{9,11},{10,... | collective-permute-start | bytes 221192 | tf_op jit(solution)/shard_map/ppermute | solution.py:291
  37.4 0.3 convert_add_fusion
  38.1 2.0 %collective-permute-done.6 = f32[16,1152]{1,0:T(8,128)S(1)} collective-permute-done((f32[16,1152]{1,0:T(8,128)S(1)}, f32[16,1152]{1,0:T(8,128)S(1)}, u32[]{:S(2)}, u32[]{:S(2)}) %collective-permute-start.6) | collective-permute-done | bytes 73760 | tf_op jit(solution)/shard_map/ppermute | solution.py:291
  40.1 1.9 %collective-permute-start.8 = (f32[16,1152]{1,0:T(8,128)S(1)}, f32[16,1152]{1,0:T(8,128)S(1)}, u32[]{:S(2)}, u32[]{:S(2)}) collective-permute-start(f32[16,1152]{1,0:T(8,128)S(1)} %pad_add_fusion.1), channel_id=1, source_target_pairs={{0,4},{1,5},{2,6},{3,7},{4,0},{5,1},{6,2},{7,3},{8,12},{9,13},{10,... | collective-permute-start | bytes 221192 | tf_op jit(solution)/shard_map/ppermute | solution.py:291
  41.9 2.6 %collective-permute-done.8 = f32[16,1152]{1,0:T(8,128)S(1)} collective-permute-done((f32[16,1152]{1,0:T(8,128)S(1)}, f32[16,1152]{1,0:T(8,128)S(1)}, u32[]{:S(2)}, u32[]{:S(2)}) %collective-permute-start.8) | collective-permute-done | bytes 73760 | tf_op jit(solution)/shard_map/ppermute | solution.py:291
  44.5 3.0 %collective-permute-start.9 = (f32[16,1152]{1,0:T(8,128)S(1)}, f32[16,1152]{1,0:T(8,128)S(1)}, u32[]{:S(2)}, u32[]{:S(2)}) collective-permute-start(f32[16,1152]{1,0:T(8,128)S(1)} %add.96), channel_id=1, source_target_pairs={{0,8},{1,9},{2,10},{3,11},{4,12},{5,13},{6,14},{7,15},{8,0},{9,1},... | collective-permute-start | bytes 221192 | tf_op jit(solution)/shard_map/ppermute | solution.py:291
  47.5 1.3 %collective-permute-done.10 = bf16[384,512]{1,0:T(8,128)(2,1)S(1)} collective-permute-done((bf16[384,512]{1,0:T(8,128)(2,1)S(1)}, bf16[384,512]{1,0:T(8,128)(2,1)S(1)}, u32[]{:S(2)}, u32[]{:S(2)}) %collective-permute-start.10) | collective-permute-done | bytes 393248 | tf_op jit(solution)/shard_map/ppermute | solution.py:291
  49.0 0.9 collective-permute-done.9
  50.0 2.1 %collective-permute-start.12 = (bf16[192,512]{1,0:T(8,128)(2,1)S(1)}, bf16[192,512]{1,0:T(8,128)(2,1)S(1)}, u32[]{:S(2)}, u32[]{:S(2)}) collective-permute-start(bf16[192,512]{1,0:T(8,128)(2,1)S(1)} %select_convert_fusion.3), channel_id=1, source_target_pairs={{0,4},{1,5},{2,6},{3,7},{4,0},{5,1},{6,2},{7,3},{8,12},{9,13},{10,... | collective-permute-start | bytes 589832 | tf_op jit(solution)/shard_map/ppermute | solution.py:291
  52.1 6.4 %norm_back.1 = (f32[512,1024]{1,0:T(8,128)S(1)}, f32[1,1024]{1,0:T(1,128)}, f32[1,1024]{1,0:T(1,128)}) custom-call(bf16[4,512,512]{2,1,0:T(8,128)(2,1)S(1)} %bitcast.23, f32[4,512,1024]{2,1,0:T(8,128)S(1)} %get-tuple-element.25.before_ref, bf16[512,1024]{1,0:T(8,128)(2,1)S(1)} %get-tuple-element.32.grad_embedded_ref, s32[1,512]{1,0:T(1,128)S(1)} %copy-done.6, ...), custom_call_target="tpu_custom_call" | custom-call | flops 7699999744 | bytes 8388608 | tf_op jit(solution)/shard_map/norm_back/pallas_call | solution.py:438
  59.0 1.7 %collective-permute-done.13 = bf16[256,1024]{1,0:T(8,128)(2,1)S(1)} collective-permute-done((bf16[256,1024]{1,0:T(8,128)(2,1)S(1)}, bf16[256,1024]{1,0:T(8,128)(2,1)S(1)}, u32[]{:S(2)}, u32[]{:S(2)}) %collective-permute-start.13) | collective-permute-done | bytes 524320 | tf_op jit(solution)/shard_map/ppermute | solution.py:291
  60.7 0.3 convert_add_fusion.1
  61.0 2.3 %collective-permute-start.14 = (bf16[128,1024]{1,0:T(8,128)(2,1)S(1)}, bf16[128,1024]{1,0:T(8,128)(2,1)S(1)}, u32[]{:S(2)}, u32[]{:S(2)}) collective-permute-start(bf16[128,1024]{1,0:T(8,128)(2,1)S(1)} %select_convert_fusion.2), channel_id=1, source_target_pairs={{0,2},{1,3},{2,0},{3,1},{4,6},{5,7},{6,4},{7,5},{8,10},{9,11},{10,... | collective-permute-start | bytes 786440 | tf_op jit(solution)/shard_map/ppermute | solution.py:291
  63.4 3.1 %collective-permute-start.17 = (bf16[192,512]{1,0:T(8,128)(2,1)S(1)}, bf16[192,512]{1,0:T(8,128)(2,1)S(1)}, u32[]{:S(2)}, u32[]{:S(2)}) collective-permute-start(bf16[192,512]{1,0:T(8,128)(2,1)S(1)} %get-tuple-element.36), channel_id=1, source_target_pairs={{0,8},{1,9},{2,10},{3,11},{4,12},{5,13},{6,14},{7,15},{8,0},{9,1},... | collective-permute-start | bytes 589832 | tf_op jit(solution)/shard_map/ppermute | solution.py:291
  66.5 3.5 %collective-permute-done.14 = bf16[128,1024]{1,0:T(8,128)(2,1)S(1)} collective-permute-done((bf16[128,1024]{1,0:T(8,128)(2,1)S(1)}, bf16[128,1024]{1,0:T(8,128)(2,1)S(1)}, u32[]{:S(2)}, u32[]{:S(2)}) %collective-permute-start.14) | collective-permute-done | bytes 262176 | tf_op jit(solution)/shard_map/ppermute | solution.py:291
  70.2 1.2 %collective-permute-start.15 = (bf16[64,1024]{1,0:T(8,128)(2,1)S(1)}, bf16[64,1024]{1,0:T(8,128)(2,1)S(1)}, u32[]{:S(2)}, u32[]{:S(2)}) collective-permute-start(bf16[64,1024]{1,0:T(8,128)(2,1)S(1)} %select_convert_fusion.4), channel_id=1, source_target_pairs={{0,4},{1,5},{2,6},{3,7},{4,0},{5,1},{6,2},{7,3},{8,12},{9,13},{10,... | collective-permute-start | bytes 393224 | tf_op jit(solution)/shard_map/ppermute | solution.py:291
  71.4 4.5 %collective-permute-done.17 = bf16[192,512]{1,0:T(8,128)(2,1)S(1)} collective-permute-done((bf16[192,512]{1,0:T(8,128)(2,1)S(1)}, bf16[192,512]{1,0:T(8,128)(2,1)S(1)}, u32[]{:S(2)}, u32[]{:S(2)}) %collective-permute-start.17) | collective-permute-done | bytes 196640 | tf_op jit(solution)/shard_map/ppermute | solution.py:291
  75.9 0.3 collective-permute-start.18
  76.3 2.4 %collective-permute-done.15 = bf16[64,1024]{1,0:T(8,128)(2,1)S(1)} collective-permute-done((bf16[64,1024]{1,0:T(8,128)(2,1)S(1)}, bf16[64,1024]{1,0:T(8,128)(2,1)S(1)}, u32[]{:S(2)}, u32[]{:S(2)}) %collective-permute-start.15) | collective-permute-done | bytes 131104 | tf_op jit(solution)/shard_map/ppermute | solution.py:291
  78.7 1.3 %collective-permute-start.16 = (bf16[64,1024]{1,0:T(8,128)(2,1)S(1)}, bf16[64,1024]{1,0:T(8,128)(2,1)S(1)}, u32[]{:S(2)}, u32[]{:S(2)}) collective-permute-start(bf16[64,1024]{1,0:T(8,128)(2,1)S(1)} %get-tuple-element.38), channel_id=1, source_target_pairs={{0,8},{1,9},{2,10},{3,11},{4,12},{5,13},{6,14},{7,15},{8,0},{9,1},... | collective-permute-start | bytes 393224 | tf_op jit(solution)/shard_map/ppermute | solution.py:291
  80.0 3.9 %collective-permute-done.18 = bf16[192,512]{1,0:T(8,128)(2,1)S(1)} collective-permute-done((bf16[192,512]{1,0:T(8,128)(2,1)S(1)}, bf16[192,512]{1,0:T(8,128)(2,1)S(1)}, u32[]{:S(2)}, u32[]{:S(2)}) %collective-permute-start.18) | collective-permute-done | bytes 196640 | tf_op jit(solution)/shard_map/ppermute | solution.py:291
  84.0 0.4 collective-permute-start.20
  84.4 3.4 %collective-permute-done.16 = bf16[64,1024]{1,0:T(8,128)(2,1)S(1)} collective-permute-done((bf16[64,1024]{1,0:T(8,128)(2,1)S(1)}, bf16[64,1024]{1,0:T(8,128)(2,1)S(1)}, u32[]{:S(2)}, u32[]{:S(2)}) %collective-permute-start.16) | collective-permute-done | bytes 131104 | tf_op jit(solution)/shard_map/ppermute | solution.py:291
  87.9 5.0 %collective-permute-done.19 = bf16[64,1024]{1,0:T(8,128)(2,1)S(1)} collective-permute-done((bf16[64,1024]{1,0:T(8,128)(2,1)S(1)}, bf16[64,1024]{1,0:T(8,128)(2,1)S(1)}, u32[]{:S(2)}, u32[]{:S(2)}) %collective-permute-start.19) | collective-permute-done | bytes 131104 | tf_op jit(solution)/shard_map/ppermute | solution.py:291
  93.2 0.4 collective-permute-start.21
  93.7 8.3 %collective-permute-done.21 = bf16[128,1024]{1,0:T(8,128)(2,1)S(1)} collective-permute-done((bf16[128,1024]{1,0:T(8,128)(2,1)S(1)}, bf16[128,1024]{1,0:T(8,128)(2,1)S(1)}, u32[]{:S(2)}, u32[]{:S(2)}) %collective-permute-start.21) | collective-permute-done | bytes 262176 | tf_op jit(solution)/shard_map/ppermute | solution.py:291
  102.0 0.3 broadcast_select_fusion.1
  102.5 0.3 maximum_convert_fusion
  102.8 1.3 %copy-done.10 = f32[1024,512]{1,0:T(8,128)} copy-done((f32[1024,512]{1,0:T(8,128)}, f32[1024,512]{1,0:T(8,128)S(1)}, u32[]{:S(2)}) %copy-start.10) | copy-done | bytes 2097176
  104.2 0.5 slice.124
  104.7 0.6 reshape.55
  105.3 0.6 slice_bitcast_fusion
  105.9 1.1 %maximum_convert_fusion.2 = f32[512,512]{1,0:T(8,128)} fusion(bf16[256,512]{1,0:T(8,128)(2,1)S(1)} %slice.140, bf16[256,512]{1,0:T(8,128)(2,1)S(1)} %slice.139), kind=kLoop, calls=%fused_computation.13 | loop fusion | flops 1048576 | bytes 1572864 | tf_op jit(solution)/shard_map/convert_element_type | solution.py:472
  107.1 1.6 %maximum_convert_fusion.1 = f32[512,1024]{1,0:T(8,128)} fusion(bf16[256,1024]{1,0:T(8,128)(2,1)S(1)} %get-tuple-element.43, bf16[256,1024]{1,0:T(8,128)(2,1)S(1)} %get-tuple-element.42), kind=kLoop, calls=%fused_computation.3 | loop fusion | flops 2097152 | bytes 3145728 | tf_op jit(solution)/shard_map/convert_element_type | solution.py:475
  (80 shorter events, 2.7 us)
Async XLA Ops:
  0.6 2.1 %copy-start = (bf16[512,1024]{1,0:T(8,128)(2,1)S(1)}, bf16[512,1024]{1,0:T(8,128)(2,1)}, u32[]{:S(2)}) copy-start(bf16[512,1024]{1,0:T(8,128)(2,1)} %w_ref.1) | copy-start | bytes 3145732
  0.7 2.1 %copy-start.6 = (s32[1,512]{1,0:T(1,128)S(1)}, s32[1,512]{1,0:T(1,128)}, u32[]{:S(2)}) copy-start(s32[1,512]{1,0:T(1,128)} %assign_ref.5) | copy-start | bytes 6148
  2.8 21.2 %copy-start.1 = (bf16[1024,512]{1,0:T(8,128)(2,1)S(1)}, bf16[1024,512]{1,0:T(8,128)(2,1)}, u32[]{:S(2)}) copy-start(bf16[1024,512]{1,0:T(8,128)(2,1)} %w_fc_ref.1) | copy-start | bytes 3145732
  2.8 21.2 %copy-start.2 = (bf16[512,512]{1,0:T(8,128)(2,1)S(1)}, bf16[512,512]{1,0:T(8,128)(2,1)}, u32[]{:S(2)}) copy-start(bf16[512,512]{1,0:T(8,128)(2,1)} %w_gate_ref.1) | copy-start | bytes 1572868
  2.8 21.2 %copy-start.3 = (f32[512,2]{0,1:T(2,128)S(1)}, f32[512,2]{0,1:T(2,128)}, u32[]{:S(2)}) copy-start(f32[512,2]{0,1:T(2,128)} %param.21) | copy-start | bytes 12292
  2.8 21.2 %copy-start.4 = (f32[1024]{0:T(1024)S(1)}, f32[1024]{0:T(1024)}, u32[]{:S(2)}) copy-start(f32[1024]{0:T(1024)} %param.16) | copy-start | bytes 12292
  2.8 21.2 %copy-start.5 = (f32[1024]{0:T(1024)S(1)}, f32[1024]{0:T(1024)}, u32[]{:S(2)}) copy-start(f32[1024]{0:T(1024)} %param.17) | copy-start | bytes 12292
  2.8 21.2 %copy-start.7 = (f32[256]{0:T(256)S(1)}, f32[256]{0:T(256)}, u32[]{:S(2)}) copy-start(f32[256]{0:T(256)} %param.20) | copy-start | bytes 3076
  2.8 21.2 %copy-start.8 = (s32[1,4]{1,0:T(1,128)S(1)}, s32[1,4]{1,0:T(1,128)}, u32[]{:S(2)}) copy-start(s32[1,4]{1,0:T(1,128)} %counts_ref.1) | copy-start | bytes 52
  2.9 21.2 %copy-start.9 = (s32[1,4]{1,0:T(1,128)S(1)}, s32[1,4]{1,0:T(1,128)}, u32[]{:S(2)}) copy-start(s32[1,4]{1,0:T(1,128)} %labels_ref.1) | copy-start | bytes 52
  6.3 1.4 %collective-permute-start = (f32[16,1024]{1,0:T(8,128)S(1)}, f32[16,1024]{1,0:T(8,128)S(1)}, u32[]{:S(2)}, u32[]{:S(2)}) collective-permute-start(f32[16,1024]{1,0:T(8,128)S(1)} %select_bitcast_fusion.1), channel_id=1, source_target_pairs={{0,1},{1,0},{2,3},{3,2},{4,5},{5,4},{6,7},{7,6},{8,9},{9,8},{10,11... | collective-permute-start | bytes 196616 | tf_op jit(solution)/shard_map/ppermute | solution.py:291
  7.7 5.3 %collective-permute-start.1 = (f32[16,1024]{1,0:T(8,128)S(1)}, f32[16,1024]{1,0:T(8,128)S(1)}, u32[]{:S(2)}, u32[]{:S(2)}) collective-permute-start(f32[16,1024]{1,0:T(8,128)S(1)} %bitcast_add_fusion.1), channel_id=1, source_target_pairs={{0,2},{1,3},{2,0},{3,1},{4,6},{5,7},{6,4},{7,5},{8,10},{9,11},{10,... | collective-permute-start | bytes 196616 | tf_op jit(solution)/shard_map/ppermute | solution.py:291
  13.1 4.3 %collective-permute-start.2 = (f32[16,1024]{1,0:T(8,128)S(1)}, f32[16,1024]{1,0:T(8,128)S(1)}, u32[]{:S(2)}, u32[]{:S(2)}) collective-permute-start(f32[16,1024]{1,0:T(8,128)S(1)} %add.89), channel_id=1, source_target_pairs={{0,4},{1,5},{2,6},{3,7},{4,0},{5,1},{6,2},{7,3},{8,12},{9,13},{10,... | collective-permute-start | bytes 196616 | tf_op jit(solution)/shard_map/ppermute | solution.py:291
  17.4 5.2 %collective-permute-start.3 = (f32[16,1024]{1,0:T(8,128)S(1)}, f32[16,1024]{1,0:T(8,128)S(1)}, u32[]{:S(2)}, u32[]{:S(2)}) collective-permute-start(f32[16,1024]{1,0:T(8,128)S(1)} %add.90), channel_id=1, source_target_pairs={{0,8},{1,9},{2,10},{3,11},{4,12},{5,13},{6,14},{7,15},{8,0},{9,1},... | collective-permute-start | bytes 196616 | tf_op jit(solution)/shard_map/ppermute | solution.py:291
  22.7 1.3 %collective-permute-start.4 = (f32[16,1024]{1,0:T(8,128)S(1)}, f32[16,1024]{1,0:T(8,128)S(1)}, u32[]{:S(2)}, u32[]{:S(2)}) collective-permute-start(f32[16,1024]{1,0:T(8,128)S(1)} %add.91), channel_id=1, source_target_pairs={{0,1},{1,0},{2,3},{3,2},{4,5},{5,4},{6,7},{7,6},{8,9},{9,8},{10,11... | collective-permute-start | bytes 196616 | tf_op jit(solution)/shard_map/ppermute | solution.py:291
  33.1 4.3 %collective-permute-start.7 = (bf16[768,512]{1,0:T(8,128)(2,1)S(1)}, bf16[768,512]{1,0:T(8,128)(2,1)S(1)}, u32[]{:S(2)}, u32[]{:S(2)}) collective-permute-start(bf16[768,512]{1,0:T(8,128)(2,1)S(1)} %get-tuple-element.29), channel_id=1, source_target_pairs={{0,1},{1,0},{2,3},{3,2},{4,5},{5,4},{6,7},{7,6},{8,9},{9,8},{10,11... | collective-permute-start | bytes 2359304 | tf_op jit(solution)/shard_map/ppermute | solution.py:291
  33.3 2.2 %collective-permute-start.5 = (f32[16,1152]{1,0:T(8,128)S(1)}, f32[16,1152]{1,0:T(8,128)S(1)}, u32[]{:S(2)}, u32[]{:S(2)}) collective-permute-start(f32[16,1152]{1,0:T(8,128)S(1)} %select_bitcast_fusion), channel_id=1, source_target_pairs={{0,1},{1,0},{2,3},{3,2},{4,5},{5,4},{6,7},{7,6},{8,9},{9,8},{10,11... | collective-permute-start | bytes 221192 | tf_op jit(solution)/shard_map/ppermute | solution.py:291
  35.5 4.5 %collective-permute-start.6 = (f32[16,1152]{1,0:T(8,128)S(1)}, f32[16,1152]{1,0:T(8,128)S(1)}, u32[]{:S(2)}, u32[]{:S(2)}) collective-permute-start(f32[16,1152]{1,0:T(8,128)S(1)} %bitcast_add_fusion), channel_id=1, source_target_pairs={{0,2},{1,3},{2,0},{3,1},{4,6},{5,7},{6,4},{7,5},{8,10},{9,11},{10,... | collective-permute-start | bytes 221192 | tf_op jit(solution)/shard_map/ppermute | solution.py:291
  37.8 11.0 %collective-permute-start.10 = (bf16[384,512]{1,0:T(8,128)(2,1)S(1)}, bf16[384,512]{1,0:T(8,128)(2,1)S(1)}, u32[]{:S(2)}, u32[]{:S(2)}) collective-permute-start(bf16[384,512]{1,0:T(8,128)(2,1)S(1)} %select_convert_fusion.1), channel_id=1, source_target_pairs={{0,2},{1,3},{2,0},{3,1},{4,6},{5,7},{6,4},{7,5},{8,10},{9,11},{10,... | collective-permute-start | bytes 1179656 | tf_op jit(solution)/shard_map/ppermute | solution.py:291
  40.1 4.4 %collective-permute-start.8 = (f32[16,1152]{1,0:T(8,128)S(1)}, f32[16,1152]{1,0:T(8,128)S(1)}, u32[]{:S(2)}, u32[]{:S(2)}) collective-permute-start(f32[16,1152]{1,0:T(8,128)S(1)} %pad_add_fusion.1), channel_id=1, source_target_pairs={{0,4},{1,5},{2,6},{3,7},{4,0},{5,1},{6,2},{7,3},{8,12},{9,13},{10,... | collective-permute-start | bytes 221192 | tf_op jit(solution)/shard_map/ppermute | solution.py:291
  44.5 5.3 %collective-permute-start.9 = (f32[16,1152]{1,0:T(8,128)S(1)}, f32[16,1152]{1,0:T(8,128)S(1)}, u32[]{:S(2)}, u32[]{:S(2)}) collective-permute-start(f32[16,1152]{1,0:T(8,128)S(1)} %add.96), channel_id=1, source_target_pairs={{0,8},{1,9},{2,10},{3,11},{4,12},{5,13},{6,14},{7,15},{8,0},{9,1},... | collective-permute-start | bytes 221192 | tf_op jit(solution)/shard_map/ppermute | solution.py:291
  49.8 2.2 %collective-permute-start.11 = (f32[16,1152]{1,0:T(8,128)S(1)}, f32[16,1152]{1,0:T(8,128)S(1)}, u32[]{:S(2)}, u32[]{:S(2)}) collective-permute-start(f32[16,1152]{1,0:T(8,128)S(1)} %pad_add_fusion), channel_id=1, source_target_pairs={{0,1},{1,0},{2,3},{3,2},{4,5},{5,4},{6,7},{7,6},{8,9},{9,8},{10,11... | collective-permute-start | bytes 221192 | tf_op jit(solution)/shard_map/ppermute | solution.py:291
  50.0 8.5 %collective-permute-start.12 = (bf16[192,512]{1,0:T(8,128)(2,1)S(1)}, bf16[192,512]{1,0:T(8,128)(2,1)S(1)}, u32[]{:S(2)}, u32[]{:S(2)}) collective-permute-start(bf16[192,512]{1,0:T(8,128)(2,1)S(1)} %select_convert_fusion.3), channel_id=1, source_target_pairs={{0,4},{1,5},{2,6},{3,7},{4,0},{5,1},{6,2},{7,3},{8,12},{9,13},{10,... | collective-permute-start | bytes 589832 | tf_op jit(solution)/shard_map/ppermute | solution.py:291
  58.7 2.0 %collective-permute-start.13 = (bf16[256,1024]{1,0:T(8,128)(2,1)S(1)}, bf16[256,1024]{1,0:T(8,128)(2,1)S(1)}, u32[]{:S(2)}, u32[]{:S(2)}) collective-permute-start(bf16[256,1024]{1,0:T(8,128)(2,1)S(1)} %fusion), channel_id=1, source_target_pairs={{0,1},{1,0},{2,3},{3,2},{4,5},{5,4},{6,7},{7,6},{8,9},{9,8},{10,11... | collective-permute-start | bytes 1572872 | tf_op jit(solution)/shard_map/ppermute | solution.py:291
  61.0 9.0 %collective-permute-start.14 = (bf16[128,1024]{1,0:T(8,128)(2,1)S(1)}, bf16[128,1024]{1,0:T(8,128)(2,1)S(1)}, u32[]{:S(2)}, u32[]{:S(2)}) collective-permute-start(bf16[128,1024]{1,0:T(8,128)(2,1)S(1)} %select_convert_fusion.2), channel_id=1, source_target_pairs={{0,2},{1,3},{2,0},{3,1},{4,6},{5,7},{6,4},{7,5},{8,10},{9,11},{10,... | collective-permute-start | bytes 786440 | tf_op jit(solution)/shard_map/ppermute | solution.py:291
  63.4 12.5 %collective-permute-start.17 = (bf16[192,512]{1,0:T(8,128)(2,1)S(1)}, bf16[192,512]{1,0:T(8,128)(2,1)S(1)}, u32[]{:S(2)}, u32[]{:S(2)}) collective-permute-start(bf16[192,512]{1,0:T(8,128)(2,1)S(1)} %get-tuple-element.36), channel_id=1, source_target_pairs={{0,8},{1,9},{2,10},{3,11},{4,12},{5,13},{6,14},{7,15},{8,0},{9,1},... | collective-permute-start | bytes 589832 | tf_op jit(solution)/shard_map/ppermute | solution.py:291
  70.2 8.4 %collective-permute-start.15 = (bf16[64,1024]{1,0:T(8,128)(2,1)S(1)}, bf16[64,1024]{1,0:T(8,128)(2,1)S(1)}, u32[]{:S(2)}, u32[]{:S(2)}) collective-permute-start(bf16[64,1024]{1,0:T(8,128)(2,1)S(1)} %select_convert_fusion.4), channel_id=1, source_target_pairs={{0,4},{1,5},{2,6},{3,7},{4,0},{5,1},{6,2},{7,3},{8,12},{9,13},{10,... | collective-permute-start | bytes 393224 | tf_op jit(solution)/shard_map/ppermute | solution.py:291
  75.9 8.0 %collective-permute-start.18 = (bf16[192,512]{1,0:T(8,128)(2,1)S(1)}, bf16[192,512]{1,0:T(8,128)(2,1)S(1)}, u32[]{:S(2)}, u32[]{:S(2)}) collective-permute-start(bf16[192,512]{1,0:T(8,128)(2,1)S(1)} %fusion.1), channel_id=1, source_target_pairs={{0,4},{1,5},{2,6},{3,7},{4,0},{5,1},{6,2},{7,3},{8,12},{9,13},{10,... | collective-permute-start | bytes 589832 | tf_op jit(solution)/shard_map/ppermute | solution.py:291
  78.7 9.1 %collective-permute-start.16 = (bf16[64,1024]{1,0:T(8,128)(2,1)S(1)}, bf16[64,1024]{1,0:T(8,128)(2,1)S(1)}, u32[]{:S(2)}, u32[]{:S(2)}) collective-permute-start(bf16[64,1024]{1,0:T(8,128)(2,1)S(1)} %get-tuple-element.38), channel_id=1, source_target_pairs={{0,8},{1,9},{2,10},{3,11},{4,12},{5,13},{6,14},{7,15},{8,0},{9,1},... | collective-permute-start | bytes 393224 | tf_op jit(solution)/shard_map/ppermute | solution.py:291
  84.0 9.0 %collective-permute-start.20 = (bf16[384,512]{1,0:T(8,128)(2,1)S(1)}, bf16[384,512]{1,0:T(8,128)(2,1)S(1)}, u32[]{:S(2)}, u32[]{:S(2)}) collective-permute-start(bf16[384,512]{1,0:T(8,128)(2,1)S(1)} %maximum_add_fusion.1), channel_id=1, source_target_pairs={{0,2},{1,3},{2,0},{3,1},{4,6},{5,7},{6,4},{7,5},{8,10},{9,11},{10,... | collective-permute-start | bytes 1179656 | tf_op jit(solution)/shard_map/ppermute | solution.py:291
  87.8 5.0 %collective-permute-start.19 = (bf16[64,1024]{1,0:T(8,128)(2,1)S(1)}, bf16[64,1024]{1,0:T(8,128)(2,1)S(1)}, u32[]{:S(2)}, u32[]{:S(2)}) collective-permute-start(bf16[64,1024]{1,0:T(8,128)(2,1)S(1)} %fusion.2), channel_id=1, source_target_pairs={{0,4},{1,5},{2,6},{3,7},{4,0},{5,1},{6,2},{7,3},{8,12},{9,13},{10,... | collective-permute-start | bytes 393224 | tf_op jit(solution)/shard_map/ppermute | solution.py:291
  93.1 8.9 %collective-permute-start.22 = (bf16[768,512]{1,0:T(8,128)(2,1)S(1)}, bf16[768,512]{1,0:T(8,128)(2,1)S(1)}, u32[]{:S(2)}, u32[]{:S(2)}) collective-permute-start(bf16[768,512]{1,0:T(8,128)(2,1)S(1)} %pad_maximum_fusion), channel_id=1, source_target_pairs={{0,1},{1,0},{2,3},{3,2},{4,5},{5,4},{6,7},{7,6},{8,9},{9,8},{10,11... | collective-permute-start | bytes 2359304 | tf_op jit(solution)/shard_map/ppermute | solution.py:291
  93.2 8.8 %collective-permute-start.21 = (bf16[128,1024]{1,0:T(8,128)(2,1)S(1)}, bf16[128,1024]{1,0:T(8,128)(2,1)S(1)}, u32[]{:S(2)}, u32[]{:S(2)}) collective-permute-start(bf16[128,1024]{1,0:T(8,128)(2,1)S(1)} %maximum_add_fusion.2), channel_id=1, source_target_pairs={{0,2},{1,3},{2,0},{3,1},{4,6},{5,7},{6,4},{7,5},{8,10},{9,11},{10,... | collective-permute-start | bytes 786440 | tf_op jit(solution)/shard_map/ppermute | solution.py:291
  102.8 1.3 %copy-start.10 = (f32[1024,512]{1,0:T(8,128)}, f32[1024,512]{1,0:T(8,128)S(1)}, u32[]{:S(2)}) copy-start(f32[1024,512]{1,0:T(8,128)S(1)} %maximum_convert_fusion) | copy-start | bytes 6291460
  104.1 2.9 %collective-permute-start.23 = (bf16[256,1024]{1,0:T(8,128)(2,1)S(1)}, bf16[256,1024]{1,0:T(8,128)(2,1)S(1)}, u32[]{:S(2)}, u32[]{:S(2)}) collective-permute-start(bf16[256,1024]{1,0:T(8,128)(2,1)S(1)} %maximum_add_fusion), channel_id=1, source_target_pairs={{0,1},{1,0},{2,3},{3,2},{4,5},{5,4},{6,7},{7,6},{8,9},{9,8},{10,11... | collective-permute-start | bytes 1572872 | tf_op jit(solution)/shard_map/ppermute | solution.py:291

commit v4 on v3

--- a/solution.py
+++ b/solution.py
@@ -1,5 +1,4 @@
 import functools
-import math
 
 import jax
 import jax.numpy as jnp
@@ -247,6 +246,9 @@
     grad_ref,
     grad_gain_ref,
     grad_shift_ref,
+    grad_score_ref,
+    grad_cls_ref,
+    loss_ref,
 ):
 
     positions, tiles_all, emb_width = before_ref.shape
@@ -259,6 +261,17 @@
     constant = scale * shift_sums_ref[:, :emb_width] * (1.0 / pixel_count) - mean * slope
     grad_gain_ref[...] = jnp.sum(gain_sums_ref[:, :emb_width], axis=0, keepdims=True)
     grad_shift_ref[...] = jnp.sum(shift_sums_ref[:, :emb_width], axis=0, keepdims=True)
+    scores = grad_score_ref.shape[1] // EXTRA
+    for i in range(scores):
+        grad_score_ref[:, i * EXTRA : (i + 1) * EXTRA] = shift_sums_ref[i : i + 1, emb_width:]
+    loss_ref[...] = shift_sums_ref[scores : scores + 1, emb_width : emb_width + 1]
+    classes, hid_width = grad_cls_ref.shape
+    for c in range(classes):
+        for i in range(hid_width // EXTRA):
+            spot = c * (hid_width // EXTRA) + i
+            grad_cls_ref[c : c + 1, i * EXTRA : (i + 1) * EXTRA] = gain_sums_ref[
+                spot : spot + 1, emb_width:
+            ]
     every = jnp.concatenate([scale, offset, slope, constant], axis=1)
     for start in range(0, tiles_all, tiles):
         rows = pl.ds(start, tiles)
@@ -282,18 +295,56 @@
             grad_ref[...] += part
 
 
+def finish_kernel(
+    core_ref,
+    head_ref,
+    head_other_ref,
+    conv_ref,
+    conv_other_ref,
+    fc_out,
+    gate_out,
+    conv_out,
+    fc_ref,
+    gate_ref,
+    conv_wide_ref,
+    copied,
+):
+    core = core_ref[0, 0]
+    copies = []
+
+    def place(value, spot, wide_ref, out):
+        half = value.shape[0]
+        rows = pl.ds(pl.multiple_of(spot * half, half), half)
+        wide_ref[rows] = value.astype(f32)
+        copies.append(
+            pltpu.make_async_copy(wide_ref.at[rows], out.at[rows], copied.at[len(copies)])
+        )
+        copies[-1].start()
+
+    rows_fc = fc_ref.shape[0] // 2
+    for ref, spot in ((head_ref, core), (head_other_ref, 1 - core)):
+        place(ref[:rows_fc], spot, fc_ref, fc_out)
+        place(ref[rows_fc:], spot, gate_ref, gate_out)
+    for ref, spot in ((conv_ref, core), (conv_other_ref, 1 - core)):
+        place(ref[...], spot, conv_wide_ref, conv_out)
+    for c in copies:
+        c.wait()
+
+
 def round_low(x):
     return lax.reduce_precision(x, 8, 7)
 
 
-def swap(x, bit):
+def swap(x, *levels):
+    mask = sum(1 << level for level in levels)
     count = lax.axis_size("enc")
-    return lax.ppermute(x, "enc", [(i, i ^ (1 << bit)) for i in range(count)])
+    return lax.ppermute(x, "enc", [(i, i ^ mask) for i in range(count)])
 
 
 def wait_for(x, other):
-    corner = (other[:16, :128] * 0).astype(x.dtype)
-    return x + jnp.pad(corner, ((0, x.shape[0] - 16), (0, x.shape[1] - 128)))
+    rows = min(16, x.shape[0], other.shape[0])
+    corner = (other[:rows, :128] * 0).astype(x.dtype)
+    return x + jnp.pad(corner, ((0, x.shape[0] - rows), (0, x.shape[1] - 128)))
 
 
 class SmallSum:
@@ -304,6 +355,10 @@
 
     def hop(self, level):
         self.x += swap(self.x, level)
+
+    def cross(self, one, two):
+        x = self.x
+        self.x = (x + swap(x, one)) + (swap(x, two) + swap(x, one, two))
 
     def result(self):
         other = swap(self.x, 0)
@@ -386,7 +441,8 @@
         **settings(20, 6),
     )(work, assign, w_conv)
     total = SmallSum(sums, firsts)
-    for level in range(1, levels):
+    total.cross(1, 2)
+    for level in range(3, levels):
         total.hop(level)
     first, second = total.result()
 
@@ -425,24 +481,26 @@
         w_cls.T,
     )
     total = SmallSum(sums, firsts)
-    rows_fc = emb_width // 2
     head = LargeSum(keep + swap(send, 0).astype(f32), firsts)
-    total.hop(1)
+    total.cross(1, 2)
     total.x = wait_for(total.x, head.x)
     head.halve(1)
-    for level in range(2, levels):
+    for level in range(3, levels):
         total.hop(level)
     total.x = wait_for(total.x, head.x)
     shift_sums, gain_sums = total.result()
 
-    grad_conv, grad_gain, grad_shift = pl.pallas_call(
+    grad_conv, grad_gain, grad_shift, grad_score, grad_cls, loss = pl.pallas_call(
         functools.partial(back_kernel, cap_rows, pixel_count),
         in_specs=[vmem] * 10,
-        out_specs=[vmem] * 3,
+        out_specs=[vmem] * 6,
         out_shape=[
             jax.ShapeDtypeStruct((input_width, emb_width), f32),
             jax.ShapeDtypeStruct((1, emb_width), f32),
             jax.ShapeDtypeStruct((1, emb_width), f32),
+            jax.ShapeDtypeStruct((1, w_score.shape[0]), f32),
+            jax.ShapeDtypeStruct(w_cls.shape[::-1], f32),
+            jax.ShapeDtypeStruct((1, 1), f32),
         ],
         name="norm_back",
         **settings(20, 7),
@@ -467,23 +525,28 @@
     head.double(1)
     conv.x = wait_for(conv.x, head.x)
     conv.double(1)
-    low, high = head.pair(0)
-    grad_fc = jnp.concatenate([low[:rows_fc], high[:rows_fc]], axis=0).astype(f32)
-    grad_gate = jnp.concatenate([low[rows_fc:], high[rows_fc:]], axis=0).astype(f32)
-    conv.x = wait_for(conv.x, grad_fc)
-    conv.double(0)
-    grad_conv = conv.x.astype(f32)
-    scores = w_score.shape[0] // EXTRA
-    classes = math.prod(w_cls.shape) // EXTRA
+    head_other = swap(head.x, 0)
+    conv.x = wait_for(conv.x, head_other)
+    wide = [(emb_width, hid_width), (hid_width, hid_width), (input_width, emb_width)]
+    grad_fc, grad_gate, grad_conv = pl.pallas_call(
+        finish_kernel,
+        in_specs=[smem] + [vmem] * 4,
+        out_specs=[pl.BlockSpec(memory_space=pl.ANY)] * 3,
+        out_shape=[jax.ShapeDtypeStruct(shape, f32) for shape in wide],
+        scratch_shapes=[pltpu.VMEM(shape, f32) for shape in wide]
+        + [pltpu.SemaphoreType.DMA((6,))],
+        name="finish",
+        **settings(12, 3),
+    )(core, head.x, head_other, conv.x, swap(conv.x, 0))
     return (
-        shift_sums[scores, emb_width : emb_width + 1],
+        loss.reshape(1),
         grad_conv,
         grad_gain.reshape(emb_width),
         grad_shift.reshape(emb_width),
         grad_fc,
         grad_gate,
-        shift_sums[:scores, emb_width:].reshape(-1),
-        gain_sums[:classes, emb_width:].reshape(w_cls.shape[::-1]).T,
+        grad_score.reshape(-1),
+        grad_cls.T,
     )
 
 

time: 109 us -> 106 us (0.972)
  waiting for transfers between devices: 50.4 us -> 54.2 us
  other arithmetic: 5.26 us -> 1.91 us
  local copies, waits for them, and re-layouts: 5.25 us -> 2.14 us
  starting transfers between devices: 27.9 us -> 24.8 us
  Pallas kernels: 18.7 us -> 21.2 us
    ppermute x24 -> x26, waiting for transfers between devices: 50.4 us -> 54.2 us  [swap(): return lax.ppermute(x, 'enc', [(i, i ^ mask) for i in range(count)])]
    ppermute x24 -> x26, starting transfers between devices: 27.9 us -> 24.8 us  [swap(): return lax.ppermute(x, 'enc', [(i, i ^ mask) for i in range(count)])]
    convert_element_type x7 -> x3, other arithmetic: 2.97 us -> 0.01 us  [wait_for(): corner = (other[:rows, :128] * 0).astype(x.dtype)]
    pallas_call x0 -> x1, Pallas kernels: none -> 2.47 us  [local(): pl.pallas_call(finish_kernel, in_specs=[smem] + [vmem] * 4, out_specs=[pl...]
    unnamed x23 -> x21, local copies, waits for them, and re-layouts: 3.46 us -> 2.14 us
    reshape x2 -> x0, local copies, waits for them, and re-layouts: 1.17 us -> none  [the longest x1 0.6 us: local(): gain_sums[:classes, emb_width:].reshape(w_cls.shape[::-1])]
  transfers between devices with their start and end apart: 24 -> 26, of which waited for: 19 -> 21; matrix products, arithmetic and copies ran while one was open for 4% -> 1% of each run, Pallas kernels for 6% -> 6%
where the time goes in v4:
time: 106 us; the launch traced here: 105 us
  waiting for transfers between devices  54.2 us (51%)
  starting transfers between devices  24.8 us (23%)
  Pallas kernels  21.2 us (20%)
  local copies, waits for them, and re-layouts  2.14 us (2%)
  other arithmetic  1.91 us (2%)
  between operations  1.26 us (1%)
    ppermute x26, waiting for transfers between devices, swap(): return lax.ppermute(x, 'enc', [(i, i ^ mask) for i in range(count)])  54.2 us
    ppermute x26, starting transfers between devices, swap(): return lax.ppermute(x, 'enc', [(i, i ^ mask) for i in range(count)])  24.8 us
    pallas_call x1, Pallas kernels, local(): pl.pallas_call(functools.partial(head_kernel, cap_rows, pixel_count, slid...  9.01 us
    pallas_call x1, Pallas kernels, local(): pl.pallas_call(functools.partial(back_kernel, cap_rows, pixel_count), in_...  6.3 us
    pallas_call x1, Pallas kernels, local(): pl.pallas_call(functools.partial(conv_kernel, cap_rows), in_specs=[vmem]...  3.38 us
    pallas_call x1, Pallas kernels, local(): pl.pallas_call(finish_kernel, in_specs=[smem] + [vmem] * 4, out_specs=[pl...  2.47 us
    unnamed x21, local copies, waits for them, and re-layouts  2.14 us
  transfers between devices with their start and end apart: 26, of which 21 were waited for; matrix products, arithmetic and copies ran while one was open for 1% of the time, Pallas kernels for 6%

profile of v4, /device:TPU:0, one launch (start us, length us, event | category | flops | bytes accessed | tf_op | source)
XLA Modules:
  0.0 105.5 jit_solution(17863947312249625402)
XLA Ops:
  0.7 2.1 %copy.21 = bf16[512,4,512]{2,0,1:T(8,128)(2,1)S(1)} copy(bf16[512,4,512]{2,1,0:T(4,128)(2,1)} %param.11) | data formatting | bytes 4194304 | tf_op args[0]
  2.9 3.4 %conv_sums.1 = (f32[4,512,1024]{2,1,0:T(8,128)S(1)}, f32[2,16,1024]{2,1,0:T(8,128)S(1)}) custom-call(bf16[4,512,512]{2,1,0:T(8,128)(2,1)S(1)} %bitcast.21, s32[1,512]{1,0:T(1,128)S(1)} %copy-done.6, bf16[512,1024]{1,0:T(8,128)(2,1)S(1)} %copy-done), custom_call_target="tpu_custom_call" | custom-call | flops 6600000000 | bytes 8388608 | tf_op jit(solution)/shard_map/conv_sums/pallas_call | solution.py:432
  6.3 0.5 collective-permute-start
  6.8 0.9 collective-permute-done
  7.7 2.9 %collective-permute-start.1 = (f32[16,1024]{1,0:T(8,128)S(1)}, f32[16,1024]{1,0:T(8,128)S(1)}, u32[]{:S(2)}, u32[]{:S(2)}) collective-permute-start(f32[16,1024]{1,0:T(8,128)S(1)} %bitcast_add_fusion.1), channel_id=1, source_target_pairs={{0,2},{1,3},{2,0},{3,1},{4,6},{5,7},{6,4},{7,5},{8,10},{9,11},{10,... | collective-permute-start | bytes 196616 | tf_op jit(solution)/shard_map/ppermute | solution.py:341
  10.7 1.6 %collective-permute-start.2 = (f32[16,1024]{1,0:T(8,128)S(1)}, f32[16,1024]{1,0:T(8,128)S(1)}, u32[]{:S(2)}, u32[]{:S(2)}) collective-permute-start(f32[16,1024]{1,0:T(8,128)S(1)} %bitcast_add_fusion.1), channel_id=1, source_target_pairs={{0,4},{1,5},{2,6},{3,7},{4,0},{5,1},{6,2},{7,3},{8,12},{9,13},{10,... | collective-permute-start | bytes 196616 | tf_op jit(solution)/shard_map/ppermute | solution.py:341
  12.2 0.8 collective-permute-done.1
  13.1 2.4 %collective-permute-done.2 = f32[16,1024]{1,0:T(8,128)S(1)} collective-permute-done((f32[16,1024]{1,0:T(8,128)S(1)}, f32[16,1024]{1,0:T(8,128)S(1)}, u32[]{:S(2)}, u32[]{:S(2)}) %collective-permute-start.2) | collective-permute-done | bytes 65568 | tf_op jit(solution)/shard_map/ppermute | solution.py:341
  15.5 1.9 %collective-permute-done.3 = f32[16,1024]{1,0:T(8,128)S(1)} collective-permute-done((f32[16,1024]{1,0:T(8,128)S(1)}, f32[16,1024]{1,0:T(8,128)S(1)}, u32[]{:S(2)}, u32[]{:S(2)}) %collective-permute-start.3) | collective-permute-done | bytes 65568 | tf_op jit(solution)/shard_map/ppermute | solution.py:341
  17.4 2.7 %collective-permute-start.4 = (f32[16,1024]{1,0:T(8,128)S(1)}, f32[16,1024]{1,0:T(8,128)S(1)}, u32[]{:S(2)}, u32[]{:S(2)}) collective-permute-start(f32[16,1024]{1,0:T(8,128)S(1)} %add_add_fusion), channel_id=1, source_target_pairs={{0,8},{1,9},{2,10},{3,11},{4,12},{5,13},{6,14},{7,15},{8,0},{9,1},... | collective-permute-start | bytes 196616 | tf_op jit(solution)/shard_map/ppermute | solution.py:341
  20.1 3.2 %collective-permute-done.4 = f32[16,1024]{1,0:T(8,128)S(1)} collective-permute-done((f32[16,1024]{1,0:T(8,128)S(1)}, f32[16,1024]{1,0:T(8,128)S(1)}, u32[]{:S(2)}, u32[]{:S(2)}) %collective-permute-start.4) | collective-permute-done | bytes 65568 | tf_op jit(solution)/shard_map/ppermute | solution.py:341
  23.3 1.2 %collective-permute-done.5 = f32[16,1024]{1,0:T(8,128)S(1)} collective-permute-done((f32[16,1024]{1,0:T(8,128)S(1)}, f32[16,1024]{1,0:T(8,128)S(1)}, u32[]{:S(2)}, u32[]{:S(2)}) %collective-permute-start.5) | collective-permute-done | bytes 65568 | tf_op jit(solution)/shard_map/ppermute | solution.py:341
  24.7 9.0 %norm_head.1 = (bf16[768,512]{1,0:T(8,128)(2,1)S(1)}, f32[768,512]{1,0:T(8,128)S(1)}, bf16[512,1024]{1,0:T(8,128)(2,1)S(1)}, f32[2,16,1152]{2,1,0:T(8,128)S(1)}) custom-call(s32[1,4]{1,0:T(1,128)S(1)} %copy-done.8, s32[1,4]{1,0:T(1,128)S(1)} %copy-done.9, s32[1,1]{1,0:T(1,128)} %bitcast.core_ref, f32[4,512,1024]{2,1,0:T(8,128)S(1)} %get-tuple-element.29.before_ref, ...), custom_call_target="tpu_custom_call" | custom-call | flops 13200000000 | bytes 8388608 | tf_op jit(solution)/shard_map/norm_head/pallas_call | solution.py:450
  33.7 0.2 collective-permute-start.10
  33.9 0.4 collective-permute-start.6
  34.3 1.8 %collective-permute-done.6 = f32[16,1152]{1,0:T(8,128)S(1)} collective-permute-done((f32[16,1152]{1,0:T(8,128)S(1)}, f32[16,1152]{1,0:T(8,128)S(1)}, u32[]{:S(2)}, u32[]{:S(2)}) %collective-permute-start.6) | collective-permute-done | bytes 73760 | tf_op jit(solution)/shard_map/ppermute | solution.py:341
  36.1 0.7 collective-permute-start.7
  36.8 0.5 collective-permute-start.8
  37.2 2.4 %collective-permute-start.9 = (f32[16,1152]{1,0:T(8,128)S(1)}, f32[16,1152]{1,0:T(8,128)S(1)}, u32[]{:S(2)}, u32[]{:S(2)}) collective-permute-start(f32[16,1152]{1,0:T(8,128)S(1)} %bitcast_add_fusion), channel_id=1, source_target_pairs={{0,6},{1,7},{2,4},{3,5},{4,2},{5,3},{6,0},{7,1},{8,14},{9,15},{10,... | collective-permute-start | bytes 221192 | tf_op jit(solution)/shard_map/ppermute | solution.py:341
  39.7 0.3 convert_add_fusion
  40.0 0.7 collective-permute-start.12
  40.7 1.0 collective-permute-done.8
  41.7 1.7 %collective-permute-done.9 = f32[16,1152]{1,0:T(8,128)S(1)} collective-permute-done((f32[16,1152]{1,0:T(8,128)S(1)}, f32[16,1152]{1,0:T(8,128)S(1)}, u32[]{:S(2)}, u32[]{:S(2)}) %collective-permute-start.9) | collective-permute-done | bytes 73760 | tf_op jit(solution)/shard_map/ppermute | solution.py:341
  43.4 2.5 %collective-permute-start.11 = (f32[16,1152]{1,0:T(8,128)S(1)}, f32[16,1152]{1,0:T(8,128)S(1)}, u32[]{:S(2)}, u32[]{:S(2)}) collective-permute-start(f32[16,1152]{1,0:T(8,128)S(1)} %pad_add_fusion.1), channel_id=1, source_target_pairs={{0,8},{1,9},{2,10},{3,11},{4,12},{5,13},{6,14},{7,15},{8,0},{9,1},... | collective-permute-start | bytes 221192 | tf_op jit(solution)/shard_map/ppermute | solution.py:341
  45.8 5.5 %collective-permute-done.12 = bf16[384,512]{1,0:T(8,128)(2,1)S(1)} collective-permute-done((bf16[384,512]{1,0:T(8,128)(2,1)S(1)}, bf16[384,512]{1,0:T(8,128)(2,1)S(1)}, u32[]{:S(2)}, u32[]{:S(2)}) %collective-permute-start.12) | collective-permute-done | bytes 393248 | tf_op jit(solution)/shard_map/ppermute | solution.py:341
  51.3 0.2 convert_add_fusion.2
  51.7 0.9 collective-permute-start.14
  52.6 0.3 collective-permute-done.13
  52.9 6.3 %norm_back.1 = (f32[512,1024]{1,0:T(8,128)S(1)}, f32[1,1024]{1,0:T(1,128)}, f32[1,1024]{1,0:T(1,128)}, f32[1,256]{1,0:T(1,128)}, f32[2,512]{1,0:T(2,128)}, /*index=5*/f32[1,1]{1,0:T(1,128)}) custom-call(bf16[4,512,512]{2,1,0:T(8,128)(2,1)S(1)} %bitcast.22, f32[4,512,1024]{2,1,0:T(8,128)S(1)} %get-tuple-element.29.before_ref, ...), custom_call_target="tpu_custom_call" | custom-call | flops 7699999744 | bytes 8388608 | tf_op jit(solution)/shard_map/norm_back/pallas_call | solution.py:493
  59.5 0.2 collective-permute-start.16
  59.7 1.8 %collective-permute-done.16 = bf16[256,1024]{1,0:T(8,128)(2,1)S(1)} collective-permute-done((bf16[256,1024]{1,0:T(8,128)(2,1)S(1)}, bf16[256,1024]{1,0:T(8,128)(2,1)S(1)}, u32[]{:S(2)}, u32[]{:S(2)}) %collective-permute-start.16) | collective-permute-done | bytes 524320 | tf_op jit(solution)/shard_map/ppermute | solution.py:341
  61.4 0.3 convert_add_fusion.1
  61.8 0.9 collective-permute-start.17
  62.7 2.6 %collective-permute-start.15 = (bf16[192,512]{1,0:T(8,128)(2,1)S(1)}, bf16[192,512]{1,0:T(8,128)(2,1)S(1)}, u32[]{:S(2)}, u32[]{:S(2)}) collective-permute-start(bf16[192,512]{1,0:T(8,128)(2,1)S(1)} %get-tuple-element.50), channel_id=1, source_target_pairs={{0,8},{1,9},{2,10},{3,11},{4,12},{5,13},{6,14},{7,15},{8,0},{9,1},... | collective-permute-start | bytes 589832 | tf_op jit(solution)/shard_map/ppermute | solution.py:341
  65.3 4.9 %collective-permute-done.17 = bf16[128,1024]{1,0:T(8,128)(2,1)S(1)} collective-permute-done((bf16[128,1024]{1,0:T(8,128)(2,1)S(1)}, bf16[128,1024]{1,0:T(8,128)(2,1)S(1)}, u32[]{:S(2)}, u32[]{:S(2)}) %collective-permute-start.17) | collective-permute-done | bytes 262176 | tf_op jit(solution)/shard_map/ppermute | solution.py:341
  70.4 1.2 %collective-permute-start.19 = (bf16[64,1024]{1,0:T(8,128)(2,1)S(1)}, bf16[64,1024]{1,0:T(8,128)(2,1)S(1)}, u32[]{:S(2)}, u32[]{:S(2)}) collective-permute-start(bf16[64,1024]{1,0:T(8,128)(2,1)S(1)} %select_convert_fusion.4), channel_id=1, source_target_pairs={{0,4},{1,5},{2,6},{3,7},{4,0},{5,1},{6,2},{7,3},{8,12},{9,13},{10,... | collective-permute-start | bytes 393224 | tf_op jit(solution)/shard_map/ppermute | solution.py:341
  71.6 3.1 %collective-permute-done.15 = bf16[192,512]{1,0:T(8,128)(2,1)S(1)} collective-permute-done((bf16[192,512]{1,0:T(8,128)(2,1)S(1)}, bf16[192,512]{1,0:T(8,128)(2,1)S(1)}, u32[]{:S(2)}, u32[]{:S(2)}) %collective-permute-start.15) | collective-permute-done | bytes 196640 | tf_op jit(solution)/shard_map/ppermute | solution.py:341
  74.7 0.2 collective-permute-start.18
  74.9 2.6 %collective-permute-done.19 = bf16[64,1024]{1,0:T(8,128)(2,1)S(1)} collective-permute-done((bf16[64,1024]{1,0:T(8,128)(2,1)S(1)}, bf16[64,1024]{1,0:T(8,128)(2,1)S(1)}, u32[]{:S(2)}, u32[]{:S(2)}) %collective-permute-start.19) | collective-permute-done | bytes 131104 | tf_op jit(solution)/shard_map/ppermute | solution.py:341
  77.5 1.1 %collective-permute-start.22 = (bf16[64,1024]{1,0:T(8,128)(2,1)S(1)}, bf16[64,1024]{1,0:T(8,128)(2,1)S(1)}, u32[]{:S(2)}, u32[]{:S(2)}) collective-permute-start(bf16[64,1024]{1,0:T(8,128)(2,1)S(1)} %get-tuple-element.48), channel_id=1, source_target_pairs={{0,8},{1,9},{2,10},{3,11},{4,12},{5,13},{6,14},{7,15},{8,0},{9,1},... | collective-permute-start | bytes 393224 | tf_op jit(solution)/shard_map/ppermute | solution.py:341
  78.6 3.9 %collective-permute-done.18 = bf16[192,512]{1,0:T(8,128)(2,1)S(1)} collective-permute-done((bf16[192,512]{1,0:T(8,128)(2,1)S(1)}, bf16[192,512]{1,0:T(8,128)(2,1)S(1)}, u32[]{:S(2)}, u32[]{:S(2)}) %collective-permute-start.18) | collective-permute-done | bytes 196640 | tf_op jit(solution)/shard_map/ppermute | solution.py:341
  82.6 1.2 %collective-permute-start.20 = (bf16[384,512]{1,0:T(8,128)(2,1)S(1)}, bf16[384,512]{1,0:T(8,128)(2,1)S(1)}, u32[]{:S(2)}, u32[]{:S(2)}) collective-permute-start(bf16[384,512]{1,0:T(8,128)(2,1)S(1)} %maximum_add_fusion.1), channel_id=1, source_target_pairs={{0,2},{1,3},{2,0},{3,1},{4,6},{5,7},{6,4},{7,5},{8,10},{9,11},{10,... | collective-permute-start | bytes 1179656 | tf_op jit(solution)/shard_map/ppermute | solution.py:341
  83.8 2.8 %collective-permute-done.22 = bf16[64,1024]{1,0:T(8,128)(2,1)S(1)} collective-permute-done((bf16[64,1024]{1,0:T(8,128)(2,1)S(1)}, bf16[64,1024]{1,0:T(8,128)(2,1)S(1)}, u32[]{:S(2)}, u32[]{:S(2)}) %collective-permute-start.22) | collective-permute-done | bytes 131104 | tf_op jit(solution)/shard_map/ppermute | solution.py:341
  86.7 5.0 %collective-permute-done.23 = bf16[64,1024]{1,0:T(8,128)(2,1)S(1)} collective-permute-done((bf16[64,1024]{1,0:T(8,128)(2,1)S(1)}, bf16[64,1024]{1,0:T(8,128)(2,1)S(1)}, u32[]{:S(2)}, u32[]{:S(2)}) %collective-permute-start.23) | collective-permute-done | bytes 131104 | tf_op jit(solution)/shard_map/ppermute | solution.py:341
  92.0 1.2 %collective-permute-start.24 = (bf16[128,1024]{1,0:T(8,128)(2,1)S(1)}, bf16[128,1024]{1,0:T(8,128)(2,1)S(1)}, u32[]{:S(2)}, u32[]{:S(2)}) collective-permute-start(bf16[128,1024]{1,0:T(8,128)(2,1)S(1)} %maximum_add_fusion.2), channel_id=1, source_target_pairs={{0,2},{1,3},{2,0},{3,1},{4,6},{5,7},{6,4},{7,5},{8,10},{9,11},{10,... | collective-permute-start | bytes 786440 | tf_op jit(solution)/shard_map/ppermute | solution.py:341
  93.2 7.6 %collective-permute-done.24 = bf16[128,1024]{1,0:T(8,128)(2,1)S(1)} collective-permute-done((bf16[128,1024]{1,0:T(8,128)(2,1)S(1)}, bf16[128,1024]{1,0:T(8,128)(2,1)S(1)}, u32[]{:S(2)}, u32[]{:S(2)}) %collective-permute-start.24) | collective-permute-done | bytes 262176 | tf_op jit(solution)/shard_map/ppermute | solution.py:341
  101.0 1.9 %collective-permute-done.25.conv_other_ref = bf16[256,1024]{1,0:T(8,128)(2,1)S(1)} collective-permute-done((bf16[256,1024]{1,0:T(8,128)(2,1)S(1)}, bf16[256,1024]{1,0:T(8,128)(2,1)S(1)}, u32[]{:S(2)}, u32[]{:S(2)}) %collective-permute-start.25) | collective-permute-done | bytes 524320 | tf_op jit(solution)/shard_map/ppermute | solution.py:341
  102.9 2.5 %finish.1 = (f32[1024,512]{1,0:T(8,128)}, f32[512,512]{1,0:T(8,128)}, f32[512,1024]{1,0:T(8,128)}) custom-call(s32[1,1]{1,0:T(1,128)} %bitcast.core_ref, bf16[768,512]{1,0:T(8,128)(2,1)S(1)} %pad_maximum_fusion.head_ref, bf16[768,512]{1,0:T(8,128)(2,1)S(1)} %collective-permute-done.21.head_other_ref, bf16[256,1024]{1,0:T(8,128)(2,1)S(1)} %maximum_add_fusion.conv_ref, ...), custom_call_target="tpu_custom_call" | custom-call | flops 3300000000 | bytes 8388608 | tf_op jit(solution)/shard_map/finish/pallas_call | solution.py:531
  (68 shorter events, 1.7 us)
Async XLA Ops:
  0.6 2.1 %copy-start = (bf16[512,1024]{1,0:T(8,128)(2,1)S(1)}, bf16[512,1024]{1,0:T(8,128)(2,1)}, u32[]{:S(2)}) copy-start(bf16[512,1024]{1,0:T(8,128)(2,1)} %w_ref.1) | copy-start | bytes 3145732
  0.7 2.1 %copy-start.6 = (s32[1,512]{1,0:T(1,128)S(1)}, s32[1,512]{1,0:T(1,128)}, u32[]{:S(2)}) copy-start(s32[1,512]{1,0:T(1,128)} %assign_ref.5) | copy-start | bytes 6148
  2.8 21.8 %copy-start.1 = (bf16[1024,512]{1,0:T(8,128)(2,1)S(1)}, bf16[1024,512]{1,0:T(8,128)(2,1)}, u32[]{:S(2)}) copy-start(bf16[1024,512]{1,0:T(8,128)(2,1)} %w_fc_ref.1) | copy-start | bytes 3145732
  2.8 21.8 %copy-start.2 = (bf16[512,512]{1,0:T(8,128)(2,1)S(1)}, bf16[512,512]{1,0:T(8,128)(2,1)}, u32[]{:S(2)}) copy-start(bf16[512,512]{1,0:T(8,128)(2,1)} %w_gate_ref.1) | copy-start | bytes 1572868
  2.8 21.8 %copy-start.3 = (f32[512,2]{0,1:T(2,128)S(1)}, f32[512,2]{0,1:T(2,128)}, u32[]{:S(2)}) copy-start(f32[512,2]{0,1:T(2,128)} %param.21) | copy-start | bytes 12292
  2.8 21.8 %copy-start.4 = (f32[1024]{0:T(1024)S(1)}, f32[1024]{0:T(1024)}, u32[]{:S(2)}) copy-start(f32[1024]{0:T(1024)} %param.16) | copy-start | bytes 12292
  2.8 21.8 %copy-start.5 = (f32[1024]{0:T(1024)S(1)}, f32[1024]{0:T(1024)}, u32[]{:S(2)}) copy-start(f32[1024]{0:T(1024)} %param.17) | copy-start | bytes 12292
  2.8 21.8 %copy-start.7 = (f32[256]{0:T(256)S(1)}, f32[256]{0:T(256)}, u32[]{:S(2)}) copy-start(f32[256]{0:T(256)} %param.20) | copy-start | bytes 3076
  2.8 21.8 %copy-start.8 = (s32[1,4]{1,0:T(1,128)S(1)}, s32[1,4]{1,0:T(1,128)}, u32[]{:S(2)}) copy-start(s32[1,4]{1,0:T(1,128)} %counts_ref.1) | copy-start | bytes 52
  2.9 21.8 %copy-start.9 = (s32[1,4]{1,0:T(1,128)S(1)}, s32[1,4]{1,0:T(1,128)}, u32[]{:S(2)}) copy-start(s32[1,4]{1,0:T(1,128)} %labels_ref.1) | copy-start | bytes 52
  6.3 1.4 %collective-permute-start = (f32[16,1024]{1,0:T(8,128)S(1)}, f32[16,1024]{1,0:T(8,128)S(1)}, u32[]{:S(2)}, u32[]{:S(2)}) collective-permute-start(f32[16,1024]{1,0:T(8,128)S(1)} %select_bitcast_fusion.1), channel_id=1, source_target_pairs={{0,1},{1,0},{2,3},{3,2},{4,5},{5,4},{6,7},{7,6},{8,9},{9,8},{10,11... | collective-permute-start | bytes 196616 | tf_op jit(solution)/shard_map/ppermute | solution.py:341
  7.7 5.3 %collective-permute-start.1 = (f32[16,1024]{1,0:T(8,128)S(1)}, f32[16,1024]{1,0:T(8,128)S(1)}, u32[]{:S(2)}, u32[]{:S(2)}) collective-permute-start(f32[16,1024]{1,0:T(8,128)S(1)} %bitcast_add_fusion.1), channel_id=1, source_target_pairs={{0,2},{1,3},{2,0},{3,1},{4,6},{5,7},{6,4},{7,5},{8,10},{9,11},{10,... | collective-permute-start | bytes 196616 | tf_op jit(solution)/shard_map/ppermute | solution.py:341
  10.7 4.8 %collective-permute-start.2 = (f32[16,1024]{1,0:T(8,128)S(1)}, f32[16,1024]{1,0:T(8,128)S(1)}, u32[]{:S(2)}, u32[]{:S(2)}) collective-permute-start(f32[16,1024]{1,0:T(8,128)S(1)} %bitcast_add_fusion.1), channel_id=1, source_target_pairs={{0,4},{1,5},{2,6},{3,7},{4,0},{5,1},{6,2},{7,3},{8,12},{9,13},{10,... | collective-permute-start | bytes 196616 | tf_op jit(solution)/shard_map/ppermute | solution.py:341
  12.2 5.2 %collective-permute-start.3 = (f32[16,1024]{1,0:T(8,128)S(1)}, f32[16,1024]{1,0:T(8,128)S(1)}, u32[]{:S(2)}, u32[]{:S(2)}) collective-permute-start(f32[16,1024]{1,0:T(8,128)S(1)} %bitcast_add_fusion.1), channel_id=1, source_target_pairs={{0,6},{1,7},{2,4},{3,5},{4,2},{5,3},{6,0},{7,1},{8,14},{9,15},{10,... | collective-permute-start | bytes 196616 | tf_op jit(solution)/shard_map/ppermute | solution.py:341
  17.4 5.8 %collective-permute-start.4 = (f32[16,1024]{1,0:T(8,128)S(1)}, f32[16,1024]{1,0:T(8,128)S(1)}, u32[]{:S(2)}, u32[]{:S(2)}) collective-permute-start(f32[16,1024]{1,0:T(8,128)S(1)} %add_add_fusion), channel_id=1, source_target_pairs={{0,8},{1,9},{2,10},{3,11},{4,12},{5,13},{6,14},{7,15},{8,0},{9,1},... | collective-permute-start | bytes 196616 | tf_op jit(solution)/shard_map/ppermute | solution.py:341
  23.2 1.3 %collective-permute-start.5 = (f32[16,1024]{1,0:T(8,128)S(1)}, f32[16,1024]{1,0:T(8,128)S(1)}, u32[]{:S(2)}, u32[]{:S(2)}) collective-permute-start(f32[16,1024]{1,0:T(8,128)S(1)} %add.98), channel_id=1, source_target_pairs={{0,1},{1,0},{2,3},{3,2},{4,5},{5,4},{6,7},{7,6},{8,9},{9,8},{10,11... | collective-permute-start | bytes 196616 | tf_op jit(solution)/shard_map/ppermute | solution.py:341
  33.7 6.0 %collective-permute-start.10 = (bf16[768,512]{1,0:T(8,128)(2,1)S(1)}, bf16[768,512]{1,0:T(8,128)(2,1)S(1)}, u32[]{:S(2)}, u32[]{:S(2)}) collective-permute-start(bf16[768,512]{1,0:T(8,128)(2,1)S(1)} %get-tuple-element.36), channel_id=1, source_target_pairs={{0,1},{1,0},{2,3},{3,2},{4,5},{5,4},{6,7},{7,6},{8,9},{9,8},{10,11... | collective-permute-start | bytes 2359304 | tf_op jit(solution)/shard_map/ppermute | solution.py:341
  33.9 2.2 %collective-permute-start.6 = (f32[16,1152]{1,0:T(8,128)S(1)}, f32[16,1152]{1,0:T(8,128)S(1)}, u32[]{:S(2)}, u32[]{:S(2)}) collective-permute-start(f32[16,1152]{1,0:T(8,128)S(1)} %select_bitcast_fusion), channel_id=1, source_target_pairs={{0,1},{1,0},{2,3},{3,2},{4,5},{5,4},{6,7},{7,6},{8,9},{9,8},{10,11... | collective-permute-start | bytes 221192 | tf_op jit(solution)/shard_map/ppermute | solution.py:341
  36.1 4.6 %collective-permute-start.7 = (f32[16,1152]{1,0:T(8,128)S(1)}, f32[16,1152]{1,0:T(8,128)S(1)}, u32[]{:S(2)}, u32[]{:S(2)}) collective-permute-start(f32[16,1152]{1,0:T(8,128)S(1)} %bitcast_add_fusion), channel_id=1, source_target_pairs={{0,2},{1,3},{2,0},{3,1},{4,6},{5,7},{6,4},{7,5},{8,10},{9,11},{10,... | collective-permute-start | bytes 221192 | tf_op jit(solution)/shard_map/ppermute | solution.py:341
  36.8 4.9 %collective-permute-start.8 = (f32[16,1152]{1,0:T(8,128)S(1)}, f32[16,1152]{1,0:T(8,128)S(1)}, u32[]{:S(2)}, u32[]{:S(2)}) collective-permute-start(f32[16,1152]{1,0:T(8,128)S(1)} %bitcast_add_fusion), channel_id=1, source_target_pairs={{0,4},{1,5},{2,6},{3,7},{4,0},{5,1},{6,2},{7,3},{8,12},{9,13},{10,... | collective-permute-start | bytes 221192 | tf_op jit(solution)/shard_map/ppermute | solution.py:341
  37.2 6.1 %collective-permute-start.9 = (f32[16,1152]{1,0:T(8,128)S(1)}, f32[16,1152]{1,0:T(8,128)S(1)}, u32[]{:S(2)}, u32[]{:S(2)}) collective-permute-start(f32[16,1152]{1,0:T(8,128)S(1)} %bitcast_add_fusion), channel_id=1, source_target_pairs={{0,6},{1,7},{2,4},{3,5},{4,2},{5,3},{6,0},{7,1},{8,14},{9,15},{10,... | collective-permute-start | bytes 221192 | tf_op jit(solution)/shard_map/ppermute | solution.py:341
  40.0 11.3 %collective-permute-start.12 = (bf16[384,512]{1,0:T(8,128)(2,1)S(1)}, bf16[384,512]{1,0:T(8,128)(2,1)S(1)}, u32[]{:S(2)}, u32[]{:S(2)}) collective-permute-start(bf16[384,512]{1,0:T(8,128)(2,1)S(1)} %select_convert_fusion.1), channel_id=1, source_target_pairs={{0,2},{1,3},{2,0},{3,1},{4,6},{5,7},{6,4},{7,5},{8,10},{9,11},{10,... | collective-permute-start | bytes 1179656 | tf_op jit(solution)/shard_map/ppermute | solution.py:341
  43.4 8.1 %collective-permute-start.11 = (f32[16,1152]{1,0:T(8,128)S(1)}, f32[16,1152]{1,0:T(8,128)S(1)}, u32[]{:S(2)}, u32[]{:S(2)}) collective-permute-start(f32[16,1152]{1,0:T(8,128)S(1)} %pad_add_fusion.1), channel_id=1, source_target_pairs={{0,8},{1,9},{2,10},{3,11},{4,12},{5,13},{6,14},{7,15},{8,0},{9,1},... | collective-permute-start | bytes 221192 | tf_op jit(solution)/shard_map/ppermute | solution.py:341
  51.5 1.3 %collective-permute-start.13 = (f32[16,1152]{1,0:T(8,128)S(1)}, f32[16,1152]{1,0:T(8,128)S(1)}, u32[]{:S(2)}, u32[]{:S(2)}) collective-permute-start(f32[16,1152]{1,0:T(8,128)S(1)} %pad_add_fusion), channel_id=1, source_target_pairs={{0,1},{1,0},{2,3},{3,2},{4,5},{5,4},{6,7},{7,6},{8,9},{9,8},{10,11... | collective-permute-start | bytes 221192 | tf_op jit(solution)/shard_map/ppermute | solution.py:341
  51.7 7.5 %collective-permute-start.14 = (bf16[192,512]{1,0:T(8,128)(2,1)S(1)}, bf16[192,512]{1,0:T(8,128)(2,1)S(1)}, u32[]{:S(2)}, u32[]{:S(2)}) collective-permute-start(bf16[192,512]{1,0:T(8,128)(2,1)S(1)} %select_convert_fusion.3), channel_id=1, source_target_pairs={{0,4},{1,5},{2,6},{3,7},{4,0},{5,1},{6,2},{7,3},{8,12},{9,13},{10,... | collective-permute-start | bytes 589832 | tf_op jit(solution)/shard_map/ppermute | solution.py:341
  59.5 2.0 %collective-permute-start.16 = (bf16[256,1024]{1,0:T(8,128)(2,1)S(1)}, bf16[256,1024]{1,0:T(8,128)(2,1)S(1)}, u32[]{:S(2)}, u32[]{:S(2)}) collective-permute-start(bf16[256,1024]{1,0:T(8,128)(2,1)S(1)} %fusion), channel_id=1, source_target_pairs={{0,1},{1,0},{2,3},{3,2},{4,5},{5,4},{6,7},{7,6},{8,9},{9,8},{10,11... | collective-permute-start | bytes 1572872 | tf_op jit(solution)/shard_map/ppermute | solution.py:341
  61.8 8.4 %collective-permute-start.17 = (bf16[128,1024]{1,0:T(8,128)(2,1)S(1)}, bf16[128,1024]{1,0:T(8,128)(2,1)S(1)}, u32[]{:S(2)}, u32[]{:S(2)}) collective-permute-start(bf16[128,1024]{1,0:T(8,128)(2,1)S(1)} %select_convert_fusion.2), channel_id=1, source_target_pairs={{0,2},{1,3},{2,0},{3,1},{4,6},{5,7},{6,4},{7,5},{8,10},{9,11},{10,... | collective-permute-start | bytes 786440 | tf_op jit(solution)/shard_map/ppermute | solution.py:341
  62.7 12.0 %collective-permute-start.15 = (bf16[192,512]{1,0:T(8,128)(2,1)S(1)}, bf16[192,512]{1,0:T(8,128)(2,1)S(1)}, u32[]{:S(2)}, u32[]{:S(2)}) collective-permute-start(bf16[192,512]{1,0:T(8,128)(2,1)S(1)} %get-tuple-element.50), channel_id=1, source_target_pairs={{0,8},{1,9},{2,10},{3,11},{4,12},{5,13},{6,14},{7,15},{8,0},{9,1},... | collective-permute-start | bytes 589832 | tf_op jit(solution)/shard_map/ppermute | solution.py:341
  70.4 7.1 %collective-permute-start.19 = (bf16[64,1024]{1,0:T(8,128)(2,1)S(1)}, bf16[64,1024]{1,0:T(8,128)(2,1)S(1)}, u32[]{:S(2)}, u32[]{:S(2)}) collective-permute-start(bf16[64,1024]{1,0:T(8,128)(2,1)S(1)} %select_convert_fusion.4), channel_id=1, source_target_pairs={{0,4},{1,5},{2,6},{3,7},{4,0},{5,1},{6,2},{7,3},{8,12},{9,13},{10,... | collective-permute-start | bytes 393224 | tf_op jit(solution)/shard_map/ppermute | solution.py:341
  74.7 7.8 %collective-permute-start.18 = (bf16[192,512]{1,0:T(8,128)(2,1)S(1)}, bf16[192,512]{1,0:T(8,128)(2,1)S(1)}, u32[]{:S(2)}, u32[]{:S(2)}) collective-permute-start(bf16[192,512]{1,0:T(8,128)(2,1)S(1)} %fusion.1), channel_id=1, source_target_pairs={{0,4},{1,5},{2,6},{3,7},{4,0},{5,1},{6,2},{7,3},{8,12},{9,13},{10,... | collective-permute-start | bytes 589832 | tf_op jit(solution)/shard_map/ppermute | solution.py:341
  77.5 9.1 %collective-permute-start.22 = (bf16[64,1024]{1,0:T(8,128)(2,1)S(1)}, bf16[64,1024]{1,0:T(8,128)(2,1)S(1)}, u32[]{:S(2)}, u32[]{:S(2)}) collective-permute-start(bf16[64,1024]{1,0:T(8,128)(2,1)S(1)} %get-tuple-element.48), channel_id=1, source_target_pairs={{0,8},{1,9},{2,10},{3,11},{4,12},{5,13},{6,14},{7,15},{8,0},{9,1},... | collective-permute-start | bytes 393224 | tf_op jit(solution)/shard_map/ppermute | solution.py:341
  82.6 9.2 %collective-permute-start.20 = (bf16[384,512]{1,0:T(8,128)(2,1)S(1)}, bf16[384,512]{1,0:T(8,128)(2,1)S(1)}, u32[]{:S(2)}, u32[]{:S(2)}) collective-permute-start(bf16[384,512]{1,0:T(8,128)(2,1)S(1)} %maximum_add_fusion.1), channel_id=1, source_target_pairs={{0,2},{1,3},{2,0},{3,1},{4,6},{5,7},{6,4},{7,5},{8,10},{9,11},{10,... | collective-permute-start | bytes 1179656 | tf_op jit(solution)/shard_map/ppermute | solution.py:341
  86.6 5.0 %collective-permute-start.23 = (bf16[64,1024]{1,0:T(8,128)(2,1)S(1)}, bf16[64,1024]{1,0:T(8,128)(2,1)S(1)}, u32[]{:S(2)}, u32[]{:S(2)}) collective-permute-start(bf16[64,1024]{1,0:T(8,128)(2,1)S(1)} %fusion.2), channel_id=1, source_target_pairs={{0,4},{1,5},{2,6},{3,7},{4,0},{5,1},{6,2},{7,3},{8,12},{9,13},{10,... | collective-permute-start | bytes 393224 | tf_op jit(solution)/shard_map/ppermute | solution.py:341
  91.9 8.9 %collective-permute-start.21 = (bf16[768,512]{1,0:T(8,128)(2,1)S(1)}, bf16[768,512]{1,0:T(8,128)(2,1)S(1)}, u32[]{:S(2)}, u32[]{:S(2)}) collective-permute-start(bf16[768,512]{1,0:T(8,128)(2,1)S(1)} %pad_maximum_fusion.head_ref), channel_id=1, source_target_pairs={{0,1},{1,0},{2,3},{3,2},{4,5},{5,4},{6,7},{7,6},{8,9},{9,8},{10,11... | collective-permute-start | bytes 2359304 | tf_op jit(solution)/shard_map/ppermute | solution.py:341
  92.0 8.8 %collective-permute-start.24 = (bf16[128,1024]{1,0:T(8,128)(2,1)S(1)}, bf16[128,1024]{1,0:T(8,128)(2,1)S(1)}, u32[]{:S(2)}, u32[]{:S(2)}) collective-permute-start(bf16[128,1024]{1,0:T(8,128)(2,1)S(1)} %maximum_add_fusion.2), channel_id=1, source_target_pairs={{0,2},{1,3},{2,0},{3,1},{4,6},{5,7},{6,4},{7,5},{8,10},{9,11},{10,... | collective-permute-start | bytes 786440 | tf_op jit(solution)/shard_map/ppermute | solution.py:341
  100.9 2.0 %collective-permute-start.25 = (bf16[256,1024]{1,0:T(8,128)(2,1)S(1)}, bf16[256,1024]{1,0:T(8,128)(2,1)S(1)}, u32[]{:S(2)}, u32[]{:S(2)}) collective-permute-start(bf16[256,1024]{1,0:T(8,128)(2,1)S(1)} %maximum_add_fusion.conv_ref), channel_id=1, source_target_pairs={{0,1},{1,0},{2,3},{3,2},{4,5},{5,4},{6,7},{7,6},{8,9},{9,8},{10,11... | collective-permute-start | bytes 1572872 | tf_op jit(solution)/shard_map/ppermute | solution.py:341

commit v5 on v4

--- a/solution.py
+++ b/solution.py
@@ -9,7 +9,7 @@
 
 epsilon = 1e-05
 f32, bf16 = jnp.float32, jnp.bfloat16
-CHUNK_CONV, CHUNK_HEAD, CHUNK_BACK = 128, 128, 128
+CHUNK_CONV, CHUNK_HEAD, CHUNK_BACK = 256, 256, 128
 EXTRA = 128
 
 
@@ -481,11 +481,11 @@
         w_cls.T,
     )
     total = SmallSum(sums, firsts)
-    head = LargeSum(keep + swap(send, 0).astype(f32), firsts)
-    total.cross(1, 2)
+    head = LargeSum(keep + swap(wait_for(send, total.x), 0).astype(f32), firsts)
+    total.hop(1)
     total.x = wait_for(total.x, head.x)
     head.halve(1)
-    for level in range(3, levels):
+    for level in range(2, levels):
         total.hop(level)
     total.x = wait_for(total.x, head.x)
     shift_sums, gain_sums = total.result()

time: 106 us -> 104 us (0.981)
  waiting for transfers between devices: 54.2 us -> 52.1 us
    ppermute x26 -> x25, waiting for transfers between devices: 54.2 us -> 52.1 us  [swap(): return lax.ppermute(x, 'enc', [(i, i ^ mask) for i in range(count)])]
    ppermute x26 -> x25, starting transfers between devices: 24.8 us -> 25.6 us  [swap(): return lax.ppermute(x, 'enc', [(i, i ^ mask) for i in range(count)])]
  transfers between devices with their start and end apart: 26 -> 25, of which waited for: 21 -> 22; matrix products, arithmetic and copies ran while one was open for 1% -> 1% of each run, Pallas kernels for 6% -> 6%
where the time goes in v5:
time: 104 us
  waiting for transfers between devices  52.1 us (50%)
  starting transfers between devices  25.6 us (25%)
  Pallas kernels  21 us (20%)
  local copies, waits for them, and re-layouts  2.14 us (2%)
  other arithmetic  1.93 us (2%)
  between operations  1.28 us (1%)
    ppermute x25, waiting for transfers between devices, swap(): return lax.ppermute(x, 'enc', [(i, i ^ mask) for i in range(count)])  52.1 us
    ppermute x25, starting transfers between devices, swap(): return lax.ppermute(x, 'enc', [(i, i ^ mask) for i in range(count)])  25.6 us
    pallas_call x1, Pallas kernels, local(): pl.pallas_call(functools.partial(head_kernel, cap_rows, pixel_count, slid...  8.84 us
    pallas_call x1, Pallas kernels, local(): pl.pallas_call(functools.partial(back_kernel, cap_rows, pixel_count), in_...  6.48 us
    pallas_call x1, Pallas kernels, local(): pl.pallas_call(functools.partial(conv_kernel, cap_rows), in_specs=[vmem]...  3.22 us
    pallas_call x1, Pallas kernels, local(): pl.pallas_call(finish_kernel, in_specs=[smem] + [vmem] * 4, out_specs=[pl...  2.47 us
    unnamed x21, local copies, waits for them, and re-layouts  2.14 us
  transfers between devices with their start and end apart: 25, of which 22 were waited for; matrix products, arithmetic and copies ran while one was open for 1% of the time, Pallas kernels for 6%

profile of v5, /device:TPU:0, one launch (start us, length us, event | category | flops | bytes accessed | tf_op | source)
XLA Modules:
  0.0 104.1 jit_solution(3369200581392099812)
XLA Ops:
  0.7 2.1 %copy.21 = bf16[512,4,512]{2,0,1:T(8,128)(2,1)S(1)} copy(bf16[512,4,512]{2,1,0:T(4,128)(2,1)} %param.11) | data formatting | bytes 4194304 | tf_op args[0]
  2.9 3.2 %conv_sums.1 = (f32[4,512,1024]{2,1,0:T(8,128)S(1)}, f32[2,16,1024]{2,1,0:T(8,128)S(1)}) custom-call(bf16[4,512,512]{2,1,0:T(8,128)(2,1)S(1)} %bitcast.21, s32[1,512]{1,0:T(1,128)S(1)} %copy-done.6, bf16[512,1024]{1,0:T(8,128)(2,1)S(1)} %copy-done), custom_call_target="tpu_custom_call" | custom-call | flops 6600000000 | bytes 8388608 | tf_op jit(solution)/shard_map/conv_sums/pallas_call | solution.py:432
  6.1 0.5 collective-permute-start
  6.6 0.9 collective-permute-done
  7.6 3.0 %collective-permute-start.2 = (f32[16,1024]{1,0:T(8,128)S(1)}, f32[16,1024]{1,0:T(8,128)S(1)}, u32[]{:S(2)}, u32[]{:S(2)}) collective-permute-start(f32[16,1024]{1,0:T(8,128)S(1)} %bitcast_add_fusion.1), channel_id=1, source_target_pairs={{0,4},{1,5},{2,6},{3,7},{4,0},{5,1},{6,2},{7,3},{8,12},{9,13},{10,... | collective-permute-start | bytes 196616 | tf_op jit(solution)/shard_map/ppermute | solution.py:341
  10.5 1.4 %collective-permute-start.3 = (f32[16,1024]{1,0:T(8,128)S(1)}, f32[16,1024]{1,0:T(8,128)S(1)}, u32[]{:S(2)}, u32[]{:S(2)}) collective-permute-start(f32[16,1024]{1,0:T(8,128)S(1)} %bitcast_add_fusion.1), channel_id=1, source_target_pairs={{0,6},{1,7},{2,4},{3,5},{4,2},{5,3},{6,0},{7,1},{8,14},{9,15},{10,... | collective-permute-start | bytes 196616 | tf_op jit(solution)/shard_map/ppermute | solution.py:341
  11.9 0.1 collective-permute-start.1
  12.1 0.9 collective-permute-done.2
  13.0 2.8 %collective-permute-done.3 = f32[16,1024]{1,0:T(8,128)S(1)} collective-permute-done((f32[16,1024]{1,0:T(8,128)S(1)}, f32[16,1024]{1,0:T(8,128)S(1)}, u32[]{:S(2)}, u32[]{:S(2)}) %collective-permute-start.3) | collective-permute-done | bytes 65568 | tf_op jit(solution)/shard_map/ppermute | solution.py:341
  15.8 1.0 collective-permute-done.1
  16.8 2.7 %collective-permute-start.4 = (f32[16,1024]{1,0:T(8,128)S(1)}, f32[16,1024]{1,0:T(8,128)S(1)}, u32[]{:S(2)}, u32[]{:S(2)}) collective-permute-start(f32[16,1024]{1,0:T(8,128)S(1)} %add_add_fusion), channel_id=1, source_target_pairs={{0,8},{1,9},{2,10},{3,11},{4,12},{5,13},{6,14},{7,15},{8,0},{9,1},... | collective-permute-start | bytes 196616 | tf_op jit(solution)/shard_map/ppermute | solution.py:341
  19.5 2.7 %collective-permute-done.4 = f32[16,1024]{1,0:T(8,128)S(1)} collective-permute-done((f32[16,1024]{1,0:T(8,128)S(1)}, f32[16,1024]{1,0:T(8,128)S(1)}, u32[]{:S(2)}, u32[]{:S(2)}) %collective-permute-start.4) | collective-permute-done | bytes 65568 | tf_op jit(solution)/shard_map/ppermute | solution.py:341
  22.3 1.2 %collective-permute-done.5 = f32[16,1024]{1,0:T(8,128)S(1)} collective-permute-done((f32[16,1024]{1,0:T(8,128)S(1)}, f32[16,1024]{1,0:T(8,128)S(1)}, u32[]{:S(2)}, u32[]{:S(2)}) %collective-permute-start.5) | collective-permute-done | bytes 65568 | tf_op jit(solution)/shard_map/ppermute | solution.py:341
  23.6 8.8 %norm_head.1 = (bf16[768,512]{1,0:T(8,128)(2,1)S(1)}, f32[768,512]{1,0:T(8,128)S(1)}, bf16[512,1024]{1,0:T(8,128)(2,1)S(1)}, f32[2,16,1152]{2,1,0:T(8,128)S(1)}) custom-call(s32[1,4]{1,0:T(1,128)S(1)} %copy-done.8, s32[1,4]{1,0:T(1,128)S(1)} %copy-done.9, s32[1,1]{1,0:T(1,128)} %bitcast.core_ref, f32[4,512,1024]{2,1,0:T(8,128)S(1)} %get-tuple-element.29.before_ref, ...), custom_call_target="tpu_custom_call" | custom-call | flops 13200000000 | bytes 8388608 | tf_op jit(solution)/shard_map/norm_head/pallas_call | solution.py:450
  32.5 0.2 collective-permute-start.6
  32.7 1.1 %collective-permute-done.6 = f32[16,1152]{1,0:T(8,128)S(1)} collective-permute-done((f32[16,1152]{1,0:T(8,128)S(1)}, f32[16,1152]{1,0:T(8,128)S(1)}, u32[]{:S(2)}, u32[]{:S(2)}) %collective-permute-start.6) | collective-permute-done | bytes 73760 | tf_op jit(solution)/shard_map/ppermute | solution.py:341
  33.9 0.2 collective-permute-start.8
  34.1 1.6 %collective-permute-start.7 = (f32[16,1152]{1,0:T(8,128)S(1)}, f32[16,1152]{1,0:T(8,128)S(1)}, u32[]{:S(2)}, u32[]{:S(2)}) collective-permute-start(f32[16,1152]{1,0:T(8,128)S(1)} %bitcast_add_fusion), channel_id=1, source_target_pairs={{0,2},{1,3},{2,0},{3,1},{4,6},{5,7},{6,4},{7,5},{8,10},{9,11},{10,... | collective-permute-start | bytes 221192 | tf_op jit(solution)/shard_map/ppermute | solution.py:341
  35.7 0.5 collective-permute-done.8
  36.2 0.2 convert_add_fusion
  36.6 1.7 %collective-permute-start.11 = (bf16[384,512]{1,0:T(8,128)(2,1)S(1)}, bf16[384,512]{1,0:T(8,128)(2,1)S(1)}, u32[]{:S(2)}, u32[]{:S(2)}) collective-permute-start(bf16[384,512]{1,0:T(8,128)(2,1)S(1)} %select_convert_fusion.1), channel_id=1, source_target_pairs={{0,2},{1,3},{2,0},{3,1},{4,6},{5,7},{6,4},{7,5},{8,10},{9,11},{10,... | collective-permute-start | bytes 1179656 | tf_op jit(solution)/shard_map/ppermute | solution.py:341
  38.2 0.4 collective-permute-done.7
  38.7 1.3 %collective-permute-start.9 = (f32[16,1152]{1,0:T(8,128)S(1)}, f32[16,1152]{1,0:T(8,128)S(1)}, u32[]{:S(2)}, u32[]{:S(2)}) collective-permute-start(f32[16,1152]{1,0:T(8,128)S(1)} %pad_add_fusion.2), channel_id=1, source_target_pairs={{0,4},{1,5},{2,6},{3,7},{4,0},{5,1},{6,2},{7,3},{8,12},{9,13},{10,... | collective-permute-start | bytes 221192 | tf_op jit(solution)/shard_map/ppermute | solution.py:341
  40.0 3.1 %collective-permute-done.9 = f32[16,1152]{1,0:T(8,128)S(1)} collective-permute-done((f32[16,1152]{1,0:T(8,128)S(1)}, f32[16,1152]{1,0:T(8,128)S(1)}, u32[]{:S(2)}, u32[]{:S(2)}) %collective-permute-start.9) | collective-permute-done | bytes 73760 | tf_op jit(solution)/shard_map/ppermute | solution.py:341
  43.1 2.6 %collective-permute-start.10 = (f32[16,1152]{1,0:T(8,128)S(1)}, f32[16,1152]{1,0:T(8,128)S(1)}, u32[]{:S(2)}, u32[]{:S(2)}) collective-permute-start(f32[16,1152]{1,0:T(8,128)S(1)} %add.106), channel_id=1, source_target_pairs={{0,8},{1,9},{2,10},{3,11},{4,12},{5,13},{6,14},{7,15},{8,0},{9,1},... | collective-permute-start | bytes 221192 | tf_op jit(solution)/shard_map/ppermute | solution.py:341
  45.7 2.1 %collective-permute-done.11 = bf16[384,512]{1,0:T(8,128)(2,1)S(1)} collective-permute-done((bf16[384,512]{1,0:T(8,128)(2,1)S(1)}, bf16[384,512]{1,0:T(8,128)(2,1)S(1)}, u32[]{:S(2)}, u32[]{:S(2)}) %collective-permute-start.11) | collective-permute-done | bytes 393248 | tf_op jit(solution)/shard_map/ppermute | solution.py:341
  47.8 0.2 convert_add_fusion.2
  48.0 0.4 collective-permute-done.10
  48.5 1.6 %collective-permute-start.13 = (bf16[192,512]{1,0:T(8,128)(2,1)S(1)}, bf16[192,512]{1,0:T(8,128)(2,1)S(1)}, u32[]{:S(2)}, u32[]{:S(2)}) collective-permute-start(bf16[192,512]{1,0:T(8,128)(2,1)S(1)} %select_convert_fusion.3), channel_id=1, source_target_pairs={{0,4},{1,5},{2,6},{3,7},{4,0},{5,1},{6,2},{7,3},{8,12},{9,13},{10,... | collective-permute-start | bytes 589832 | tf_op jit(solution)/shard_map/ppermute | solution.py:341
  50.2 6.5 %norm_back.1 = (f32[512,1024]{1,0:T(8,128)S(1)}, f32[1,1024]{1,0:T(1,128)}, f32[1,1024]{1,0:T(1,128)}, f32[1,256]{1,0:T(1,128)}, f32[2,512]{1,0:T(2,128)}, /*index=5*/f32[1,1]{1,0:T(1,128)}) custom-call(bf16[4,512,512]{2,1,0:T(8,128)(2,1)S(1)} %bitcast.22, f32[4,512,1024]{2,1,0:T(8,128)S(1)} %get-tuple-element.29.before_ref, ...), custom_call_target="tpu_custom_call" | custom-call | flops 7699999744 | bytes 8388608 | tf_op jit(solution)/shard_map/norm_back/pallas_call | solution.py:493
  57.0 0.3 collective-permute-start.15
  57.2 1.7 %collective-permute-done.15 = bf16[256,1024]{1,0:T(8,128)(2,1)S(1)} collective-permute-done((bf16[256,1024]{1,0:T(8,128)(2,1)S(1)}, bf16[256,1024]{1,0:T(8,128)(2,1)S(1)}, u32[]{:S(2)}, u32[]{:S(2)}) %collective-permute-start.15) | collective-permute-done | bytes 524320 | tf_op jit(solution)/shard_map/ppermute | solution.py:341
  58.9 0.3 convert_add_fusion.1
  59.3 2.0 %collective-permute-start.16 = (bf16[128,1024]{1,0:T(8,128)(2,1)S(1)}, bf16[128,1024]{1,0:T(8,128)(2,1)S(1)}, u32[]{:S(2)}, u32[]{:S(2)}) collective-permute-start(bf16[128,1024]{1,0:T(8,128)(2,1)S(1)} %select_convert_fusion.2), channel_id=1, source_target_pairs={{0,2},{1,3},{2,0},{3,1},{4,6},{5,7},{6,4},{7,5},{8,10},{9,11},{10,... | collective-permute-start | bytes 786440 | tf_op jit(solution)/shard_map/ppermute | solution.py:341
  61.3 2.0 %collective-permute-start.14 = (bf16[192,512]{1,0:T(8,128)(2,1)S(1)}, bf16[192,512]{1,0:T(8,128)(2,1)S(1)}, u32[]{:S(2)}, u32[]{:S(2)}) collective-permute-start(bf16[192,512]{1,0:T(8,128)(2,1)S(1)} %get-tuple-element.50), channel_id=1, source_target_pairs={{0,8},{1,9},{2,10},{3,11},{4,12},{5,13},{6,14},{7,15},{8,0},{9,1},... | collective-permute-start | bytes 589832 | tf_op jit(solution)/shard_map/ppermute | solution.py:341
  63.3 4.6 %collective-permute-done.16 = bf16[128,1024]{1,0:T(8,128)(2,1)S(1)} collective-permute-done((bf16[128,1024]{1,0:T(8,128)(2,1)S(1)}, bf16[128,1024]{1,0:T(8,128)(2,1)S(1)}, u32[]{:S(2)}, u32[]{:S(2)}) %collective-permute-start.16) | collective-permute-done | bytes 262176 | tf_op jit(solution)/shard_map/ppermute | solution.py:341
  68.1 1.0 collective-permute-start.18
  69.1 4.1 %collective-permute-done.14 = bf16[192,512]{1,0:T(8,128)(2,1)S(1)} collective-permute-done((bf16[192,512]{1,0:T(8,128)(2,1)S(1)}, bf16[192,512]{1,0:T(8,128)(2,1)S(1)}, u32[]{:S(2)}, u32[]{:S(2)}) %collective-permute-start.14) | collective-permute-done | bytes 196640 | tf_op jit(solution)/shard_map/ppermute | solution.py:341
  73.4 2.7 %collective-permute-done.18 = bf16[64,1024]{1,0:T(8,128)(2,1)S(1)} collective-permute-done((bf16[64,1024]{1,0:T(8,128)(2,1)S(1)}, bf16[64,1024]{1,0:T(8,128)(2,1)S(1)}, u32[]{:S(2)}, u32[]{:S(2)}) %collective-permute-start.18) | collective-permute-done | bytes 131104 | tf_op jit(solution)/shard_map/ppermute | solution.py:341
  76.1 0.8 collective-permute-start.21
  76.8 3.9 %collective-permute-done.17 = bf16[192,512]{1,0:T(8,128)(2,1)S(1)} collective-permute-done((bf16[192,512]{1,0:T(8,128)(2,1)S(1)}, bf16[192,512]{1,0:T(8,128)(2,1)S(1)}, u32[]{:S(2)}, u32[]{:S(2)}) %collective-permute-start.17) | collective-permute-done | bytes 196640 | tf_op jit(solution)/shard_map/ppermute | solution.py:341
  80.8 1.3 %collective-permute-start.19 = (bf16[384,512]{1,0:T(8,128)(2,1)S(1)}, bf16[384,512]{1,0:T(8,128)(2,1)S(1)}, u32[]{:S(2)}, u32[]{:S(2)}) collective-permute-start(bf16[384,512]{1,0:T(8,128)(2,1)S(1)} %maximum_add_fusion.1), channel_id=1, source_target_pairs={{0,2},{1,3},{2,0},{3,1},{4,6},{5,7},{6,4},{7,5},{8,10},{9,11},{10,... | collective-permute-start | bytes 1179656 | tf_op jit(solution)/shard_map/ppermute | solution.py:341
  82.2 3.0 %collective-permute-done.21 = bf16[64,1024]{1,0:T(8,128)(2,1)S(1)} collective-permute-done((bf16[64,1024]{1,0:T(8,128)(2,1)S(1)}, bf16[64,1024]{1,0:T(8,128)(2,1)S(1)}, u32[]{:S(2)}, u32[]{:S(2)}) %collective-permute-start.21) | collective-permute-done | bytes 131104 | tf_op jit(solution)/shard_map/ppermute | solution.py:341
  85.3 5.0 %collective-permute-done.22 = bf16[64,1024]{1,0:T(8,128)(2,1)S(1)} collective-permute-done((bf16[64,1024]{1,0:T(8,128)(2,1)S(1)}, bf16[64,1024]{1,0:T(8,128)(2,1)S(1)}, u32[]{:S(2)}, u32[]{:S(2)}) %collective-permute-start.22) | collective-permute-done | bytes 131104 | tf_op jit(solution)/shard_map/ppermute | solution.py:341
  90.6 0.8 collective-permute-start.23
  91.4 8.0 %collective-permute-done.23 = bf16[128,1024]{1,0:T(8,128)(2,1)S(1)} collective-permute-done((bf16[128,1024]{1,0:T(8,128)(2,1)S(1)}, bf16[128,1024]{1,0:T(8,128)(2,1)S(1)}, u32[]{:S(2)}, u32[]{:S(2)}) %collective-permute-start.23) | collective-permute-done | bytes 262176 | tf_op jit(solution)/shard_map/ppermute | solution.py:341
  99.5 1.9 %collective-permute-done.24.conv_other_ref = bf16[256,1024]{1,0:T(8,128)(2,1)S(1)} collective-permute-done((bf16[256,1024]{1,0:T(8,128)(2,1)S(1)}, bf16[256,1024]{1,0:T(8,128)(2,1)S(1)}, u32[]{:S(2)}, u32[]{:S(2)}) %collective-permute-start.24) | collective-permute-done | bytes 524320 | tf_op jit(solution)/shard_map/ppermute | solution.py:341
  101.4 2.5 %finish.1 = (f32[1024,512]{1,0:T(8,128)}, f32[512,512]{1,0:T(8,128)}, f32[512,1024]{1,0:T(8,128)}) custom-call(s32[1,1]{1,0:T(1,128)} %bitcast.core_ref, bf16[768,512]{1,0:T(8,128)(2,1)S(1)} %pad_maximum_fusion.head_ref, bf16[768,512]{1,0:T(8,128)(2,1)S(1)} %collective-permute-done.20.head_other_ref, bf16[256,1024]{1,0:T(8,128)(2,1)S(1)} %maximum_add_fusion.conv_ref, ...), custom_call_target="tpu_custom_call" | custom-call | flops 3300000000 | bytes 8388608 | tf_op jit(solution)/shard_map/finish/pallas_call | solution.py:531
  (69 shorter events, 1.8 us)
Async XLA Ops:
  0.6 2.1 %copy-start = (bf16[512,1024]{1,0:T(8,128)(2,1)S(1)}, bf16[512,1024]{1,0:T(8,128)(2,1)}, u32[]{:S(2)}) copy-start(bf16[512,1024]{1,0:T(8,128)(2,1)} %w_ref.1) | copy-start | bytes 3145732
  0.7 2.1 %copy-start.6 = (s32[1,512]{1,0:T(1,128)S(1)}, s32[1,512]{1,0:T(1,128)}, u32[]{:S(2)}) copy-start(s32[1,512]{1,0:T(1,128)} %assign_ref.5) | copy-start | bytes 6148
  2.8 20.8 %copy-start.1 = (bf16[1024,512]{1,0:T(8,128)(2,1)S(1)}, bf16[1024,512]{1,0:T(8,128)(2,1)}, u32[]{:S(2)}) copy-start(bf16[1024,512]{1,0:T(8,128)(2,1)} %w_fc_ref.1) | copy-start | bytes 3145732
  2.8 20.8 %copy-start.2 = (bf16[512,512]{1,0:T(8,128)(2,1)S(1)}, bf16[512,512]{1,0:T(8,128)(2,1)}, u32[]{:S(2)}) copy-start(bf16[512,512]{1,0:T(8,128)(2,1)} %w_gate_ref.1) | copy-start | bytes 1572868
  2.8 20.8 %copy-start.3 = (f32[512,2]{0,1:T(2,128)S(1)}, f32[512,2]{0,1:T(2,128)}, u32[]{:S(2)}) copy-start(f32[512,2]{0,1:T(2,128)} %param.21) | copy-start | bytes 12292
  2.8 20.8 %copy-start.4 = (f32[1024]{0:T(1024)S(1)}, f32[1024]{0:T(1024)}, u32[]{:S(2)}) copy-start(f32[1024]{0:T(1024)} %param.16) | copy-start | bytes 12292
  2.8 20.8 %copy-start.5 = (f32[1024]{0:T(1024)S(1)}, f32[1024]{0:T(1024)}, u32[]{:S(2)}) copy-start(f32[1024]{0:T(1024)} %param.17) | copy-start | bytes 12292
  2.8 20.7 %copy-start.7 = (f32[256]{0:T(256)S(1)}, f32[256]{0:T(256)}, u32[]{:S(2)}) copy-start(f32[256]{0:T(256)} %param.20) | copy-start | bytes 3076
  2.8 20.7 %copy-start.8 = (s32[1,4]{1,0:T(1,128)S(1)}, s32[1,4]{1,0:T(1,128)}, u32[]{:S(2)}) copy-start(s32[1,4]{1,0:T(1,128)} %counts_ref.1) | copy-start | bytes 52
  2.9 20.7 %copy-start.9 = (s32[1,4]{1,0:T(1,128)S(1)}, s32[1,4]{1,0:T(1,128)}, u32[]{:S(2)}) copy-start(s32[1,4]{1,0:T(1,128)} %labels_ref.1) | copy-start | bytes 52
  6.1 1.4 %collective-permute-start = (f32[16,1024]{1,0:T(8,128)S(1)}, f32[16,1024]{1,0:T(8,128)S(1)}, u32[]{:S(2)}, u32[]{:S(2)}) collective-permute-start(f32[16,1024]{1,0:T(8,128)S(1)} %select_bitcast_fusion.1), channel_id=1, source_target_pairs={{0,1},{1,0},{2,3},{3,2},{4,5},{5,4},{6,7},{7,6},{8,9},{9,8},{10,11... | collective-permute-start | bytes 196616 | tf_op jit(solution)/shard_map/ppermute | solution.py:341
  7.6 5.4 %collective-permute-start.2 = (f32[16,1024]{1,0:T(8,128)S(1)}, f32[16,1024]{1,0:T(8,128)S(1)}, u32[]{:S(2)}, u32[]{:S(2)}) collective-permute-start(f32[16,1024]{1,0:T(8,128)S(1)} %bitcast_add_fusion.1), channel_id=1, source_target_pairs={{0,4},{1,5},{2,6},{3,7},{4,0},{5,1},{6,2},{7,3},{8,12},{9,13},{10,... | collective-permute-start | bytes 196616 | tf_op jit(solution)/shard_map/ppermute | solution.py:341
  10.5 5.2 %collective-permute-start.3 = (f32[16,1024]{1,0:T(8,128)S(1)}, f32[16,1024]{1,0:T(8,128)S(1)}, u32[]{:S(2)}, u32[]{:S(2)}) collective-permute-start(f32[16,1024]{1,0:T(8,128)S(1)} %bitcast_add_fusion.1), channel_id=1, source_target_pairs={{0,6},{1,7},{2,4},{3,5},{4,2},{5,3},{6,0},{7,1},{8,14},{9,15},{10,... | collective-permute-start | bytes 196616 | tf_op jit(solution)/shard_map/ppermute | solution.py:341
  11.9 4.8 %collective-permute-start.1 = (f32[16,1024]{1,0:T(8,128)S(1)}, f32[16,1024]{1,0:T(8,128)S(1)}, u32[]{:S(2)}, u32[]{:S(2)}) collective-permute-start(f32[16,1024]{1,0:T(8,128)S(1)} %bitcast_add_fusion.1), channel_id=1, source_target_pairs={{0,2},{1,3},{2,0},{3,1},{4,6},{5,7},{6,4},{7,5},{8,10},{9,11},{10,... | collective-permute-start | bytes 196616 | tf_op jit(solution)/shard_map/ppermute | solution.py:341
  16.8 5.4 %collective-permute-start.4 = (f32[16,1024]{1,0:T(8,128)S(1)}, f32[16,1024]{1,0:T(8,128)S(1)}, u32[]{:S(2)}, u32[]{:S(2)}) collective-permute-start(f32[16,1024]{1,0:T(8,128)S(1)} %add_add_fusion), channel_id=1, source_target_pairs={{0,8},{1,9},{2,10},{3,11},{4,12},{5,13},{6,14},{7,15},{8,0},{9,1},... | collective-permute-start | bytes 196616 | tf_op jit(solution)/shard_map/ppermute | solution.py:341
  22.2 1.3 %collective-permute-start.5 = (f32[16,1024]{1,0:T(8,128)S(1)}, f32[16,1024]{1,0:T(8,128)S(1)}, u32[]{:S(2)}, u32[]{:S(2)}) collective-permute-start(f32[16,1024]{1,0:T(8,128)S(1)} %add.100), channel_id=1, source_target_pairs={{0,1},{1,0},{2,3},{3,2},{4,5},{5,4},{6,7},{7,6},{8,9},{9,8},{10,11... | collective-permute-start | bytes 196616 | tf_op jit(solution)/shard_map/ppermute | solution.py:341
  32.5 1.3 %collective-permute-start.6 = (f32[16,1152]{1,0:T(8,128)S(1)}, f32[16,1152]{1,0:T(8,128)S(1)}, u32[]{:S(2)}, u32[]{:S(2)}) collective-permute-start(f32[16,1152]{1,0:T(8,128)S(1)} %select_bitcast_fusion), channel_id=1, source_target_pairs={{0,1},{1,0},{2,3},{3,2},{4,5},{5,4},{6,7},{7,6},{8,9},{9,8},{10,11... | collective-permute-start | bytes 221192 | tf_op jit(solution)/shard_map/ppermute | solution.py:341
  33.9 2.4 %collective-permute-start.8 = (bf16[768,512]{1,0:T(8,128)(2,1)S(1)}, bf16[768,512]{1,0:T(8,128)(2,1)S(1)}, u32[]{:S(2)}, u32[]{:S(2)}) collective-permute-start(bf16[768,512]{1,0:T(8,128)(2,1)S(1)} %pad_add_fusion), channel_id=1, source_target_pairs={{0,1},{1,0},{2,3},{3,2},{4,5},{5,4},{6,7},{7,6},{8,9},{9,8},{10,11... | collective-permute-start | bytes 2359304 | tf_op jit(solution)/shard_map/ppermute | solution.py:341
  34.1 4.5 %collective-permute-start.7 = (f32[16,1152]{1,0:T(8,128)S(1)}, f32[16,1152]{1,0:T(8,128)S(1)}, u32[]{:S(2)}, u32[]{:S(2)}) collective-permute-start(f32[16,1152]{1,0:T(8,128)S(1)} %bitcast_add_fusion), channel_id=1, source_target_pairs={{0,2},{1,3},{2,0},{3,1},{4,6},{5,7},{6,4},{7,5},{8,10},{9,11},{10,... | collective-permute-start | bytes 221192 | tf_op jit(solution)/shard_map/ppermute | solution.py:341
  36.6 11.2 %collective-permute-start.11 = (bf16[384,512]{1,0:T(8,128)(2,1)S(1)}, bf16[384,512]{1,0:T(8,128)(2,1)S(1)}, u32[]{:S(2)}, u32[]{:S(2)}) collective-permute-start(bf16[384,512]{1,0:T(8,128)(2,1)S(1)} %select_convert_fusion.1), channel_id=1, source_target_pairs={{0,2},{1,3},{2,0},{3,1},{4,6},{5,7},{6,4},{7,5},{8,10},{9,11},{10,... | collective-permute-start | bytes 1179656 | tf_op jit(solution)/shard_map/ppermute | solution.py:341
  38.7 4.4 %collective-permute-start.9 = (f32[16,1152]{1,0:T(8,128)S(1)}, f32[16,1152]{1,0:T(8,128)S(1)}, u32[]{:S(2)}, u32[]{:S(2)}) collective-permute-start(f32[16,1152]{1,0:T(8,128)S(1)} %pad_add_fusion.2), channel_id=1, source_target_pairs={{0,4},{1,5},{2,6},{3,7},{4,0},{5,1},{6,2},{7,3},{8,12},{9,13},{10,... | collective-permute-start | bytes 221192 | tf_op jit(solution)/shard_map/ppermute | solution.py:341
  43.1 5.3 %collective-permute-start.10 = (f32[16,1152]{1,0:T(8,128)S(1)}, f32[16,1152]{1,0:T(8,128)S(1)}, u32[]{:S(2)}, u32[]{:S(2)}) collective-permute-start(f32[16,1152]{1,0:T(8,128)S(1)} %add.106), channel_id=1, source_target_pairs={{0,8},{1,9},{2,10},{3,11},{4,12},{5,13},{6,14},{7,15},{8,0},{9,1},... | collective-permute-start | bytes 221192 | tf_op jit(solution)/shard_map/ppermute | solution.py:341
  48.4 1.8 %collective-permute-start.12 = (f32[16,1152]{1,0:T(8,128)S(1)}, f32[16,1152]{1,0:T(8,128)S(1)}, u32[]{:S(2)}, u32[]{:S(2)}) collective-permute-start(f32[16,1152]{1,0:T(8,128)S(1)} %pad_add_fusion.1), channel_id=1, source_target_pairs={{0,1},{1,0},{2,3},{3,2},{4,5},{5,4},{6,7},{7,6},{8,9},{9,8},{10,11... | collective-permute-start | bytes 221192 | tf_op jit(solution)/shard_map/ppermute | solution.py:341
  48.5 8.1 %collective-permute-start.13 = (bf16[192,512]{1,0:T(8,128)(2,1)S(1)}, bf16[192,512]{1,0:T(8,128)(2,1)S(1)}, u32[]{:S(2)}, u32[]{:S(2)}) collective-permute-start(bf16[192,512]{1,0:T(8,128)(2,1)S(1)} %select_convert_fusion.3), channel_id=1, source_target_pairs={{0,4},{1,5},{2,6},{3,7},{4,0},{5,1},{6,2},{7,3},{8,12},{9,13},{10,... | collective-permute-start | bytes 589832 | tf_op jit(solution)/shard_map/ppermute | solution.py:341
  57.0 2.0 %collective-permute-start.15 = (bf16[256,1024]{1,0:T(8,128)(2,1)S(1)}, bf16[256,1024]{1,0:T(8,128)(2,1)S(1)}, u32[]{:S(2)}, u32[]{:S(2)}) collective-permute-start(bf16[256,1024]{1,0:T(8,128)(2,1)S(1)} %fusion), channel_id=1, source_target_pairs={{0,1},{1,0},{2,3},{3,2},{4,5},{5,4},{6,7},{7,6},{8,9},{9,8},{10,11... | collective-permute-start | bytes 1572872 | tf_op jit(solution)/shard_map/ppermute | solution.py:341
  59.3 8.6 %collective-permute-start.16 = (bf16[128,1024]{1,0:T(8,128)(2,1)S(1)}, bf16[128,1024]{1,0:T(8,128)(2,1)S(1)}, u32[]{:S(2)}, u32[]{:S(2)}) collective-permute-start(bf16[128,1024]{1,0:T(8,128)(2,1)S(1)} %select_convert_fusion.2), channel_id=1, source_target_pairs={{0,2},{1,3},{2,0},{3,1},{4,6},{5,7},{6,4},{7,5},{8,10},{9,11},{10,... | collective-permute-start | bytes 786440 | tf_op jit(solution)/shard_map/ppermute | solution.py:341
  61.3 11.9 %collective-permute-start.14 = (bf16[192,512]{1,0:T(8,128)(2,1)S(1)}, bf16[192,512]{1,0:T(8,128)(2,1)S(1)}, u32[]{:S(2)}, u32[]{:S(2)}) collective-permute-start(bf16[192,512]{1,0:T(8,128)(2,1)S(1)} %get-tuple-element.50), channel_id=1, source_target_pairs={{0,8},{1,9},{2,10},{3,11},{4,12},{5,13},{6,14},{7,15},{8,0},{9,1},... | collective-permute-start | bytes 589832 | tf_op jit(solution)/shard_map/ppermute | solution.py:341
  68.1 7.9 %collective-permute-start.18 = (bf16[64,1024]{1,0:T(8,128)(2,1)S(1)}, bf16[64,1024]{1,0:T(8,128)(2,1)S(1)}, u32[]{:S(2)}, u32[]{:S(2)}) collective-permute-start(bf16[64,1024]{1,0:T(8,128)(2,1)S(1)} %select_convert_fusion.4), channel_id=1, source_target_pairs={{0,4},{1,5},{2,6},{3,7},{4,0},{5,1},{6,2},{7,3},{8,12},{9,13},{10,... | collective-permute-start | bytes 393224 | tf_op jit(solution)/shard_map/ppermute | solution.py:341
  73.3 7.5 %collective-permute-start.17 = (bf16[192,512]{1,0:T(8,128)(2,1)S(1)}, bf16[192,512]{1,0:T(8,128)(2,1)S(1)}, u32[]{:S(2)}, u32[]{:S(2)}) collective-permute-start(bf16[192,512]{1,0:T(8,128)(2,1)S(1)} %fusion.1), channel_id=1, source_target_pairs={{0,4},{1,5},{2,6},{3,7},{4,0},{5,1},{6,2},{7,3},{8,12},{9,13},{10,... | collective-permute-start | bytes 589832 | tf_op jit(solution)/shard_map/ppermute | solution.py:341
  76.1 9.1 %collective-permute-start.21 = (bf16[64,1024]{1,0:T(8,128)(2,1)S(1)}, bf16[64,1024]{1,0:T(8,128)(2,1)S(1)}, u32[]{:S(2)}, u32[]{:S(2)}) collective-permute-start(bf16[64,1024]{1,0:T(8,128)(2,1)S(1)} %get-tuple-element.48), channel_id=1, source_target_pairs={{0,8},{1,9},{2,10},{3,11},{4,12},{5,13},{6,14},{7,15},{8,0},{9,1},... | collective-permute-start | bytes 393224 | tf_op jit(solution)/shard_map/ppermute | solution.py:341
  80.8 9.5 %collective-permute-start.19 = (bf16[384,512]{1,0:T(8,128)(2,1)S(1)}, bf16[384,512]{1,0:T(8,128)(2,1)S(1)}, u32[]{:S(2)}, u32[]{:S(2)}) collective-permute-start(bf16[384,512]{1,0:T(8,128)(2,1)S(1)} %maximum_add_fusion.1), channel_id=1, source_target_pairs={{0,2},{1,3},{2,0},{3,1},{4,6},{5,7},{6,4},{7,5},{8,10},{9,11},{10,... | collective-permute-start | bytes 1179656 | tf_op jit(solution)/shard_map/ppermute | solution.py:341
  85.2 5.0 %collective-permute-start.22 = (bf16[64,1024]{1,0:T(8,128)(2,1)S(1)}, bf16[64,1024]{1,0:T(8,128)(2,1)S(1)}, u32[]{:S(2)}, u32[]{:S(2)}) collective-permute-start(bf16[64,1024]{1,0:T(8,128)(2,1)S(1)} %fusion.2), channel_id=1, source_target_pairs={{0,4},{1,5},{2,6},{3,7},{4,0},{5,1},{6,2},{7,3},{8,12},{9,13},{10,... | collective-permute-start | bytes 393224 | tf_op jit(solution)/shard_map/ppermute | solution.py:341
  90.5 8.9 %collective-permute-start.20 = (bf16[768,512]{1,0:T(8,128)(2,1)S(1)}, bf16[768,512]{1,0:T(8,128)(2,1)S(1)}, u32[]{:S(2)}, u32[]{:S(2)}) collective-permute-start(bf16[768,512]{1,0:T(8,128)(2,1)S(1)} %pad_maximum_fusion.head_ref), channel_id=1, source_target_pairs={{0,1},{1,0},{2,3},{3,2},{4,5},{5,4},{6,7},{7,6},{8,9},{9,8},{10,11... | collective-permute-start | bytes 2359304 | tf_op jit(solution)/shard_map/ppermute | solution.py:341
  90.6 8.8 %collective-permute-start.23 = (bf16[128,1024]{1,0:T(8,128)(2,1)S(1)}, bf16[128,1024]{1,0:T(8,128)(2,1)S(1)}, u32[]{:S(2)}, u32[]{:S(2)}) collective-permute-start(bf16[128,1024]{1,0:T(8,128)(2,1)S(1)} %maximum_add_fusion.2), channel_id=1, source_target_pairs={{0,2},{1,3},{2,0},{3,1},{4,6},{5,7},{6,4},{7,5},{8,10},{9,11},{10,... | collective-permute-start | bytes 786440 | tf_op jit(solution)/shard_map/ppermute | solution.py:341
  99.4 2.0 %collective-permute-start.24 = (bf16[256,1024]{1,0:T(8,128)(2,1)S(1)}, bf16[256,1024]{1,0:T(8,128)(2,1)S(1)}, u32[]{:S(2)}, u32[]{:S(2)}) collective-permute-start(bf16[256,1024]{1,0:T(8,128)(2,1)S(1)} %maximum_add_fusion.conv_ref), channel_id=1, source_target_pairs={{0,1},{1,0},{2,3},{3,2},{4,5},{5,4},{6,7},{7,6},{8,9},{9,8},{10,11... | collective-permute-start | bytes 1572872 | tf_op jit(solution)/shard_map/ppermute | solution.py:341

commit v6 on v5

--- a/solution.py
+++ b/solution.py
@@ -525,8 +525,8 @@
     head.double(1)
     conv.x = wait_for(conv.x, head.x)
     conv.double(1)
+    head.x = wait_for(head.x, conv.x)
     head_other = swap(head.x, 0)
-    conv.x = wait_for(conv.x, head_other)
     wide = [(emb_width, hid_width), (hid_width, hid_width), (input_width, emb_width)]
     grad_fc, grad_gate, grad_conv = pl.pallas_call(
         finish_kernel,

time: 104 us -> 103 us (level)
  waiting for transfers between devices: 52.1 us -> 50.8 us
    ppermute x25, waiting for transfers between devices: 52.1 us -> 50.8 us  [swap(): return lax.ppermute(x, 'enc', [(i, i ^ mask) for i in range(count)])]
where the time goes in v6:
time: 103 us
  waiting for transfers between devices  50.8 us (49%)
  starting transfers between devices  26.1 us (25%)
  Pallas kernels  21 us (20%)
  local copies, waits for them, and re-layouts  2.14 us (2%)
  other arithmetic  1.93 us (2%)
  between operations  1.26 us (1%)
    ppermute x25, waiting for transfers between devices, swap(): return lax.ppermute(x, 'enc', [(i, i ^ mask) for i in range(count)])  50.8 us
    ppermute x25, starting transfers between devices, swap(): return lax.ppermute(x, 'enc', [(i, i ^ mask) for i in range(count)])  26.1 us
    pallas_call x1, Pallas kernels, local(): pl.pallas_call(functools.partial(head_kernel, cap_rows, pixel_count, slid...  8.84 us
    pallas_call x1, Pallas kernels, local(): pl.pallas_call(functools.partial(back_kernel, cap_rows, pixel_count), in_...  6.48 us
    pallas_call x1, Pallas kernels, local(): pl.pallas_call(functools.partial(conv_kernel, cap_rows), in_specs=[vmem]...  3.22 us
    pallas_call x1, Pallas kernels, local(): pl.pallas_call(finish_kernel, in_specs=[smem] + [vmem] * 4, out_specs=[pl...  2.47 us
    unnamed x21, local copies, waits for them, and re-layouts  2.14 us
  transfers between devices with their start and end apart: 25, of which 22 were waited for; matrix products, arithmetic and copies ran while one was open for 1% of the time, Pallas kernels for 6%

profile of v6, /device:TPU:0, one launch (start us, length us, event | category | flops | bytes accessed | tf_op | source)
XLA Modules:
  0.0 103.2 jit_solution(5212205451591088035)
XLA Ops:
  0.7 2.1 %copy.21 = bf16[512,4,512]{2,0,1:T(8,128)(2,1)S(1)} copy(bf16[512,4,512]{2,1,0:T(4,128)(2,1)} %param.11) | data formatting | bytes 4194304 | tf_op args[0]
  2.9 3.2 %conv_sums.1 = (f32[4,512,1024]{2,1,0:T(8,128)S(1)}, f32[2,16,1024]{2,1,0:T(8,128)S(1)}) custom-call(bf16[4,512,512]{2,1,0:T(8,128)(2,1)S(1)} %bitcast.21, s32[1,512]{1,0:T(1,128)S(1)} %copy-done.6, bf16[512,1024]{1,0:T(8,128)(2,1)S(1)} %copy-done), custom_call_target="tpu_custom_call" | custom-call | flops 6600000000 | bytes 8388608 | tf_op jit(solution)/shard_map/conv_sums/pallas_call | solution.py:432
  6.1 0.5 collective-permute-start
  6.6 0.9 collective-permute-done
  7.6 3.0 %collective-permute-start.2 = (f32[16,1024]{1,0:T(8,128)S(1)}, f32[16,1024]{1,0:T(8,128)S(1)}, u32[]{:S(2)}, u32[]{:S(2)}) collective-permute-start(f32[16,1024]{1,0:T(8,128)S(1)} %bitcast_add_fusion.1), channel_id=1, source_target_pairs={{0,4},{1,5},{2,6},{3,7},{4,0},{5,1},{6,2},{7,3},{8,12},{9,13},{10,... | collective-permute-start | bytes 196616 | tf_op jit(solution)/shard_map/ppermute | solution.py:341
  10.5 1.4 %collective-permute-start.3 = (f32[16,1024]{1,0:T(8,128)S(1)}, f32[16,1024]{1,0:T(8,128)S(1)}, u32[]{:S(2)}, u32[]{:S(2)}) collective-permute-start(f32[16,1024]{1,0:T(8,128)S(1)} %bitcast_add_fusion.1), channel_id=1, source_target_pairs={{0,6},{1,7},{2,4},{3,5},{4,2},{5,3},{6,0},{7,1},{8,14},{9,15},{10,... | collective-permute-start | bytes 196616 | tf_op jit(solution)/shard_map/ppermute | solution.py:341
  12.1 0.9 collective-permute-done.2
  13.0 2.8 %collective-permute-done.3 = f32[16,1024]{1,0:T(8,128)S(1)} collective-permute-done((f32[16,1024]{1,0:T(8,128)S(1)}, f32[16,1024]{1,0:T(8,128)S(1)}, u32[]{:S(2)}, u32[]{:S(2)}) %collective-permute-start.3) | collective-permute-done | bytes 65568 | tf_op jit(solution)/shard_map/ppermute | solution.py:341
  15.8 1.0 collective-permute-done.1
  16.8 2.7 %collective-permute-start.4 = (f32[16,1024]{1,0:T(8,128)S(1)}, f32[16,1024]{1,0:T(8,128)S(1)}, u32[]{:S(2)}, u32[]{:S(2)}) collective-permute-start(f32[16,1024]{1,0:T(8,128)S(1)} %add_add_fusion), channel_id=1, source_target_pairs={{0,8},{1,9},{2,10},{3,11},{4,12},{5,13},{6,14},{7,15},{8,0},{9,1},... | collective-permute-start | bytes 196616 | tf_op jit(solution)/shard_map/ppermute | solution.py:341
  19.5 2.7 %collective-permute-done.4 = f32[16,1024]{1,0:T(8,128)S(1)} collective-permute-done((f32[16,1024]{1,0:T(8,128)S(1)}, f32[16,1024]{1,0:T(8,128)S(1)}, u32[]{:S(2)}, u32[]{:S(2)}) %collective-permute-start.4) | collective-permute-done | bytes 65568 | tf_op jit(solution)/shard_map/ppermute | solution.py:341
  22.3 1.2 %collective-permute-done.5 = f32[16,1024]{1,0:T(8,128)S(1)} collective-permute-done((f32[16,1024]{1,0:T(8,128)S(1)}, f32[16,1024]{1,0:T(8,128)S(1)}, u32[]{:S(2)}, u32[]{:S(2)}) %collective-permute-start.5) | collective-permute-done | bytes 65568 | tf_op jit(solution)/shard_map/ppermute | solution.py:341
  23.6 8.8 %norm_head.1 = (bf16[768,512]{1,0:T(8,128)(2,1)S(1)}, f32[768,512]{1,0:T(8,128)S(1)}, bf16[512,1024]{1,0:T(8,128)(2,1)S(1)}, f32[2,16,1152]{2,1,0:T(8,128)S(1)}) custom-call(s32[1,4]{1,0:T(1,128)S(1)} %copy-done.8, s32[1,4]{1,0:T(1,128)S(1)} %copy-done.9, s32[1,1]{1,0:T(1,128)} %bitcast.core_ref, f32[4,512,1024]{2,1,0:T(8,128)S(1)} %get-tuple-element.29.before_ref, ...), custom_call_target="tpu_custom_call" | custom-call | flops 13200000000 | bytes 8388608 | tf_op jit(solution)/shard_map/norm_head/pallas_call | solution.py:450
  32.5 0.2 collective-permute-start.6
  32.7 1.1 %collective-permute-done.6 = f32[16,1152]{1,0:T(8,128)S(1)} collective-permute-done((f32[16,1152]{1,0:T(8,128)S(1)}, f32[16,1152]{1,0:T(8,128)S(1)}, u32[]{:S(2)}, u32[]{:S(2)}) %collective-permute-start.6) | collective-permute-done | bytes 73760 | tf_op jit(solution)/shard_map/ppermute | solution.py:341
  33.9 0.2 collective-permute-start.8
  34.1 1.6 %collective-permute-start.7 = (f32[16,1152]{1,0:T(8,128)S(1)}, f32[16,1152]{1,0:T(8,128)S(1)}, u32[]{:S(2)}, u32[]{:S(2)}) collective-permute-start(f32[16,1152]{1,0:T(8,128)S(1)} %bitcast_add_fusion), channel_id=1, source_target_pairs={{0,2},{1,3},{2,0},{3,1},{4,6},{5,7},{6,4},{7,5},{8,10},{9,11},{10,... | collective-permute-start | bytes 221192 | tf_op jit(solution)/shard_map/ppermute | solution.py:341
  35.7 0.5 collective-permute-done.8
  36.2 0.2 convert_add_fusion
  36.6 1.7 %collective-permute-start.11 = (bf16[384,512]{1,0:T(8,128)(2,1)S(1)}, bf16[384,512]{1,0:T(8,128)(2,1)S(1)}, u32[]{:S(2)}, u32[]{:S(2)}) collective-permute-start(bf16[384,512]{1,0:T(8,128)(2,1)S(1)} %select_convert_fusion.1), channel_id=1, source_target_pairs={{0,2},{1,3},{2,0},{3,1},{4,6},{5,7},{6,4},{7,5},{8,10},{9,11},{10,... | collective-permute-start | bytes 1179656 | tf_op jit(solution)/shard_map/ppermute | solution.py:341
  38.2 0.4 collective-permute-done.7
  38.7 1.3 %collective-permute-start.9 = (f32[16,1152]{1,0:T(8,128)S(1)}, f32[16,1152]{1,0:T(8,128)S(1)}, u32[]{:S(2)}, u32[]{:S(2)}) collective-permute-start(f32[16,1152]{1,0:T(8,128)S(1)} %pad_add_fusion.2), channel_id=1, source_target_pairs={{0,4},{1,5},{2,6},{3,7},{4,0},{5,1},{6,2},{7,3},{8,12},{9,13},{10,... | collective-permute-start | bytes 221192 | tf_op jit(solution)/shard_map/ppermute | solution.py:341
  40.0 3.1 %collective-permute-done.9 = f32[16,1152]{1,0:T(8,128)S(1)} collective-permute-done((f32[16,1152]{1,0:T(8,128)S(1)}, f32[16,1152]{1,0:T(8,128)S(1)}, u32[]{:S(2)}, u32[]{:S(2)}) %collective-permute-start.9) | collective-permute-done | bytes 73760 | tf_op jit(solution)/shard_map/ppermute | solution.py:341
  43.1 2.6 %collective-permute-start.10 = (f32[16,1152]{1,0:T(8,128)S(1)}, f32[16,1152]{1,0:T(8,128)S(1)}, u32[]{:S(2)}, u32[]{:S(2)}) collective-permute-start(f32[16,1152]{1,0:T(8,128)S(1)} %add.106), channel_id=1, source_target_pairs={{0,8},{1,9},{2,10},{3,11},{4,12},{5,13},{6,14},{7,15},{8,0},{9,1},... | collective-permute-start | bytes 221192 | tf_op jit(solution)/shard_map/ppermute | solution.py:341
  45.7 2.1 %collective-permute-done.11 = bf16[384,512]{1,0:T(8,128)(2,1)S(1)} collective-permute-done((bf16[384,512]{1,0:T(8,128)(2,1)S(1)}, bf16[384,512]{1,0:T(8,128)(2,1)S(1)}, u32[]{:S(2)}, u32[]{:S(2)}) %collective-permute-start.11) | collective-permute-done | bytes 393248 | tf_op jit(solution)/shard_map/ppermute | solution.py:341
  47.8 0.2 convert_add_fusion.2
  48.0 0.4 collective-permute-done.10
  48.5 1.6 %collective-permute-start.13 = (bf16[192,512]{1,0:T(8,128)(2,1)S(1)}, bf16[192,512]{1,0:T(8,128)(2,1)S(1)}, u32[]{:S(2)}, u32[]{:S(2)}) collective-permute-start(bf16[192,512]{1,0:T(8,128)(2,1)S(1)} %select_convert_fusion.3), channel_id=1, source_target_pairs={{0,4},{1,5},{2,6},{3,7},{4,0},{5,1},{6,2},{7,3},{8,12},{9,13},{10,... | collective-permute-start | bytes 589832 | tf_op jit(solution)/shard_map/ppermute | solution.py:341
  50.2 6.5 %norm_back.1 = (f32[512,1024]{1,0:T(8,128)S(1)}, f32[1,1024]{1,0:T(1,128)}, f32[1,1024]{1,0:T(1,128)}, f32[1,256]{1,0:T(1,128)}, f32[2,512]{1,0:T(2,128)}, /*index=5*/f32[1,1]{1,0:T(1,128)}) custom-call(bf16[4,512,512]{2,1,0:T(8,128)(2,1)S(1)} %bitcast.22, f32[4,512,1024]{2,1,0:T(8,128)S(1)} %get-tuple-element.29.before_ref, ...), custom_call_target="tpu_custom_call" | custom-call | flops 7699999744 | bytes 8388608 | tf_op jit(solution)/shard_map/norm_back/pallas_call | solution.py:493
  57.0 0.3 collective-permute-start.15
  57.2 1.7 %collective-permute-done.15 = bf16[256,1024]{1,0:T(8,128)(2,1)S(1)} collective-permute-done((bf16[256,1024]{1,0:T(8,128)(2,1)S(1)}, bf16[256,1024]{1,0:T(8,128)(2,1)S(1)}, u32[]{:S(2)}, u32[]{:S(2)}) %collective-permute-start.15) | collective-permute-done | bytes 524320 | tf_op jit(solution)/shard_map/ppermute | solution.py:341
  58.9 0.3 convert_add_fusion.1
  59.3 2.0 %collective-permute-start.16 = (bf16[128,1024]{1,0:T(8,128)(2,1)S(1)}, bf16[128,1024]{1,0:T(8,128)(2,1)S(1)}, u32[]{:S(2)}, u32[]{:S(2)}) collective-permute-start(bf16[128,1024]{1,0:T(8,128)(2,1)S(1)} %select_convert_fusion.2), channel_id=1, source_target_pairs={{0,2},{1,3},{2,0},{3,1},{4,6},{5,7},{6,4},{7,5},{8,10},{9,11},{10,... | collective-permute-start | bytes 786440 | tf_op jit(solution)/shard_map/ppermute | solution.py:341
  61.3 2.0 %collective-permute-start.14 = (bf16[192,512]{1,0:T(8,128)(2,1)S(1)}, bf16[192,512]{1,0:T(8,128)(2,1)S(1)}, u32[]{:S(2)}, u32[]{:S(2)}) collective-permute-start(bf16[192,512]{1,0:T(8,128)(2,1)S(1)} %get-tuple-element.50), channel_id=1, source_target_pairs={{0,8},{1,9},{2,10},{3,11},{4,12},{5,13},{6,14},{7,15},{8,0},{9,1},... | collective-permute-start | bytes 589832 | tf_op jit(solution)/shard_map/ppermute | solution.py:341
  63.3 4.6 %collective-permute-done.16 = bf16[128,1024]{1,0:T(8,128)(2,1)S(1)} collective-permute-done((bf16[128,1024]{1,0:T(8,128)(2,1)S(1)}, bf16[128,1024]{1,0:T(8,128)(2,1)S(1)}, u32[]{:S(2)}, u32[]{:S(2)}) %collective-permute-start.16) | collective-permute-done | bytes 262176 | tf_op jit(solution)/shard_map/ppermute | solution.py:341
  68.1 1.0 collective-permute-start.18
  69.1 4.1 %collective-permute-done.14 = bf16[192,512]{1,0:T(8,128)(2,1)S(1)} collective-permute-done((bf16[192,512]{1,0:T(8,128)(2,1)S(1)}, bf16[192,512]{1,0:T(8,128)(2,1)S(1)}, u32[]{:S(2)}, u32[]{:S(2)}) %collective-permute-start.14) | collective-permute-done | bytes 196640 | tf_op jit(solution)/shard_map/ppermute | solution.py:341
  73.4 2.7 %collective-permute-done.18 = bf16[64,1024]{1,0:T(8,128)(2,1)S(1)} collective-permute-done((bf16[64,1024]{1,0:T(8,128)(2,1)S(1)}, bf16[64,1024]{1,0:T(8,128)(2,1)S(1)}, u32[]{:S(2)}, u32[]{:S(2)}) %collective-permute-start.18) | collective-permute-done | bytes 131104 | tf_op jit(solution)/shard_map/ppermute | solution.py:341
  76.1 0.8 collective-permute-start.20
  76.8 3.9 %collective-permute-done.17 = bf16[192,512]{1,0:T(8,128)(2,1)S(1)} collective-permute-done((bf16[192,512]{1,0:T(8,128)(2,1)S(1)}, bf16[192,512]{1,0:T(8,128)(2,1)S(1)}, u32[]{:S(2)}, u32[]{:S(2)}) %collective-permute-start.17) | collective-permute-done | bytes 196640 | tf_op jit(solution)/shard_map/ppermute | solution.py:341
  80.8 1.3 %collective-permute-start.19 = (bf16[384,512]{1,0:T(8,128)(2,1)S(1)}, bf16[384,512]{1,0:T(8,128)(2,1)S(1)}, u32[]{:S(2)}, u32[]{:S(2)}) collective-permute-start(bf16[384,512]{1,0:T(8,128)(2,1)S(1)} %maximum_add_fusion.1), channel_id=1, source_target_pairs={{0,2},{1,3},{2,0},{3,1},{4,6},{5,7},{6,4},{7,5},{8,10},{9,11},{10,... | collective-permute-start | bytes 1179656 | tf_op jit(solution)/shard_map/ppermute | solution.py:341
  82.2 3.0 %collective-permute-done.20 = bf16[64,1024]{1,0:T(8,128)(2,1)S(1)} collective-permute-done((bf16[64,1024]{1,0:T(8,128)(2,1)S(1)}, bf16[64,1024]{1,0:T(8,128)(2,1)S(1)}, u32[]{:S(2)}, u32[]{:S(2)}) %collective-permute-start.20) | collective-permute-done | bytes 131104 | tf_op jit(solution)/shard_map/ppermute | solution.py:341
  85.3 5.0 %collective-permute-done.21 = bf16[64,1024]{1,0:T(8,128)(2,1)S(1)} collective-permute-done((bf16[64,1024]{1,0:T(8,128)(2,1)S(1)}, bf16[64,1024]{1,0:T(8,128)(2,1)S(1)}, u32[]{:S(2)}, u32[]{:S(2)}) %collective-permute-start.21) | collective-permute-done | bytes 131104 | tf_op jit(solution)/shard_map/ppermute | solution.py:341
  90.4 0.8 collective-permute-start.22
  91.2 6.1 %collective-permute-done.22 = bf16[128,1024]{1,0:T(8,128)(2,1)S(1)} collective-permute-done((bf16[128,1024]{1,0:T(8,128)(2,1)S(1)}, bf16[128,1024]{1,0:T(8,128)(2,1)S(1)}, u32[]{:S(2)}, u32[]{:S(2)}) %collective-permute-start.22) | collective-permute-done | bytes 262176 | tf_op jit(solution)/shard_map/ppermute | solution.py:341
  97.6 0.6 collective-permute-start.24
  98.2 2.4 %collective-permute-done.24.conv_other_ref = bf16[256,1024]{1,0:T(8,128)(2,1)S(1)} collective-permute-done((bf16[256,1024]{1,0:T(8,128)(2,1)S(1)}, bf16[256,1024]{1,0:T(8,128)(2,1)S(1)}, u32[]{:S(2)}, u32[]{:S(2)}) %collective-permute-start.24) | collective-permute-done | bytes 524320 | tf_op jit(solution)/shard_map/ppermute | solution.py:341
  100.6 2.5 %finish.1 = (f32[1024,512]{1,0:T(8,128)}, f32[512,512]{1,0:T(8,128)}, f32[512,1024]{1,0:T(8,128)}) custom-call(s32[1,1]{1,0:T(1,128)} %bitcast.core_ref, bf16[768,512]{1,0:T(8,128)(2,1)S(1)} %maximum_add_fusion.head_ref, bf16[768,512]{1,0:T(8,128)(2,1)S(1)} %collective-permute-done.23.head_other_ref, bf16[256,1024]{1,0:T(8,128)(2,1)S(1)} %pad_maximum_fusion.conv_ref, ...), custom_call_target="tpu_custom_call" | custom-call | flops 3300000000 | bytes 8388608 | tf_op jit(solution)/shard_map/finish/pallas_call | solution.py:531
  (69 shorter events, 1.8 us)
Async XLA Ops:
  0.6 2.1 %copy-start = (bf16[512,1024]{1,0:T(8,128)(2,1)S(1)}, bf16[512,1024]{1,0:T(8,128)(2,1)}, u32[]{:S(2)}) copy-start(bf16[512,1024]{1,0:T(8,128)(2,1)} %w_ref.1) | copy-start | bytes 3145732
  0.7 2.1 %copy-start.6 = (s32[1,512]{1,0:T(1,128)S(1)}, s32[1,512]{1,0:T(1,128)}, u32[]{:S(2)}) copy-start(s32[1,512]{1,0:T(1,128)} %assign_ref.5) | copy-start | bytes 6148
  2.8 20.8 %copy-start.1 = (bf16[1024,512]{1,0:T(8,128)(2,1)S(1)}, bf16[1024,512]{1,0:T(8,128)(2,1)}, u32[]{:S(2)}) copy-start(bf16[1024,512]{1,0:T(8,128)(2,1)} %w_fc_ref.1) | copy-start | bytes 3145732
  2.8 20.8 %copy-start.2 = (bf16[512,512]{1,0:T(8,128)(2,1)S(1)}, bf16[512,512]{1,0:T(8,128)(2,1)}, u32[]{:S(2)}) copy-start(bf16[512,512]{1,0:T(8,128)(2,1)} %w_gate_ref.1) | copy-start | bytes 1572868
  2.8 20.8 %copy-start.3 = (f32[512,2]{0,1:T(2,128)S(1)}, f32[512,2]{0,1:T(2,128)}, u32[]{:S(2)}) copy-start(f32[512,2]{0,1:T(2,128)} %param.21) | copy-start | bytes 12292
  2.8 20.8 %copy-start.4 = (f32[1024]{0:T(1024)S(1)}, f32[1024]{0:T(1024)}, u32[]{:S(2)}) copy-start(f32[1024]{0:T(1024)} %param.16) | copy-start | bytes 12292
  2.8 20.8 %copy-start.5 = (f32[1024]{0:T(1024)S(1)}, f32[1024]{0:T(1024)}, u32[]{:S(2)}) copy-start(f32[1024]{0:T(1024)} %param.17) | copy-start | bytes 12292
  2.8 20.7 %copy-start.7 = (f32[256]{0:T(256)S(1)}, f32[256]{0:T(256)}, u32[]{:S(2)}) copy-start(f32[256]{0:T(256)} %param.20) | copy-start | bytes 3076
  2.8 20.7 %copy-start.8 = (s32[1,4]{1,0:T(1,128)S(1)}, s32[1,4]{1,0:T(1,128)}, u32[]{:S(2)}) copy-start(s32[1,4]{1,0:T(1,128)} %counts_ref.1) | copy-start | bytes 52
  2.9 20.7 %copy-start.9 = (s32[1,4]{1,0:T(1,128)S(1)}, s32[1,4]{1,0:T(1,128)}, u32[]{:S(2)}) copy-start(s32[1,4]{1,0:T(1,128)} %labels_ref.1) | copy-start | bytes 52
  6.1 1.4 %collective-permute-start = (f32[16,1024]{1,0:T(8,128)S(1)}, f32[16,1024]{1,0:T(8,128)S(1)}, u32[]{:S(2)}, u32[]{:S(2)}) collective-permute-start(f32[16,1024]{1,0:T(8,128)S(1)} %select_bitcast_fusion.1), channel_id=1, source_target_pairs={{0,1},{1,0},{2,3},{3,2},{4,5},{5,4},{6,7},{7,6},{8,9},{9,8},{10,11... | collective-permute-start | bytes 196616 | tf_op jit(solution)/shard_map/ppermute | solution.py:341
  7.6 5.4 %collective-permute-start.2 = (f32[16,1024]{1,0:T(8,128)S(1)}, f32[16,1024]{1,0:T(8,128)S(1)}, u32[]{:S(2)}, u32[]{:S(2)}) collective-permute-start(f32[16,1024]{1,0:T(8,128)S(1)} %bitcast_add_fusion.1), channel_id=1, source_target_pairs={{0,4},{1,5},{2,6},{3,7},{4,0},{5,1},{6,2},{7,3},{8,12},{9,13},{10,... | collective-permute-start | bytes 196616 | tf_op jit(solution)/shard_map/ppermute | solution.py:341
  10.5 5.2 %collective-permute-start.3 = (f32[16,1024]{1,0:T(8,128)S(1)}, f32[16,1024]{1,0:T(8,128)S(1)}, u32[]{:S(2)}, u32[]{:S(2)}) collective-permute-start(f32[16,1024]{1,0:T(8,128)S(1)} %bitcast_add_fusion.1), channel_id=1, source_target_pairs={{0,6},{1,7},{2,4},{3,5},{4,2},{5,3},{6,0},{7,1},{8,14},{9,15},{10,... | collective-permute-start | bytes 196616 | tf_op jit(solution)/shard_map/ppermute | solution.py:341
  11.9 4.8 %collective-permute-start.1 = (f32[16,1024]{1,0:T(8,128)S(1)}, f32[16,1024]{1,0:T(8,128)S(1)}, u32[]{:S(2)}, u32[]{:S(2)}) collective-permute-start(f32[16,1024]{1,0:T(8,128)S(1)} %bitcast_add_fusion.1), channel_id=1, source_target_pairs={{0,2},{1,3},{2,0},{3,1},{4,6},{5,7},{6,4},{7,5},{8,10},{9,11},{10,... | collective-permute-start | bytes 196616 | tf_op jit(solution)/shard_map/ppermute | solution.py:341
  16.8 5.4 %collective-permute-start.4 = (f32[16,1024]{1,0:T(8,128)S(1)}, f32[16,1024]{1,0:T(8,128)S(1)}, u32[]{:S(2)}, u32[]{:S(2)}) collective-permute-start(f32[16,1024]{1,0:T(8,128)S(1)} %add_add_fusion), channel_id=1, source_target_pairs={{0,8},{1,9},{2,10},{3,11},{4,12},{5,13},{6,14},{7,15},{8,0},{9,1},... | collective-permute-start | bytes 196616 | tf_op jit(solution)/shard_map/ppermute | solution.py:341
  22.2 1.3 %collective-permute-start.5 = (f32[16,1024]{1,0:T(8,128)S(1)}, f32[16,1024]{1,0:T(8,128)S(1)}, u32[]{:S(2)}, u32[]{:S(2)}) collective-permute-start(f32[16,1024]{1,0:T(8,128)S(1)} %add.100), channel_id=1, source_target_pairs={{0,1},{1,0},{2,3},{3,2},{4,5},{5,4},{6,7},{7,6},{8,9},{9,8},{10,11... | collective-permute-start | bytes 196616 | tf_op jit(solution)/shard_map/ppermute | solution.py:341
  32.5 1.3 %collective-permute-start.6 = (f32[16,1152]{1,0:T(8,128)S(1)}, f32[16,1152]{1,0:T(8,128)S(1)}, u32[]{:S(2)}, u32[]{:S(2)}) collective-permute-start(f32[16,1152]{1,0:T(8,128)S(1)} %select_bitcast_fusion), channel_id=1, source_target_pairs={{0,1},{1,0},{2,3},{3,2},{4,5},{5,4},{6,7},{7,6},{8,9},{9,8},{10,11... | collective-permute-start | bytes 221192 | tf_op jit(solution)/shard_map/ppermute | solution.py:341
  33.9 2.4 %collective-permute-start.8 = (bf16[768,512]{1,0:T(8,128)(2,1)S(1)}, bf16[768,512]{1,0:T(8,128)(2,1)S(1)}, u32[]{:S(2)}, u32[]{:S(2)}) collective-permute-start(bf16[768,512]{1,0:T(8,128)(2,1)S(1)} %pad_add_fusion), channel_id=1, source_target_pairs={{0,1},{1,0},{2,3},{3,2},{4,5},{5,4},{6,7},{7,6},{8,9},{9,8},{10,11... | collective-permute-start | bytes 2359304 | tf_op jit(solution)/shard_map/ppermute | solution.py:341
  34.1 4.5 %collective-permute-start.7 = (f32[16,1152]{1,0:T(8,128)S(1)}, f32[16,1152]{1,0:T(8,128)S(1)}, u32[]{:S(2)}, u32[]{:S(2)}) collective-permute-start(f32[16,1152]{1,0:T(8,128)S(1)} %bitcast_add_fusion), channel_id=1, source_target_pairs={{0,2},{1,3},{2,0},{3,1},{4,6},{5,7},{6,4},{7,5},{8,10},{9,11},{10,... | collective-permute-start | bytes 221192 | tf_op jit(solution)/shard_map/ppermute | solution.py:341
  36.6 11.2 %collective-permute-start.11 = (bf16[384,512]{1,0:T(8,128)(2,1)S(1)}, bf16[384,512]{1,0:T(8,128)(2,1)S(1)}, u32[]{:S(2)}, u32[]{:S(2)}) collective-permute-start(bf16[384,512]{1,0:T(8,128)(2,1)S(1)} %select_convert_fusion.1), channel_id=1, source_target_pairs={{0,2},{1,3},{2,0},{3,1},{4,6},{5,7},{6,4},{7,5},{8,10},{9,11},{10,... | collective-permute-start | bytes 1179656 | tf_op jit(solution)/shard_map/ppermute | solution.py:341
  38.7 4.4 %collective-permute-start.9 = (f32[16,1152]{1,0:T(8,128)S(1)}, f32[16,1152]{1,0:T(8,128)S(1)}, u32[]{:S(2)}, u32[]{:S(2)}) collective-permute-start(f32[16,1152]{1,0:T(8,128)S(1)} %pad_add_fusion.2), channel_id=1, source_target_pairs={{0,4},{1,5},{2,6},{3,7},{4,0},{5,1},{6,2},{7,3},{8,12},{9,13},{10,... | collective-permute-start | bytes 221192 | tf_op jit(solution)/shard_map/ppermute | solution.py:341
  43.1 5.3 %collective-permute-start.10 = (f32[16,1152]{1,0:T(8,128)S(1)}, f32[16,1152]{1,0:T(8,128)S(1)}, u32[]{:S(2)}, u32[]{:S(2)}) collective-permute-start(f32[16,1152]{1,0:T(8,128)S(1)} %add.106), channel_id=1, source_target_pairs={{0,8},{1,9},{2,10},{3,11},{4,12},{5,13},{6,14},{7,15},{8,0},{9,1},... | collective-permute-start | bytes 221192 | tf_op jit(solution)/shard_map/ppermute | solution.py:341
  48.4 1.8 %collective-permute-start.12 = (f32[16,1152]{1,0:T(8,128)S(1)}, f32[16,1152]{1,0:T(8,128)S(1)}, u32[]{:S(2)}, u32[]{:S(2)}) collective-permute-start(f32[16,1152]{1,0:T(8,128)S(1)} %pad_add_fusion.1), channel_id=1, source_target_pairs={{0,1},{1,0},{2,3},{3,2},{4,5},{5,4},{6,7},{7,6},{8,9},{9,8},{10,11... | collective-permute-start | bytes 221192 | tf_op jit(solution)/shard_map/ppermute | solution.py:341
  48.5 8.1 %collective-permute-start.13 = (bf16[192,512]{1,0:T(8,128)(2,1)S(1)}, bf16[192,512]{1,0:T(8,128)(2,1)S(1)}, u32[]{:S(2)}, u32[]{:S(2)}) collective-permute-start(bf16[192,512]{1,0:T(8,128)(2,1)S(1)} %select_convert_fusion.3), channel_id=1, source_target_pairs={{0,4},{1,5},{2,6},{3,7},{4,0},{5,1},{6,2},{7,3},{8,12},{9,13},{10,... | collective-permute-start | bytes 589832 | tf_op jit(solution)/shard_map/ppermute | solution.py:341
  57.0 2.0 %collective-permute-start.15 = (bf16[256,1024]{1,0:T(8,128)(2,1)S(1)}, bf16[256,1024]{1,0:T(8,128)(2,1)S(1)}, u32[]{:S(2)}, u32[]{:S(2)}) collective-permute-start(bf16[256,1024]{1,0:T(8,128)(2,1)S(1)} %fusion), channel_id=1, source_target_pairs={{0,1},{1,0},{2,3},{3,2},{4,5},{5,4},{6,7},{7,6},{8,9},{9,8},{10,11... | collective-permute-start | bytes 1572872 | tf_op jit(solution)/shard_map/ppermute | solution.py:341
  59.3 8.6 %collective-permute-start.16 = (bf16[128,1024]{1,0:T(8,128)(2,1)S(1)}, bf16[128,1024]{1,0:T(8,128)(2,1)S(1)}, u32[]{:S(2)}, u32[]{:S(2)}) collective-permute-start(bf16[128,1024]{1,0:T(8,128)(2,1)S(1)} %select_convert_fusion.2), channel_id=1, source_target_pairs={{0,2},{1,3},{2,0},{3,1},{4,6},{5,7},{6,4},{7,5},{8,10},{9,11},{10,... | collective-permute-start | bytes 786440 | tf_op jit(solution)/shard_map/ppermute | solution.py:341
  61.3 11.9 %collective-permute-start.14 = (bf16[192,512]{1,0:T(8,128)(2,1)S(1)}, bf16[192,512]{1,0:T(8,128)(2,1)S(1)}, u32[]{:S(2)}, u32[]{:S(2)}) collective-permute-start(bf16[192,512]{1,0:T(8,128)(2,1)S(1)} %get-tuple-element.50), channel_id=1, source_target_pairs={{0,8},{1,9},{2,10},{3,11},{4,12},{5,13},{6,14},{7,15},{8,0},{9,1},... | collective-permute-start | bytes 589832 | tf_op jit(solution)/shard_map/ppermute | solution.py:341
  68.1 7.9 %collective-permute-start.18 = (bf16[64,1024]{1,0:T(8,128)(2,1)S(1)}, bf16[64,1024]{1,0:T(8,128)(2,1)S(1)}, u32[]{:S(2)}, u32[]{:S(2)}) collective-permute-start(bf16[64,1024]{1,0:T(8,128)(2,1)S(1)} %select_convert_fusion.4), channel_id=1, source_target_pairs={{0,4},{1,5},{2,6},{3,7},{4,0},{5,1},{6,2},{7,3},{8,12},{9,13},{10,... | collective-permute-start | bytes 393224 | tf_op jit(solution)/shard_map/ppermute | solution.py:341
  73.3 7.5 %collective-permute-start.17 = (bf16[192,512]{1,0:T(8,128)(2,1)S(1)}, bf16[192,512]{1,0:T(8,128)(2,1)S(1)}, u32[]{:S(2)}, u32[]{:S(2)}) collective-permute-start(bf16[192,512]{1,0:T(8,128)(2,1)S(1)} %fusion.1), channel_id=1, source_target_pairs={{0,4},{1,5},{2,6},{3,7},{4,0},{5,1},{6,2},{7,3},{8,12},{9,13},{10,... | collective-permute-start | bytes 589832 | tf_op jit(solution)/shard_map/ppermute | solution.py:341
  76.1 9.1 %collective-permute-start.20 = (bf16[64,1024]{1,0:T(8,128)(2,1)S(1)}, bf16[64,1024]{1,0:T(8,128)(2,1)S(1)}, u32[]{:S(2)}, u32[]{:S(2)}) collective-permute-start(bf16[64,1024]{1,0:T(8,128)(2,1)S(1)} %get-tuple-element.48), channel_id=1, source_target_pairs={{0,8},{1,9},{2,10},{3,11},{4,12},{5,13},{6,14},{7,15},{8,0},{9,1},... | collective-permute-start | bytes 393224 | tf_op jit(solution)/shard_map/ppermute | solution.py:341
  80.8 9.5 %collective-permute-start.19 = (bf16[384,512]{1,0:T(8,128)(2,1)S(1)}, bf16[384,512]{1,0:T(8,128)(2,1)S(1)}, u32[]{:S(2)}, u32[]{:S(2)}) collective-permute-start(bf16[384,512]{1,0:T(8,128)(2,1)S(1)} %maximum_add_fusion.1), channel_id=1, source_target_pairs={{0,2},{1,3},{2,0},{3,1},{4,6},{5,7},{6,4},{7,5},{8,10},{9,11},{10,... | collective-permute-start | bytes 1179656 | tf_op jit(solution)/shard_map/ppermute | solution.py:341
  85.2 5.0 %collective-permute-start.21 = (bf16[64,1024]{1,0:T(8,128)(2,1)S(1)}, bf16[64,1024]{1,0:T(8,128)(2,1)S(1)}, u32[]{:S(2)}, u32[]{:S(2)}) collective-permute-start(bf16[64,1024]{1,0:T(8,128)(2,1)S(1)} %fusion.2), channel_id=1, source_target_pairs={{0,4},{1,5},{2,6},{3,7},{4,0},{5,1},{6,2},{7,3},{8,12},{9,13},{10,... | collective-permute-start | bytes 393224 | tf_op jit(solution)/shard_map/ppermute | solution.py:341
  90.4 6.9 %collective-permute-start.22 = (bf16[128,1024]{1,0:T(8,128)(2,1)S(1)}, bf16[128,1024]{1,0:T(8,128)(2,1)S(1)}, u32[]{:S(2)}, u32[]{:S(2)}) collective-permute-start(bf16[128,1024]{1,0:T(8,128)(2,1)S(1)} %maximum_add_fusion.2), channel_id=1, source_target_pairs={{0,2},{1,3},{2,0},{3,1},{4,6},{5,7},{6,4},{7,5},{8,10},{9,11},{10,... | collective-permute-start | bytes 786440 | tf_op jit(solution)/shard_map/ppermute | solution.py:341
  97.5 3.1 %collective-permute-start.23 = (bf16[768,512]{1,0:T(8,128)(2,1)S(1)}, bf16[768,512]{1,0:T(8,128)(2,1)S(1)}, u32[]{:S(2)}, u32[]{:S(2)}) collective-permute-start(bf16[768,512]{1,0:T(8,128)(2,1)S(1)} %maximum_add_fusion.head_ref), channel_id=1, source_target_pairs={{0,1},{1,0},{2,3},{3,2},{4,5},{5,4},{6,7},{7,6},{8,9},{9,8},{10,11... | collective-permute-start | bytes 2359304 | tf_op jit(solution)/shard_map/ppermute | solution.py:341
  97.6 3.0 %collective-permute-start.24 = (bf16[256,1024]{1,0:T(8,128)(2,1)S(1)}, bf16[256,1024]{1,0:T(8,128)(2,1)S(1)}, u32[]{:S(2)}, u32[]{:S(2)}) collective-permute-start(bf16[256,1024]{1,0:T(8,128)(2,1)S(1)} %pad_maximum_fusion.conv_ref), channel_id=1, source_target_pairs={{0,1},{1,0},{2,3},{3,2},{4,5},{5,4},{6,7},{7,6},{8,9},{9,8},{10,11... | collective-permute-start | bytes 1572872 | tf_op jit(solution)/shard_map/ppermute | solution.py:341
